TPU v7x, 256 devices: a whole 4x4x8 slice. The times are simulated.
256 devices in a mesh: chan: 8 (over x, y_lo), tile: 32 (over y_hi, z, core).
Axes of the slice: x: 4, y: 4 (y_hi: 2, y_lo: 2; y = y_hi * 2 + y_lo), z: 8, core: 2. Of those that a mesh axis runs over, the one named last changes fastest.
Arguments:
- pixels: bfloat16 [128, 256, 1024], P('tile', None, 'chan'), may hold values from -6 to 6
- conv_weight: bfloat16 [3, 3, 1024, 1024], P(None, None, 'tile', 'chan'), may hold values from -0.0625 to 0.0625
- conv_bias: float32 [1024], P('chan'), may hold values from -3 to 3
- depth_weight: float32 [7, 7, 1024], P(None, None, 'chan'), may hold values from -0.875 to 0.875
- depth_bias: float32 [1024], P('chan'), may hold values from -3 to 3
Outputs:
- features: bfloat16 [128, 256, 1024], P('tile', None, 'chan')
All inputs are finite; a program needn't handle non-finite values.
Results may differ from a plain program's by a relative error of at most 0.0043.
Values may be sent and summed in bfloat16 or wider, within the bound.
No kernel may reach another device: no remote copies, remote signals or barrier semaphores. Data moves between devices by JAX's collectives and lax.ppermute only.
A program may use at most 64 MiB of HBM per device.

v0:
```python
import jax
import jax.numpy as jnp
from jax import lax
from jax.experimental import pallas as pl
from jax.experimental.pallas import tpu as pltpu
from jax.sharding import PartitionSpec as P


ROWS, COLS, CH = 4, 256, 128
PIX = ROWS * COLS


def over_a(x):
    return x ^ 1


def over_b(x):
    return (x + 1 if x % 2 else x - 1) % 4


def move(block, partner):
    pairs = []
    for chan in range(8):
        for tile in range(32):
            x, y, hi, z, core = partner(chan // 2, chan % 2, tile // 16, (tile // 2) % 8, tile % 2)
            pairs.append((chan * 32 + tile, (2 * x + y) * 32 + (hi * 8 + z % 8) * 2 + core))
    return lax.ppermute(block, ("chan", "tile"), pairs)


def to_y(x, y, hi, z, core):
    return x, 1 - y, hi, z, core


def to_l(x, y, hi, z, core):
    return (over_b(x) if core else over_a(x)), y, hi, z, core


def to_m(x, y, hi, z, core):
    return (over_a(x) if core else over_b(x)), y, hi, z, core


def to_hi(x, y, hi, z, core):
    return x, y, 1 - hi, z, core


def to_core(x, y, hi, z, core):
    return x, y, hi, z, 1 - core


def to_next(x, y, hi, z, core):
    return x, y, hi, (z - 1 if core else z + 1), core


PIECES = (
    ((0, 0, 0),),
    ((0, 0, 1),),
    ((1, 0, 0),),
    ((1, 0, 1),),
    ((0, 1, 1), (0, 1, 0)),
    ((0, 2, 1), (0, 2, 0), (1, 1, 0), (1, 1, 1)),
    ((0, 3, 1), (0, 3, 0), (1, 2, 0), (1, 2, 1)),
    ((0, 4, 0), (1, 3, 0), (1, 3, 1)),
    ((1, 4, 0),),
)
OTHER_PIECES = (PIECES[4] + PIECES[5],) + PIECES[6:]


def conv_kernel(*refs):
    blocks, own_w, other_w = refs[:8], refs[8:17], refs[17:21]
    small, (outer, inner, mid, own, *params), (xs, ws, acc, up, down, sems) = refs[21:24], refs[24:31], refs[31:]
    bias = params[0]
    chan, tile = lax.axis_index("chan"), lax.axis_index("tile")
    x, y = chan // 2, chan % 2
    y_hi, z, core = tile // 16, (tile // 2) % 8, tile % 2
    turn = 1 - 2 * ((x + core) % 2)
    xl, xm, xf = (x + turn + 4) % 4, (x - turn + 4) % 4, (x + 2) % 4
    copies = []

    def copy(src, dst):
        copies.append(pltpu.make_async_copy(src, dst, sems.at[len(copies)]))
        copies[-1].start()

    places = ((x, y), (x, 1 - y), (xl, y), (xm, y), (xl, 1 - y), (xf, y), (xm, 1 - y), (xf, 1 - y))
    for block, (at_x, at_y) in zip(blocks, places):
        copy(block, xs.at[:, pl.ds(pl.multiple_of((2 * at_x + at_y) * CH, CH), CH)])

    def place(array, pieces, at_core):
        back = 1 - 2 * at_core
        for row, (flip, steps, other) in enumerate(pieces):
            at_z = (z - steps * back + 8) % 8
            index = (((y_hi + flip) % 2) * 8 + at_z) * 2 + (at_core + other) % 2
            rows = pl.ds(pl.multiple_of(index * 32, 32), 32)
            copy(array.at[pl.ds(9 * row, 9)], ws.at[:, rows, :])

    for array, pieces in zip(own_w, PIECES):
        place(array, pieces, core)
    for array, pieces in zip(other_w, OTHER_PIECES):
        place(array, pieces, 1 - core)
    for source, target in zip(small, params):
        copy(source, target)
    for each in copies:
        each.wait()

    groups = (((0, 0), (0, 1)), ((0, 2), (2, 0)), ((2, 1), (2, 2)), ((1, 0), (1, 1)), ((1, 2),))
    for taps in groups:
        filters = [ws[3 * a + b] for a, b in taps]
        rhs = jnp.concatenate(filters, axis=1) if len(taps) > 1 else filters[0]
        result = jnp.dot(xs[...], rhs, preferred_element_type=jnp.float32)
        for at, (a, b) in enumerate(taps):
            part = result[:, at * CH : (at + 1) * CH]
            if a == 0:
                acc[b, 512:1536, :] = part
            elif a == 2:
                acc[b, 0:512, :] = part[0:512]
                acc[b, 512:1024, :] += part[512:1024]
            else:
                acc[b, 256:1280, :] += part

    column = lax.broadcasted_iota(jnp.int32, (COLS, CH), 0)

    def row_sum(row):
        rows = slice((row + 1) * COLS, (row + 2) * COLS)
        left = jnp.where(column == 0, 0.0, pltpu.roll(acc[0, rows, :], 1, 0))
        right = jnp.where(column == COLS - 1, 0.0, pltpu.roll(acc[2, rows, :], COLS - 1, 0))
        return acc[1, rows, :] + left + right

    for slot, row in enumerate((-1, 0, 4, 3)):
        value = row_sum(row)
        own[slot] = value
        if slot < 2:
            up[slot] = value.astype(jnp.bfloat16)
        else:
            down[slot - 2] = value.astype(jnp.bfloat16)
    for slot, row in enumerate((1, 2)):
        value = jnp.maximum(row_sum(row) + bias[...], 0.0).astype(jnp.bfloat16)
        mid[slot] = value
        up[2 + slot] = value
        down[3 - slot] = value

    @pl.when(core == 0)
    def _():
        outer[...] = up[...]
        inner[...] = down[...]

    @pl.when(core == 1)
    def _():
        outer[...] = down[...]
        inner[...] = up[...]


def depth_kernel(own, mid, from_outer, from_inner, bias, depth_bias, weight, out, hidden):
    tile = lax.axis_index("tile")
    has_above = (tile > 0).astype(jnp.float32)
    has_below = (tile < 31).astype(jnp.float32)
    f32 = jnp.float32
    pad = jnp.zeros((10, 8, CH), f32)
    hidden[:, 0:8, :] = pad
    hidden[:, 264:272, :] = pad

    def activate(value):
        return jnp.maximum(value + bias[...], 0.0).astype(jnp.bfloat16).astype(f32)

    def fill(above, below):
        rows = (
            above[3].astype(f32) * has_above,
            above[2].astype(f32) * has_above,
            activate(above[1].astype(f32) + own[0]) * has_above,
            activate(own[1] + above[0].astype(f32)),
            mid[0].astype(f32),
            mid[1].astype(f32),
            activate(own[3] + below[0].astype(f32)),
            activate(below[1].astype(f32) + own[2]) * has_below,
            below[2].astype(f32) * has_below,
            below[3].astype(f32) * has_below,
        )
        for at, value in enumerate(rows):
            hidden[at, 8:264, :] = value

    @pl.when(tile % 2 == 0)
    def _():
        fill(from_outer, from_inner)

    @pl.when(tile % 2 == 1)
    def _():
        fill(from_inner, from_outer)

    width = 32

    def strip(step, _):
        start = pl.multiple_of(step * width, width)
        sums = [jnp.zeros((width, CH), f32) + depth_bias[...] for _ in range(ROWS)]
        for at in range(10):
            wide = hidden[at, pl.ds(start, width + 16), :]
            for b in range(7):
                value = wide[5 + b : 5 + b + width]
                for row in range(ROWS):
                    a = at - row
                    if 0 <= a < 7:
                        sums[row] = sums[row] + value * weight[a, b : b + 1, :]
        for row in range(ROWS):
            out[row, pl.ds(start, width), :] = sums[row].astype(jnp.bfloat16)
        return 0

    lax.fori_loop(0, COLS // width, strip, 0)


def gather_all(pixels, weight):
    p0 = pixels.reshape(PIX, CH)
    w0 = weight.reshape(9, 32, CH)
    h0 = move(w0, to_hi)
    w0_other = move(w0, to_core)
    r1 = move(jnp.concatenate([w0_other, w0]), to_next)
    p_y, p_l, p_m = move(p0, to_y), move(p0, to_l), move(p0, to_m)
    h0_other = move(h0, to_core)
    r2 = move(jnp.concatenate([r1, h0, h0_other]), to_next)
    p_ly, p_ml, p_ym = move(p_l, to_y), move(p_m, to_l), move(p_y, to_m)
    r3 = move(r2, to_next)
    o2 = move(jnp.concatenate([r1, r2]), to_core)
    r4 = move(r3[9:36], to_next)
    o3 = move(r3, to_core)
    p_far = move(p_ym, to_l)
    r5 = move(r4[9:18], to_next)
    o4 = move(r4, to_core)
    o5 = move(r5, to_core)
    blocks = (p0, p_y, p_l, p_m, p_ly, p_ml, p_ym, p_far)
    return blocks, (w0, w0_other, h0, h0_other, r1, r2, r3, r4, r5), (o2, o3, o4, o5)


def body(pixels, conv_weight, conv_bias, depth_weight, depth_bias):
    blocks, own_w, other_w = gather_all(pixels, conv_weight)
    anywhere, vmem = pl.BlockSpec(memory_space=pl.ANY), pl.BlockSpec(memory_space=pltpu.VMEM)
    f32, bf16 = jnp.float32, jnp.bfloat16
    message = jax.ShapeDtypeStruct((4, COLS, CH), bf16)
    outer, inner, mid, own, *params = pl.pallas_call(
        conv_kernel,
        out_shape=(
            message,
            message,
            jax.ShapeDtypeStruct((2, COLS, CH), bf16),
            jax.ShapeDtypeStruct((4, COLS, CH), f32),
            jax.ShapeDtypeStruct((1, CH), f32),
            jax.ShapeDtypeStruct((1, CH), f32),
            jax.ShapeDtypeStruct((7, 7, CH), f32),
        ),
        in_specs=[anywhere] * 24,
        out_specs=(vmem,) * 7,
        scratch_shapes=[
            pltpu.VMEM((PIX, 8 * CH), bf16),
            pltpu.VMEM((9, 8 * CH, CH), bf16),
            pltpu.VMEM((3, 6 * COLS, CH), f32),
            pltpu.VMEM((4, COLS, CH), bf16),
            pltpu.VMEM((4, COLS, CH), bf16),
            pltpu.SemaphoreType.DMA((43,)),
        ],
        compiler_params=pltpu.CompilerParams(vmem_limit_bytes=40 << 20),
        cost_estimate=pl.CostEstimate(flops=2 * PIX * 9 * 1024 * CH, bytes_accessed=6 << 20, transcendentals=0),
        name="conv",
    )(
        *blocks, *own_w, *other_w,
        conv_bias.reshape(1, CH), depth_bias.reshape(1, CH), depth_weight,
    )
    across = [(i, i + 1) for i in range(1, 31, 2)]
    from_outer = lax.ppermute(outer, "tile", across + [(j, i) for i, j in across])
    from_inner = lax.ppermute(inner, "tile", [(i, i ^ 1) for i in range(32)])
    return pl.pallas_call(
        depth_kernel,
        out_shape=jax.ShapeDtypeStruct((ROWS, COLS, CH), bf16),
        in_specs=[vmem] * 7,
        out_specs=vmem,
        scratch_shapes=[pltpu.VMEM((10, COLS + 16, CH), f32)],
        compiler_params=pltpu.CompilerParams(vmem_limit_bytes=20 << 20),
        cost_estimate=pl.CostEstimate(flops=2 * PIX * 49 * CH, bytes_accessed=2 << 20, transcendentals=0),
        name="depth",
    )(own, mid, from_outer, from_inner, *params)


def solution(mesh):
    in_specs = (
        P("tile", None, "chan"),
        P(None, None, "tile", "chan"),
        P("chan"),
        P(None, None, "chan"),
        P("chan"),
    )
    out_specs = P("tile", None, "chan")
    return jax.shard_map(body, mesh=mesh, in_specs=in_specs, out_specs=out_specs, check_vma=False)
```

profile of v0, /device:TPU:1, one launch (start us, length us, event | category | flops | bytes accessed | tf_op | source)
XLA Modules:
  0.0 64.5 jit_solution(11813040944443603701)
XLA Ops:
  0.0 3.2 %collective-permute-start.7 = (bf16[9,32,128]{2,1,0:T(8,128)(2,1)}, bf16[9,32,128]{2,1,0:T(8,128)(2,1)S(1)}, u32[]{:S(2)}, u32[]{:S(2)}) collective-permute-start(bf16[9,32,128]{2,1,0:T(8,128)(2,1)} %bitcast.4), channel_id=1, source_target_pairs={{0,1},{1,0},{2,3},{3,2},{4,5},{5,4},{6,7},{7,6},{8,9},{9,8},{10,11... | collective-permute-start | bytes 221192 | tf_op jit(solution)/shard_map/ppermute | solution.py:27
  3.2 1.2 %collective-permute-start.8 = (bf16[9,32,128]{2,1,0:T(8,128)(2,1)}, bf16[9,32,128]{2,1,0:T(8,128)(2,1)S(1)}, u32[]{:S(2)}, u32[]{:S(2)}) collective-permute-start(bf16[9,32,128]{2,1,0:T(8,128)(2,1)} %bitcast.5), channel_id=1, source_target_pairs={{0,16},{1,17},{2,18},{3,19},{4,20},{5,21},{6,22},{7,23},{8,24},{9,... | collective-permute-start | bytes 221192 | tf_op jit(solution)/shard_map/ppermute | solution.py:27
  4.4 0.9 %pad_maximum_fusion.2 = bf16[18,32,128]{2,1,0:T(8,128)(2,1)S(1)} fusion(bf16[9,32,128]{2,1,0:T(8,128)(2,1)} %bitcast.6, bf16[9,32,128]{2,1,0:T(8,128)(2,1)S(1)} %collective-permute-done.7.refs_9_), kind=kLoop, calls=%fused_computation.2 | loop fusion | flops 73728 | bytes 294912 | tf_op jit(solution)/shard_map/concatenate | solution.py:212
  5.4 5.7 %collective-permute-start.10 = (bf16[18,32,128]{2,1,0:T(8,128)(2,1)S(1)}, bf16[18,32,128]{2,1,0:T(8,128)(2,1)S(1)}, u32[]{:S(2)}, u32[]{:S(2)}) collective-permute-start(bf16[18,32,128]{2,1,0:T(8,128)(2,1)S(1)} %pad_maximum_fusion.2), channel_id=1, source_target_pairs={{0,2},{1,15},{2,4},{3,1},{4,6},{5,3},{6,8},{7,5},{8,10},{9,7},{10,... | collective-permute-start | bytes 442376 | tf_op jit(solution)/shard_map/ppermute | solution.py:27
  11.0 1.3 %collective-permute-done.9.refs_11_ = bf16[9,32,128]{2,1,0:T(8,128)(2,1)S(1)} collective-permute-done((bf16[9,32,128]{2,1,0:T(8,128)(2,1)S(1)}, bf16[9,32,128]{2,1,0:T(8,128)(2,1)S(1)}, u32[]{:S(2)}, u32[]{:S(2)}) %collective-permute-start.9) | collective-permute-done | bytes 73760 | tf_op jit(solution)/shard_map/ppermute | solution.py:27
  12.3 0.8 %collective-permute-done.10.refs_12_ = bf16[18,32,128]{2,1,0:T(8,128)(2,1)S(1)} collective-permute-done((bf16[18,32,128]{2,1,0:T(8,128)(2,1)S(1)}, bf16[18,32,128]{2,1,0:T(8,128)(2,1)S(1)}, u32[]{:S(2)}, u32[]{:S(2)}) %collective-permute-start.10) | collective-permute-done | bytes 147488 | tf_op jit(solution)/shard_map/ppermute | solution.py:27
  13.2 3.2 %collective-permute-start.11 = (bf16[36,32,128]{2,1,0:T(8,128)(2,1)S(1)}, bf16[36,32,128]{2,1,0:T(8,128)(2,1)S(1)}, u32[]{:S(2)}, u32[]{:S(2)}) collective-permute-start(bf16[36,32,128]{2,1,0:T(8,128)(2,1)S(1)} %pad_maximum_fusion.1), channel_id=1, source_target_pairs={{0,2},{1,15},{2,4},{3,1},{4,6},{5,3},{6,8},{7,5},{8,10},{9,7},{10,... | collective-permute-start | bytes 884744 | tf_op jit(solution)/shard_map/ppermute | solution.py:27
  16.3 1.2 %collective-permute-start.2 = (bf16[1024,128]{1,0:T(8,128)(2,1)S(1)}, bf16[1024,128]{1,0:T(8,128)(2,1)S(1)}, u32[]{:S(2)}, u32[]{:S(2)}) collective-permute-start(bf16[1024,128]{1,0:T(8,128)(2,1)S(1)} %bitcast.8), channel_id=1, source_target_pairs={{0,192},{1,65},{2,194},{3,67},{4,196},{5,69},{6,198},{7,71},{8,200... | collective-permute-start | bytes 786440 | tf_op jit(solution)/shard_map/ppermute | solution.py:27
  17.9 2.1 %collective-permute-done.11.refs_13_ = bf16[36,32,128]{2,1,0:T(8,128)(2,1)S(1)} collective-permute-done((bf16[36,32,128]{2,1,0:T(8,128)(2,1)S(1)}, bf16[36,32,128]{2,1,0:T(8,128)(2,1)S(1)}, u32[]{:S(2)}, u32[]{:S(2)}) %collective-permute-start.11) | collective-permute-done | bytes 294944 | tf_op jit(solution)/shard_map/ppermute | solution.py:27
  20.0 3.4 %collective-permute-start.12 = (bf16[36,32,128]{2,1,0:T(8,128)(2,1)S(1)}, bf16[36,32,128]{2,1,0:T(8,128)(2,1)S(1)}, u32[]{:S(2)}, u32[]{:S(2)}) collective-permute-start(bf16[36,32,128]{2,1,0:T(8,128)(2,1)S(1)} %collective-permute-done.11.refs_13_), channel_id=1, source_target_pairs={{0,2},{1,15},{2,4},{3,1},{4,6},{5,3},{6,8},{7,5},{8,10},{9,7},{10,... | collective-permute-start | bytes 884744 | tf_op jit(solution)/shard_map/ppermute | solution.py:27
  23.4 2.5 %collective-permute-start.1 = (bf16[1024,128]{1,0:T(8,128)(2,1)S(1)}, bf16[1024,128]{1,0:T(8,128)(2,1)S(1)}, u32[]{:S(2)}, u32[]{:S(2)}) collective-permute-start(bf16[1024,128]{1,0:T(8,128)(2,1)S(1)} %bitcast.10), channel_id=1, source_target_pairs={{0,64},{1,193},{2,66},{3,195},{4,68},{5,197},{6,70},{7,199},{8,72}... | collective-permute-start | bytes 786440 | tf_op jit(solution)/shard_map/ppermute | solution.py:27
  26.1 1.5 %collective-permute-start.15 = (bf16[54,32,128]{2,1,0:T(8,128)(2,1)S(1)}, bf16[54,32,128]{2,1,0:T(8,128)(2,1)S(1)}, u32[]{:S(2)}, u32[]{:S(2)}) collective-permute-start(bf16[54,32,128]{2,1,0:T(8,128)(2,1)S(1)} %pad_maximum_fusion), channel_id=1, source_target_pairs={{0,1},{1,0},{2,3},{3,2},{4,5},{5,4},{6,7},{7,6},{8,9},{9,8},{10,11... | collective-permute-start | bytes 1327112 | tf_op jit(solution)/shard_map/ppermute | solution.py:27
  27.7 3.0 %collective-permute-start.13 = (bf16[27,32,128]{2,1,0:T(8,128)(2,1)S(1)}, bf16[27,32,128]{2,1,0:T(8,128)(2,1)S(1)}, u32[]{:S(2)}, u32[]{:S(2)}) collective-permute-start(bf16[27,32,128]{2,1,0:T(8,128)(2,1)S(1)} %slice.8), channel_id=1, source_target_pairs={{0,2},{1,15},{2,4},{3,1},{4,6},{5,3},{6,8},{7,5},{8,10},{9,7},{10,... | collective-permute-start | bytes 663560 | tf_op jit(solution)/shard_map/ppermute | solution.py:27
  31.2 4.1 %collective-permute-done.4.refs_5_ = bf16[1024,128]{1,0:T(8,128)(2,1)S(1)} collective-permute-done((bf16[1024,128]{1,0:T(8,128)(2,1)S(1)}, bf16[1024,128]{1,0:T(8,128)(2,1)S(1)}, u32[]{:S(2)}, u32[]{:S(2)}) %collective-permute-start.4) | collective-permute-done | bytes 262176 | tf_op jit(solution)/shard_map/ppermute | solution.py:27
  35.3 3.0 %collective-permute-start.6 = (bf16[1024,128]{1,0:T(8,128)(2,1)S(1)}, bf16[1024,128]{1,0:T(8,128)(2,1)S(1)}, u32[]{:S(2)}, u32[]{:S(2)}) collective-permute-start(bf16[1024,128]{1,0:T(8,128)(2,1)S(1)} %collective-permute-done.5.refs_6_), channel_id=1, source_target_pairs={{0,64},{1,193},{2,66},{3,195},{4,68},{5,197},{6,70},{7,199},{8,72}... | collective-permute-start | bytes 786440 | tf_op jit(solution)/shard_map/ppermute | solution.py:27
  38.5 1.8 %collective-permute-start.14 = (bf16[9,32,128]{2,1,0:T(8,128)(2,1)S(1)}, bf16[9,32,128]{2,1,0:T(8,128)(2,1)S(1)}, u32[]{:S(2)}, u32[]{:S(2)}) collective-permute-start(bf16[9,32,128]{2,1,0:T(8,128)(2,1)S(1)} %slice.9), channel_id=1, source_target_pairs={{0,2},{1,15},{2,4},{3,1},{4,6},{5,3},{6,8},{7,5},{8,10},{9,7},{10,... | collective-permute-start | bytes 221192 | tf_op jit(solution)/shard_map/ppermute | solution.py:27
  40.2 1.7 %collective-permute-done.14.refs_16_ = bf16[9,32,128]{2,1,0:T(8,128)(2,1)S(1)} collective-permute-done((bf16[9,32,128]{2,1,0:T(8,128)(2,1)S(1)}, bf16[9,32,128]{2,1,0:T(8,128)(2,1)S(1)}, u32[]{:S(2)}, u32[]{:S(2)}) %collective-permute-start.14) | collective-permute-done | bytes 73760 | tf_op jit(solution)/shard_map/ppermute | solution.py:27
  42.0 3.1 %collective-permute-start.18 = (bf16[9,32,128]{2,1,0:T(8,128)(2,1)S(1)}, bf16[9,32,128]{2,1,0:T(8,128)(2,1)S(1)}, u32[]{:S(2)}, u32[]{:S(2)}) collective-permute-start(bf16[9,32,128]{2,1,0:T(8,128)(2,1)S(1)} %collective-permute-done.14.refs_16_), channel_id=1, source_target_pairs={{0,1},{1,0},{2,3},{3,2},{4,5},{5,4},{6,7},{7,6},{8,9},{9,8},{10,11... | collective-permute-start | bytes 221192 | tf_op jit(solution)/shard_map/ppermute | solution.py:27
  45.1 0.9 %collective-permute-done.18.refs_20_ = bf16[9,32,128]{2,1,0:T(8,128)(2,1)S(1)} collective-permute-done((bf16[9,32,128]{2,1,0:T(8,128)(2,1)S(1)}, bf16[9,32,128]{2,1,0:T(8,128)(2,1)S(1)}, u32[]{:S(2)}, u32[]{:S(2)}) %collective-permute-start.18) | collective-permute-done | bytes 73760 | tf_op jit(solution)/shard_map/ppermute | solution.py:27
  46.0 0.6 copy-done.3
  46.6 4.6 %conv.1 = (bf16[4,256,128]{2,1,0:T(8,128)(2,1)S(1)}, bf16[4,256,128]{2,1,0:T(8,128)(2,1)S(1)}, bf16[2,256,128]{2,1,0:T(8,128)(2,1)S(1)}, f32[4,256,128]{2,1,0:T(...) custom-call(bf16[1024,128]{1,0:T(8,128)(2,1)S(1)} %bitcast.11, ...), custom_call_target="tpu_custom_call" | custom-call | flops 2415919104 | bytes 6291456 | tf_op jit(solution)/shard_map/conv/pallas_call | solution.py:234
  51.3 1.9 %collective-permute-start.19 = (bf16[4,256,128]{2,1,0:T(8,128)(2,1)S(1)}, bf16[4,256,128]{2,1,0:T(8,128)(2,1)S(1)}, u32[]{:S(2)}, u32[]{:S(2)}) collective-permute-start(bf16[4,256,128]{2,1,0:T(8,128)(2,1)S(1)} %get-tuple-element.14), channel_id=1, source_target_pairs={{1,2},{3,4},{5,6},{7,8},{9,10},{11,12},{13,14},{15,16},{17,18},{19... | collective-permute-start | bytes 786440 | tf_op jit(solution)/shard_map/ppermute | solution.py:263
  53.3 5.7 %collective-permute-done.19.from_outer = bf16[4,256,128]{2,1,0:T(8,128)(2,1)S(1)} collective-permute-done((bf16[4,256,128]{2,1,0:T(8,128)(2,1)S(1)}, bf16[4,256,128]{2,1,0:T(8,128)(2,1)S(1)}, u32[]{:S(2)}, u32[]{:S(2)}) %collective-permute-start.19) | collective-permute-done | bytes 262176 | tf_op jit(solution)/shard_map/ppermute | solution.py:263
  59.0 5.5 %depth.1 = bf16[4,256,128]{2,1,0:T(8,128)(2,1)} custom-call(f32[4,256,128]{2,1,0:T(8,128)S(1)} %get-tuple-element.12.own, bf16[2,256,128]{2,1,0:T(8,128)(2,1)S(1)} %get-tuple-element.13.mid, bf16[4,256,128]{2,1,0:T(8,128)(2,1)S(1)} %collective-permute-done.19.from_outer, bf16[4,256,128]{2,1,0:T(8,128)(2,1)S(1)} %collective-permute-done.20.from_inner, ...), custom_call_target="tpu_custom_call" | custom-call | flops 12845056 | bytes 2097152 | tf_op jit(solution)/shard_map/depth/pallas_call | solution.py:265
  (35 shorter events, 1.5 us)
Async XLA Ops:
  0.0 4.4 %collective-permute-start.7 = (bf16[9,32,128]{2,1,0:T(8,128)(2,1)}, bf16[9,32,128]{2,1,0:T(8,128)(2,1)S(1)}, u32[]{:S(2)}, u32[]{:S(2)}) collective-permute-start(bf16[9,32,128]{2,1,0:T(8,128)(2,1)} %bitcast.4), channel_id=1, source_target_pairs={{0,1},{1,0},{2,3},{3,2},{4,5},{5,4},{6,7},{7,6},{8,9},{9,8},{10,11... | collective-permute-start | bytes 221192 | tf_op jit(solution)/shard_map/ppermute | solution.py:27
  3.2 7.8 %collective-permute-start.8 = (bf16[9,32,128]{2,1,0:T(8,128)(2,1)}, bf16[9,32,128]{2,1,0:T(8,128)(2,1)S(1)}, u32[]{:S(2)}, u32[]{:S(2)}) collective-permute-start(bf16[9,32,128]{2,1,0:T(8,128)(2,1)} %bitcast.5), channel_id=1, source_target_pairs={{0,16},{1,17},{2,18},{3,19},{4,20},{5,21},{6,22},{7,23},{8,24},{9,... | collective-permute-start | bytes 221192 | tf_op jit(solution)/shard_map/ppermute | solution.py:27
  5.3 11.0 %copy-start.1 = (bf16[4,256,128]{2,1,0:T(8,128)(2,1)S(1)}, bf16[4,256,128]{2,1,0:T(8,128)(2,1)}, u32[]{:S(2)}) copy-start(bf16[4,256,128]{2,1,0:T(8,128)(2,1)} %param.5) | copy-start | bytes 786436
  5.4 7.8 %collective-permute-start.10 = (bf16[18,32,128]{2,1,0:T(8,128)(2,1)S(1)}, bf16[18,32,128]{2,1,0:T(8,128)(2,1)S(1)}, u32[]{:S(2)}, u32[]{:S(2)}) collective-permute-start(bf16[18,32,128]{2,1,0:T(8,128)(2,1)S(1)} %pad_maximum_fusion.2), channel_id=1, source_target_pairs={{0,2},{1,15},{2,4},{3,1},{4,6},{5,3},{6,8},{7,5},{8,10},{9,7},{10,... | collective-permute-start | bytes 442376 | tf_op jit(solution)/shard_map/ppermute | solution.py:27
  11.0 1.3 %collective-permute-start.9 = (bf16[9,32,128]{2,1,0:T(8,128)(2,1)S(1)}, bf16[9,32,128]{2,1,0:T(8,128)(2,1)S(1)}, u32[]{:S(2)}, u32[]{:S(2)}) collective-permute-start(bf16[9,32,128]{2,1,0:T(8,128)(2,1)S(1)} %collective-permute-done.8.refs_10_), channel_id=1, source_target_pairs={{0,1},{1,0},{2,3},{3,2},{4,5},{5,4},{6,7},{7,6},{8,9},{9,8},{10,11... | collective-permute-start | bytes 221192 | tf_op jit(solution)/shard_map/ppermute | solution.py:27
  13.2 6.8 %collective-permute-start.11 = (bf16[36,32,128]{2,1,0:T(8,128)(2,1)S(1)}, bf16[36,32,128]{2,1,0:T(8,128)(2,1)S(1)}, u32[]{:S(2)}, u32[]{:S(2)}) collective-permute-start(bf16[36,32,128]{2,1,0:T(8,128)(2,1)S(1)} %pad_maximum_fusion.1), channel_id=1, source_target_pairs={{0,2},{1,15},{2,4},{3,1},{4,6},{5,3},{6,8},{7,5},{8,10},{9,7},{10,... | collective-permute-start | bytes 884744 | tf_op jit(solution)/shard_map/ppermute | solution.py:27
  16.3 9.6 %collective-permute-start.2 = (bf16[1024,128]{1,0:T(8,128)(2,1)S(1)}, bf16[1024,128]{1,0:T(8,128)(2,1)S(1)}, u32[]{:S(2)}, u32[]{:S(2)}) collective-permute-start(bf16[1024,128]{1,0:T(8,128)(2,1)S(1)} %bitcast.8), channel_id=1, source_target_pairs={{0,192},{1,65},{2,194},{3,67},{4,196},{5,69},{6,198},{7,71},{8,200... | collective-permute-start | bytes 786440 | tf_op jit(solution)/shard_map/ppermute | solution.py:27
  17.5 8.5 %collective-permute-start = (bf16[1024,128]{1,0:T(8,128)(2,1)S(1)}, bf16[1024,128]{1,0:T(8,128)(2,1)S(1)}, u32[]{:S(2)}, u32[]{:S(2)}) collective-permute-start(bf16[1024,128]{1,0:T(8,128)(2,1)S(1)} %bitcast.9), channel_id=1, source_target_pairs={{0,32},{1,33},{2,34},{3,35},{4,36},{5,37},{6,38},{7,39},{8,40},{9,... | collective-permute-start | bytes 786440 | tf_op jit(solution)/shard_map/ppermute | solution.py:27
  20.0 7.7 %collective-permute-start.12 = (bf16[36,32,128]{2,1,0:T(8,128)(2,1)S(1)}, bf16[36,32,128]{2,1,0:T(8,128)(2,1)S(1)}, u32[]{:S(2)}, u32[]{:S(2)}) collective-permute-start(bf16[36,32,128]{2,1,0:T(8,128)(2,1)S(1)} %collective-permute-done.11.refs_13_), channel_id=1, source_target_pairs={{0,2},{1,15},{2,4},{3,1},{4,6},{5,3},{6,8},{7,5},{8,10},{9,7},{10,... | collective-permute-start | bytes 884744 | tf_op jit(solution)/shard_map/ppermute | solution.py:27
  23.4 7.3 %collective-permute-start.1 = (bf16[1024,128]{1,0:T(8,128)(2,1)S(1)}, bf16[1024,128]{1,0:T(8,128)(2,1)S(1)}, u32[]{:S(2)}, u32[]{:S(2)}) collective-permute-start(bf16[1024,128]{1,0:T(8,128)(2,1)S(1)} %bitcast.10), channel_id=1, source_target_pairs={{0,64},{1,193},{2,66},{3,195},{4,68},{5,197},{6,70},{7,199},{8,72}... | collective-permute-start | bytes 786440 | tf_op jit(solution)/shard_map/ppermute | solution.py:27
  25.9 9.4 %collective-permute-start.4 = (bf16[1024,128]{1,0:T(8,128)(2,1)S(1)}, bf16[1024,128]{1,0:T(8,128)(2,1)S(1)}, u32[]{:S(2)}, u32[]{:S(2)}) collective-permute-start(bf16[1024,128]{1,0:T(8,128)(2,1)S(1)} %collective-permute-done.2.refs_3_), channel_id=1, source_target_pairs={{0,64},{1,193},{2,66},{3,195},{4,68},{5,197},{6,70},{7,199},{8,72}... | collective-permute-start | bytes 786440 | tf_op jit(solution)/shard_map/ppermute | solution.py:27
  26.1 9.2 %collective-permute-start.5 = (bf16[1024,128]{1,0:T(8,128)(2,1)S(1)}, bf16[1024,128]{1,0:T(8,128)(2,1)S(1)}, u32[]{:S(2)}, u32[]{:S(2)}) collective-permute-start(bf16[1024,128]{1,0:T(8,128)(2,1)S(1)} %collective-permute-done.refs_1_), channel_id=1, source_target_pairs={{0,192},{1,65},{2,194},{3,67},{4,196},{5,69},{6,198},{7,71},{8,200... | collective-permute-start | bytes 786440 | tf_op jit(solution)/shard_map/ppermute | solution.py:27
  26.1 18.9 %collective-permute-start.15 = (bf16[54,32,128]{2,1,0:T(8,128)(2,1)S(1)}, bf16[54,32,128]{2,1,0:T(8,128)(2,1)S(1)}, u32[]{:S(2)}, u32[]{:S(2)}) collective-permute-start(bf16[54,32,128]{2,1,0:T(8,128)(2,1)S(1)} %pad_maximum_fusion), channel_id=1, source_target_pairs={{0,1},{1,0},{2,3},{3,2},{4,5},{5,4},{6,7},{7,6},{8,9},{9,8},{10,11... | collective-permute-start | bytes 1327112 | tf_op jit(solution)/shard_map/ppermute | solution.py:27
  27.7 18.3 %copy-start = (bf16[3,3,32,128]{3,2,1,0:T(8,128)(2,1)S(1)}, bf16[3,3,32,128]{3,2,1,0:T(8,128)(2,1)}, u32[]{:S(2)}) copy-start(bf16[3,3,32,128]{3,2,1,0:T(8,128)(2,1)} %param.6) | copy-start | bytes 221188
  27.7 18.3 %copy-start.2 = (f32[7,7,128]{2,1,0:T(8,128)S(1)}, f32[7,7,128]{2,1,0:T(8,128)}, u32[]{:S(2)}) copy-start(f32[7,7,128]{2,1,0:T(8,128)} %refs_23_.1) | copy-start | bytes 75268
  27.7 10.5 %collective-permute-start.13 = (bf16[27,32,128]{2,1,0:T(8,128)(2,1)S(1)}, bf16[27,32,128]{2,1,0:T(8,128)(2,1)S(1)}, u32[]{:S(2)}, u32[]{:S(2)}) collective-permute-start(bf16[27,32,128]{2,1,0:T(8,128)(2,1)S(1)} %slice.8), channel_id=1, source_target_pairs={{0,2},{1,15},{2,4},{3,1},{4,6},{5,3},{6,8},{7,5},{8,10},{9,7},{10,... | collective-permute-start | bytes 663560 | tf_op jit(solution)/shard_map/ppermute | solution.py:27
  30.8 7.7 %collective-permute-start.3 = (bf16[1024,128]{1,0:T(8,128)(2,1)S(1)}, bf16[1024,128]{1,0:T(8,128)(2,1)S(1)}, u32[]{:S(2)}, u32[]{:S(2)}) collective-permute-start(bf16[1024,128]{1,0:T(8,128)(2,1)S(1)} %collective-permute-done.1.refs_2_), channel_id=1, source_target_pairs={{0,32},{1,33},{2,34},{3,35},{4,36},{5,37},{6,38},{7,39},{8,40},{9,... | collective-permute-start | bytes 786440 | tf_op jit(solution)/shard_map/ppermute | solution.py:27
  35.2 9.8 %collective-permute-start.16 = (bf16[36,32,128]{2,1,0:T(8,128)(2,1)S(1)}, bf16[36,32,128]{2,1,0:T(8,128)(2,1)S(1)}, u32[]{:S(2)}, u32[]{:S(2)}) collective-permute-start(bf16[36,32,128]{2,1,0:T(8,128)(2,1)S(1)} %collective-permute-done.12.refs_14_), channel_id=1, source_target_pairs={{0,1},{1,0},{2,3},{3,2},{4,5},{5,4},{6,7},{7,6},{8,9},{9,8},{10,11... | collective-permute-start | bytes 884744 | tf_op jit(solution)/shard_map/ppermute | solution.py:27
  35.3 9.8 %collective-permute-start.6 = (bf16[1024,128]{1,0:T(8,128)(2,1)S(1)}, bf16[1024,128]{1,0:T(8,128)(2,1)S(1)}, u32[]{:S(2)}, u32[]{:S(2)}) collective-permute-start(bf16[1024,128]{1,0:T(8,128)(2,1)S(1)} %collective-permute-done.5.refs_6_), channel_id=1, source_target_pairs={{0,64},{1,193},{2,66},{3,195},{4,68},{5,197},{6,70},{7,199},{8,72}... | collective-permute-start | bytes 786440 | tf_op jit(solution)/shard_map/ppermute | solution.py:27
  38.2 7.7 %collective-permute-start.17 = (bf16[27,32,128]{2,1,0:T(8,128)(2,1)S(1)}, bf16[27,32,128]{2,1,0:T(8,128)(2,1)S(1)}, u32[]{:S(2)}, u32[]{:S(2)}) collective-permute-start(bf16[27,32,128]{2,1,0:T(8,128)(2,1)S(1)} %collective-permute-done.13.refs_15_), channel_id=1, source_target_pairs={{0,1},{1,0},{2,3},{3,2},{4,5},{5,4},{6,7},{7,6},{8,9},{9,8},{10,11... | collective-permute-start | bytes 663560 | tf_op jit(solution)/shard_map/ppermute | solution.py:27
  38.5 3.5 %collective-permute-start.14 = (bf16[9,32,128]{2,1,0:T(8,128)(2,1)S(1)}, bf16[9,32,128]{2,1,0:T(8,128)(2,1)S(1)}, u32[]{:S(2)}, u32[]{:S(2)}) collective-permute-start(bf16[9,32,128]{2,1,0:T(8,128)(2,1)S(1)} %slice.9), channel_id=1, source_target_pairs={{0,2},{1,15},{2,4},{3,1},{4,6},{5,3},{6,8},{7,5},{8,10},{9,7},{10,... | collective-permute-start | bytes 221192 | tf_op jit(solution)/shard_map/ppermute | solution.py:27
  42.0 4.0 %collective-permute-start.18 = (bf16[9,32,128]{2,1,0:T(8,128)(2,1)S(1)}, bf16[9,32,128]{2,1,0:T(8,128)(2,1)S(1)}, u32[]{:S(2)}, u32[]{:S(2)}) collective-permute-start(bf16[9,32,128]{2,1,0:T(8,128)(2,1)S(1)} %collective-permute-done.14.refs_16_), channel_id=1, source_target_pairs={{0,1},{1,0},{2,3},{3,2},{4,5},{5,4},{6,7},{7,6},{8,9},{9,8},{10,11... | collective-permute-start | bytes 221192 | tf_op jit(solution)/shard_map/ppermute | solution.py:27
  51.3 7.7 %collective-permute-start.19 = (bf16[4,256,128]{2,1,0:T(8,128)(2,1)S(1)}, bf16[4,256,128]{2,1,0:T(8,128)(2,1)S(1)}, u32[]{:S(2)}, u32[]{:S(2)}) collective-permute-start(bf16[4,256,128]{2,1,0:T(8,128)(2,1)S(1)} %get-tuple-element.14), channel_id=1, source_target_pairs={{1,2},{3,4},{5,6},{7,8},{9,10},{11,12},{13,14},{15,16},{17,18},{19... | collective-permute-start | bytes 786440 | tf_op jit(solution)/shard_map/ppermute | solution.py:263
  53.2 5.8 %collective-permute-start.20 = (bf16[4,256,128]{2,1,0:T(8,128)(2,1)S(1)}, bf16[4,256,128]{2,1,0:T(8,128)(2,1)S(1)}, u32[]{:S(2)}, u32[]{:S(2)}) collective-permute-start(bf16[4,256,128]{2,1,0:T(8,128)(2,1)S(1)} %get-tuple-element.15), channel_id=1, source_target_pairs={{0,1},{1,0},{2,3},{3,2},{4,5},{5,4},{6,7},{7,6},{8,9},{9,8},{10,11... | collective-permute-start | bytes 786440 | tf_op jit(solution)/shard_map/ppermute | solution.py:264
  (2 other events, 1.3 us)
where the time goes:
time: 65.6 us; the launch traced here: 64.5 us
  starting transfers between devices  35.7 us (54%)
  waiting for transfers between devices  16.8 us (26%)
  Pallas kernels  10.2 us (16%)
  other arithmetic  1 us (2%)
  local copies, waits for them, and re-layouts  0.7 us (1%)
    ppermute x19, starting transfers between devices, move(): return lax.ppermute(block, ('chan', 'tile'), pairs)  33.7 us
    ppermute x19, waiting for transfers between devices, move(): return lax.ppermute(block, ('chan', 'tile'), pairs)  11.1 us
    ppermute x1, waiting for transfers between devices, body(): lax.ppermute(outer, 'tile', across + [(j, i) for i, j in across])  5.66 us
    pallas_call x1, Pallas kernels, body(): pl.pallas_call(depth_kernel, out_shape=jax.ShapeDtypeStruct((ROWS, COLS,...  5.55 us
    pallas_call x1, Pallas kernels, body(): pl.pallas_call(conv_kernel, out_shape=(message, message, jax.ShapeDtypeSt...  4.62 us
    ppermute x1, starting transfers between devices, body(): lax.ppermute(outer, 'tile', across + [(j, i) for i, j in across])  1.92 us
  transfers between devices with their start and end apart: 21, of which 8 were waited for; matrix products, arithmetic and copies ran while one was open for 2% of the time, Pallas kernels for 0%

commit v1 on v0

--- a/solution.py
+++ b/solution.py
@@ -39,10 +39,6 @@
     return (over_a(x) if core else over_b(x)), y, hi, z, core
 
 
-def to_hi(x, y, hi, z, core):
-    return x, y, 1 - hi, z, core
-
-
 def to_core(x, y, hi, z, core):
     return x, y, hi, z, 1 - core
 
@@ -51,61 +47,15 @@
     return x, y, hi, (z - 1 if core else z + 1), core
 
 
-PIECES = (
-    ((0, 0, 0),),
-    ((0, 0, 1),),
-    ((1, 0, 0),),
-    ((1, 0, 1),),
-    ((0, 1, 1), (0, 1, 0)),
-    ((0, 2, 1), (0, 2, 0), (1, 1, 0), (1, 1, 1)),
-    ((0, 3, 1), (0, 3, 0), (1, 2, 0), (1, 2, 1)),
-    ((0, 4, 0), (1, 3, 0), (1, 3, 1)),
-    ((1, 4, 0),),
-)
-OTHER_PIECES = (PIECES[4] + PIECES[5],) + PIECES[6:]
-
-
-def conv_kernel(*refs):
-    blocks, own_w, other_w = refs[:8], refs[8:17], refs[17:21]
-    small, (outer, inner, mid, own, *params), (xs, ws, acc, up, down, sems) = refs[21:24], refs[24:31], refs[31:]
-    bias = params[0]
-    chan, tile = lax.axis_index("chan"), lax.axis_index("tile")
-    x, y = chan // 2, chan % 2
-    y_hi, z, core = tile // 16, (tile // 2) % 8, tile % 2
-    turn = 1 - 2 * ((x + core) % 2)
-    xl, xm, xf = (x + turn + 4) % 4, (x - turn + 4) % 4, (x + 2) % 4
-    copies = []
-
-    def copy(src, dst):
-        copies.append(pltpu.make_async_copy(src, dst, sems.at[len(copies)]))
-        copies[-1].start()
-
-    places = ((x, y), (x, 1 - y), (xl, y), (xm, y), (xl, 1 - y), (xf, y), (xm, 1 - y), (xf, 1 - y))
-    for block, (at_x, at_y) in zip(blocks, places):
-        copy(block, xs.at[:, pl.ds(pl.multiple_of((2 * at_x + at_y) * CH, CH), CH)])
-
-    def place(array, pieces, at_core):
-        back = 1 - 2 * at_core
-        for row, (flip, steps, other) in enumerate(pieces):
-            at_z = (z - steps * back + 8) % 8
-            index = (((y_hi + flip) % 2) * 8 + at_z) * 2 + (at_core + other) % 2
-            rows = pl.ds(pl.multiple_of(index * 32, 32), 32)
-            copy(array.at[pl.ds(9 * row, 9)], ws.at[:, rows, :])
-
-    for array, pieces in zip(own_w, PIECES):
-        place(array, pieces, core)
-    for array, pieces in zip(other_w, OTHER_PIECES):
-        place(array, pieces, 1 - core)
-    for source, target in zip(small, params):
-        copy(source, target)
-    for each in copies:
-        each.wait()
-
-    groups = (((0, 0), (0, 1)), ((0, 2), (2, 0)), ((2, 1), (2, 2)), ((1, 0), (1, 1)), ((1, 2),))
-    for taps in groups:
-        filters = [ws[3 * a + b] for a, b in taps]
-        rhs = jnp.concatenate(filters, axis=1) if len(taps) > 1 else filters[0]
-        result = jnp.dot(xs[...], rhs, preferred_element_type=jnp.float32)
+TAPS = (((0, 0), (0, 1)), ((0, 2), (2, 0)), ((2, 1), (2, 2)), ((1, 0), (1, 1)), ((1, 2),))
+EARLY = 6 * CH
+
+
+def add_taps(pixels, filters, acc):
+    for taps in TAPS:
+        columns = [filters(3 * a + b) for a, b in taps]
+        rhs = jnp.concatenate(columns, axis=1) if len(taps) > 1 else columns[0]
+        result = jnp.dot(pixels(), rhs, preferred_element_type=jnp.float32)
         for at, (a, b) in enumerate(taps):
             part = result[:, at * CH : (at + 1) * CH]
             if a == 0:
@@ -116,13 +66,80 @@
             else:
                 acc[b, 256:1280, :] += part
 
+
+class Copies:
+    def __init__(self, sems):
+        self.sems, self.started = sems, []
+
+    def start(self, src, dst):
+        copy = pltpu.make_async_copy(src, dst, self.sems.at[len(self.started)])
+        copy.start()
+        self.started.append(copy)
+
+    def wait(self):
+        for copy in self.started:
+            copy.wait()
+
+
+def block_at(pair, half, z):
+    return 2 * ((pair - z // 2 + 5) % 4) + half
+
+
+def early_kernel(*refs):
+    blocks, own_w, other_w, small = refs[:8], refs[8:12], refs[12:15], refs[15:18]
+    (xs, ws, acc, *params), sems = refs[18:24], refs[24]
+    chan, tile = lax.axis_index("chan"), lax.axis_index("tile")
+    x, y = chan // 2, chan % 2
+    z, core = (tile // 2) % 8, tile % 2
+    turn = 1 - 2 * ((x + core) % 2)
+    xl, xm, xf = (x + turn + 4) % 4, (x - turn + 4) % 4, (x + 2) % 4
+    copies = Copies(sems)
+    places = ((x, y), (x, 1 - y), (xl, y), (xm, y), (xl, 1 - y), (xf, y), (xm, 1 - y), (xf, 1 - y))
+    for block, (at_x, at_y) in zip(blocks, places):
+        index = 2 * at_x + at_y
+        at = block_at(index % 4, index // 4, z)
+        copies.start(block, xs.at[:, pl.ds(pl.multiple_of(at * CH, CH), CH)])
+
+    def place(array, at_z):
+        for half in range(2):
+            for at_core in range(2):
+                row = block_at(at_z // 2, half, z) * CH + (at_z % 2) * 64 + at_core * 32
+                rows = pl.ds(pl.multiple_of(row, 32), 32)
+                copies.start(array.at[pl.ds(9 * (2 * half + at_core), 9)], ws.at[:, rows, :])
+
+    back = 1 - 2 * core
+    for steps, array in enumerate(own_w):
+        place(array, (z - steps * back + 8) % 8)
+    for steps, array in enumerate(other_w):
+        place(array, (z + (steps + 1) * back + 8) % 8)
+    for source, target in zip(small, params):
+        copies.start(source, target)
+    copies.wait()
+    add_taps(lambda: xs[:, 0:EARLY], lambda tap: ws[tap, 0:EARLY, :], acc)
+
+
+def late_kernel(xs, ws_early, acc_early, last, bias, outer, inner, mid, own, ws, acc, up, down, sems):
+    tile = lax.axis_index("tile")
+    z, core = (tile // 2) % 8, tile % 2
+    copies = Copies(sems)
+    for half in range(2):
+        rows = pl.ds(pl.multiple_of(half * CH + (1 - z % 2) * 64, 64), 64)
+        early = pl.ds(pl.multiple_of(EARLY + half * CH + (1 - z % 2) * 64, 64), 64)
+        copies.start(ws_early.at[:, early, :], ws.at[:, rows, :])
+        for at_core in range(2):
+            rows = pl.ds(pl.multiple_of(half * CH + (z % 2) * 64 + at_core * 32, 32), 32)
+            copies.start(last.at[pl.ds(9 * (2 * half + at_core), 9)], ws.at[:, rows, :])
+    copies.wait()
+    add_taps(lambda: xs[:, EARLY : 8 * CH], lambda tap: ws[tap], acc)
+
     column = lax.broadcasted_iota(jnp.int32, (COLS, CH), 0)
 
     def row_sum(row):
         rows = slice((row + 1) * COLS, (row + 2) * COLS)
-        left = jnp.where(column == 0, 0.0, pltpu.roll(acc[0, rows, :], 1, 0))
-        right = jnp.where(column == COLS - 1, 0.0, pltpu.roll(acc[2, rows, :], COLS - 1, 0))
-        return acc[1, rows, :] + left + right
+        total = [acc[b, rows, :] + acc_early[b, rows, :] for b in range(3)]
+        left = jnp.where(column == 0, 0.0, pltpu.roll(total[0], 1, 0))
+        right = jnp.where(column == COLS - 1, 0.0, pltpu.roll(total[2], COLS - 1, 0))
+        return total[1] + left + right
 
     for slot, row in enumerate((-1, 0, 4, 3)):
         value = row_sum(row)
@@ -206,59 +223,70 @@
 
 def gather_all(pixels, weight):
     p0 = pixels.reshape(PIX, CH)
-    w0 = weight.reshape(9, 32, CH)
-    h0 = move(w0, to_hi)
-    w0_other = move(w0, to_core)
-    r1 = move(jnp.concatenate([w0_other, w0]), to_next)
+    groups = [[(hi * 8 + z) * 2 + core for hi in range(2) for core in range(2)] for z in range(8)]
+    four = jnp.broadcast_to(weight.reshape(1, 9, 32, CH), (4, 9, 32, CH)).reshape(36, 32, CH)
+    w0 = lax.all_to_all(four, "tile", 0, 0, tiled=True, axis_index_groups=groups)
+    w1 = move(w0, to_next)
     p_y, p_l, p_m = move(p0, to_y), move(p0, to_l), move(p0, to_m)
-    h0_other = move(h0, to_core)
-    r2 = move(jnp.concatenate([r1, h0, h0_other]), to_next)
+    w2 = move(w1, to_next)
+    o1 = move(w1, to_core)
     p_ly, p_ml, p_ym = move(p_l, to_y), move(p_m, to_l), move(p_y, to_m)
-    r3 = move(r2, to_next)
-    o2 = move(jnp.concatenate([r1, r2]), to_core)
-    r4 = move(r3[9:36], to_next)
-    o3 = move(r3, to_core)
+    w3 = move(w2, to_next)
+    o2 = move(w2, to_core)
     p_far = move(p_ym, to_l)
-    r5 = move(r4[9:18], to_next)
-    o4 = move(r4, to_core)
-    o5 = move(r5, to_core)
-    blocks = (p0, p_y, p_l, p_m, p_ly, p_ml, p_ym, p_far)
-    return blocks, (w0, w0_other, h0, h0_other, r1, r2, r3, r4, r5), (o2, o3, o4, o5)
+    w4 = move(w3, to_next)
+    o3 = move(w3, to_core)
+    return (p0, p_y, p_l, p_m, p_ly, p_ml, p_ym, p_far, w0, w1, w2, w3, o1, o2, o3), w4
 
 
 def body(pixels, conv_weight, conv_bias, depth_weight, depth_bias):
-    blocks, own_w, other_w = gather_all(pixels, conv_weight)
     anywhere, vmem = pl.BlockSpec(memory_space=pl.ANY), pl.BlockSpec(memory_space=pltpu.VMEM)
+    hbm = pl.BlockSpec(memory_space=pltpu.HBM)
     f32, bf16 = jnp.float32, jnp.bfloat16
     message = jax.ShapeDtypeStruct((4, COLS, CH), bf16)
-    outer, inner, mid, own, *params = pl.pallas_call(
-        conv_kernel,
+    gathered, last = gather_all(pixels, conv_weight)
+    xs, ws, acc, *params = pl.pallas_call(
+        early_kernel,
+        out_shape=(
+            jax.ShapeDtypeStruct((PIX, 8 * CH), bf16),
+            jax.ShapeDtypeStruct((9, 8 * CH, CH), bf16),
+            jax.ShapeDtypeStruct((3, 6 * COLS, CH), f32),
+            jax.ShapeDtypeStruct((1, CH), f32),
+            jax.ShapeDtypeStruct((1, CH), f32),
+            jax.ShapeDtypeStruct((7, 7, CH), f32),
+        ),
+        in_specs=[hbm] + [anywhere] * 14 + [hbm] * 3,
+        out_specs=(vmem,) * 6,
+        scratch_shapes=[pltpu.SemaphoreType.DMA((39,))],
+        compiler_params=pltpu.CompilerParams(vmem_limit_bytes=30 << 20),
+        cost_estimate=pl.CostEstimate(
+            flops=2 * PIX * 9 * EARLY * CH, bytes_accessed=6 << 20, transcendentals=0
+        ),
+        name="early",
+    )(*gathered, conv_bias.reshape(1, CH), depth_bias.reshape(1, CH), depth_weight)
+    outer, inner, mid, own = pl.pallas_call(
+        late_kernel,
         out_shape=(
             message,
             message,
             jax.ShapeDtypeStruct((2, COLS, CH), bf16),
             jax.ShapeDtypeStruct((4, COLS, CH), f32),
-            jax.ShapeDtypeStruct((1, CH), f32),
-            jax.ShapeDtypeStruct((1, CH), f32),
-            jax.ShapeDtypeStruct((7, 7, CH), f32),
         ),
-        in_specs=[anywhere] * 24,
-        out_specs=(vmem,) * 7,
+        in_specs=[vmem, anywhere, vmem, anywhere, vmem],
+        out_specs=(vmem,) * 4,
         scratch_shapes=[
-            pltpu.VMEM((PIX, 8 * CH), bf16),
-            pltpu.VMEM((9, 8 * CH, CH), bf16),
+            pltpu.VMEM((9, 2 * CH, CH), bf16),
             pltpu.VMEM((3, 6 * COLS, CH), f32),
             pltpu.VMEM((4, COLS, CH), bf16),
             pltpu.VMEM((4, COLS, CH), bf16),
-            pltpu.SemaphoreType.DMA((43,)),
+            pltpu.SemaphoreType.DMA((6,)),
         ],
-        compiler_params=pltpu.CompilerParams(vmem_limit_bytes=40 << 20),
-        cost_estimate=pl.CostEstimate(flops=2 * PIX * 9 * 1024 * CH, bytes_accessed=6 << 20, transcendentals=0),
-        name="conv",
-    )(
-        *blocks, *own_w, *other_w,
-        conv_bias.reshape(1, CH), depth_bias.reshape(1, CH), depth_weight,
-    )
+        compiler_params=pltpu.CompilerParams(vmem_limit_bytes=30 << 20),
+        cost_estimate=pl.CostEstimate(
+            flops=2 * PIX * 9 * 2 * CH * CH, bytes_accessed=4 << 20, transcendentals=0
+        ),
+        name="late",
+    )(xs, ws, acc, last, params[0])
     across = [(i, i + 1) for i in range(1, 31, 2)]
     from_outer = lax.ppermute(outer, "tile", across + [(j, i) for i, j in across])
     from_inner = lax.ppermute(inner, "tile", [(i, i ^ 1) for i in range(32)])

time: 65.6 us -> 72 us (1.098)
  the two profiles are of different devices: /device:TPU:1 before, /device:TPU:16 now
where the time goes in v1:
time: 72 us; the launch traced here: 71.7 us
  waiting for transfers between devices  27.6 us (38%)
  starting transfers between devices  20.3 us (28%)
  Pallas kernels  10.5 us (15%)
  blocking collectives  9.32 us (13%)
  local copies, waits for them, and re-layouts  3.92 us (5%)
    ppermute x14, waiting for transfers between devices, move(): return lax.ppermute(block, ('chan', 'tile'), pairs)  21.8 us
    ppermute x14, starting transfers between devices, move(): return lax.ppermute(block, ('chan', 'tile'), pairs)  14.9 us
    all_to_all x1, blocking collectives, gather_all(): lax.all_to_all(four, 'tile', 0, 0, tiled=True, axis_index_groups=groups)  9.32 us
    ppermute x1, waiting for transfers between devices, body(): lax.ppermute(outer, 'tile', across + [(j, i) for i, j in across])  5.85 us
    pallas_call x1, Pallas kernels, body(): pl.pallas_call(depth_kernel, out_shape=jax.ShapeDtypeStruct((ROWS, COLS,...  5.55 us
    ppermute x1, starting transfers between devices, body(): lax.ppermute(outer, 'tile', across + [(j, i) for i, j in across])  5.35 us
    pallas_call x1, Pallas kernels, body(): pl.pallas_call(early_kernel, out_shape=(jax.ShapeDtypeStruct((PIX, 8 * CH...  3.82 us
    unnamed x8, local copies, waits for them, and re-layouts  3 us
  transfers between devices with their start and end apart: 16, of which 7 were waited for; matrix products, arithmetic and copies ran while one was open for 0% of the time, Pallas kernels for 5%

profile of v1, /device:TPU:16, one launch (start us, length us, event | category | flops | bytes accessed | tf_op | source)
XLA Modules:
  0.0 71.7 jit_solution(7577652691545987781)
XLA Ops:
  0.0 0.9 %broadcast_in_dim.8 = bf16[4,9,32,128]{3,2,1,0:T(8,128)(2,1)S(1)} broadcast(bf16[9,32,128]{2,1,0:T(8,128)(2,1)} %bitcast.12), dimensions={1,2,3} | broadcast | bytes 368640 | tf_op jit(solution)/shard_map/broadcast_in_dim | solution.py:227
  0.9 9.3 %all_to_all.5.refs_8_ = bf16[36,32,128]{2,1,0:T(8,128)(2,1)S(1)} all-to-all(bf16[36,32,128]{2,1,0:T(8,128)(2,1)S(1)} %bitcast.11), channel_id=1, replica_groups={{0,1,16,17},{2,3,18,19},{4,5,20,21},{6,7,22,23},{8,9,24,25},{10,11,26,2..., dimensions={0} | all-to-all | bytes 589824 | tf_op jit(solution)/shard_map/all_to_all | solution.py:228
  10.2 1.9 %collective-permute-start.7 = (bf16[36,32,128]{2,1,0:T(8,128)(2,1)S(1)}, bf16[36,32,128]{2,1,0:T(8,128)(2,1)S(1)}, u32[]{:S(2)}, u32[]{:S(2)}) collective-permute-start(bf16[36,32,128]{2,1,0:T(8,128)(2,1)S(1)} %all_to_all.5.refs_8_), channel_id=1, source_target_pairs={{0,2},{1,15},{2,4},{3,1},{4,6},{5,3},{6,8},{7,5},{8,10},{9,7},{10,... | collective-permute-start | bytes 884744 | tf_op jit(solution)/shard_map/ppermute | solution.py:27
  12.2 8.6 %collective-permute-done.7.refs_9_ = bf16[36,32,128]{2,1,0:T(8,128)(2,1)S(1)} collective-permute-done((bf16[36,32,128]{2,1,0:T(8,128)(2,1)S(1)}, bf16[36,32,128]{2,1,0:T(8,128)(2,1)S(1)}, u32[]{:S(2)}, u32[]{:S(2)}) %collective-permute-start.7) | collective-permute-done | bytes 294944 | tf_op jit(solution)/shard_map/ppermute | solution.py:27
  20.8 1.3 %collective-permute-start = (bf16[1024,128]{1,0:T(8,128)(2,1)}, bf16[1024,128]{1,0:T(8,128)(2,1)S(1)}, u32[]{:S(2)}, u32[]{:S(2)}) collective-permute-start(bf16[1024,128]{1,0:T(8,128)(2,1)} %bitcast.5), channel_id=1, source_target_pairs={{0,32},{1,33},{2,34},{3,35},{4,36},{5,37},{6,38},{7,39},{8,40},{9,... | collective-permute-start | bytes 786440 | tf_op jit(solution)/shard_map/ppermute | solution.py:27
  22.1 1.5 %collective-permute-start.1 = (bf16[1024,128]{1,0:T(8,128)(2,1)}, bf16[1024,128]{1,0:T(8,128)(2,1)S(1)}, u32[]{:S(2)}, u32[]{:S(2)}) collective-permute-start(bf16[1024,128]{1,0:T(8,128)(2,1)} %bitcast.6), channel_id=1, source_target_pairs={{0,64},{1,193},{2,66},{3,195},{4,68},{5,197},{6,70},{7,199},{8,72}... | collective-permute-start | bytes 786440 | tf_op jit(solution)/shard_map/ppermute | solution.py:27
  23.6 2.1 %collective-permute-start.2 = (bf16[1024,128]{1,0:T(8,128)(2,1)}, bf16[1024,128]{1,0:T(8,128)(2,1)S(1)}, u32[]{:S(2)}, u32[]{:S(2)}) collective-permute-start(bf16[1024,128]{1,0:T(8,128)(2,1)} %bitcast.7), channel_id=1, source_target_pairs={{0,192},{1,65},{2,194},{3,67},{4,196},{5,69},{6,198},{7,71},{8,200... | collective-permute-start | bytes 786440 | tf_op jit(solution)/shard_map/ppermute | solution.py:27
  25.7 3.1 %collective-permute-done.8.refs_10_ = bf16[36,32,128]{2,1,0:T(8,128)(2,1)S(1)} collective-permute-done((bf16[36,32,128]{2,1,0:T(8,128)(2,1)S(1)}, bf16[36,32,128]{2,1,0:T(8,128)(2,1)S(1)}, u32[]{:S(2)}, u32[]{:S(2)}) %collective-permute-start.8) | collective-permute-done | bytes 294944 | tf_op jit(solution)/shard_map/ppermute | solution.py:27
  28.7 0.7 collective-permute-done.refs_1_
  29.4 2.8 %collective-permute-start.5 = (bf16[1024,128]{1,0:T(8,128)(2,1)S(1)}, bf16[1024,128]{1,0:T(8,128)(2,1)S(1)}, u32[]{:S(2)}, u32[]{:S(2)}) collective-permute-start(bf16[1024,128]{1,0:T(8,128)(2,1)S(1)} %collective-permute-done.refs_1_), channel_id=1, source_target_pairs={{0,192},{1,65},{2,194},{3,67},{4,196},{5,69},{6,198},{7,71},{8,200... | collective-permute-start | bytes 786440 | tf_op jit(solution)/shard_map/ppermute | solution.py:27
  32.2 1.3 %collective-permute-start.3 = (bf16[1024,128]{1,0:T(8,128)(2,1)S(1)}, bf16[1024,128]{1,0:T(8,128)(2,1)S(1)}, u32[]{:S(2)}, u32[]{:S(2)}) collective-permute-start(bf16[1024,128]{1,0:T(8,128)(2,1)S(1)} %collective-permute-done.1.refs_2_), channel_id=1, source_target_pairs={{0,32},{1,33},{2,34},{3,35},{4,36},{5,37},{6,38},{7,39},{8,40},{9,... | collective-permute-start | bytes 786440 | tf_op jit(solution)/shard_map/ppermute | solution.py:27
  33.7 2.2 %collective-permute-start.10 = (bf16[36,32,128]{2,1,0:T(8,128)(2,1)S(1)}, bf16[36,32,128]{2,1,0:T(8,128)(2,1)S(1)}, u32[]{:S(2)}, u32[]{:S(2)}) collective-permute-start(bf16[36,32,128]{2,1,0:T(8,128)(2,1)S(1)} %collective-permute-done.7.refs_9_), channel_id=1, source_target_pairs={{0,1},{1,0},{2,3},{3,2},{4,5},{5,4},{6,7},{7,6},{8,9},{9,8},{10,11... | collective-permute-start | bytes 884744 | tf_op jit(solution)/shard_map/ppermute | solution.py:27
  35.9 1.1 %collective-permute-done.5.refs_6_ = bf16[1024,128]{1,0:T(8,128)(2,1)S(1)} collective-permute-done((bf16[1024,128]{1,0:T(8,128)(2,1)S(1)}, bf16[1024,128]{1,0:T(8,128)(2,1)S(1)}, u32[]{:S(2)}, u32[]{:S(2)}) %collective-permute-start.5) | collective-permute-done | bytes 262176 | tf_op jit(solution)/shard_map/ppermute | solution.py:27
  37.5 3.0 %collective-permute-done.3.refs_4_ = bf16[1024,128]{1,0:T(8,128)(2,1)S(1)} collective-permute-done((bf16[1024,128]{1,0:T(8,128)(2,1)S(1)}, bf16[1024,128]{1,0:T(8,128)(2,1)S(1)}, u32[]{:S(2)}, u32[]{:S(2)}) %collective-permute-start.3) | collective-permute-done | bytes 262176 | tf_op jit(solution)/shard_map/ppermute | solution.py:27
  40.5 1.1 %collective-permute-start.6 = (bf16[1024,128]{1,0:T(8,128)(2,1)S(1)}, bf16[1024,128]{1,0:T(8,128)(2,1)S(1)}, u32[]{:S(2)}, u32[]{:S(2)}) collective-permute-start(bf16[1024,128]{1,0:T(8,128)(2,1)S(1)} %collective-permute-done.5.refs_6_), channel_id=1, source_target_pairs={{0,64},{1,193},{2,66},{3,195},{4,68},{5,197},{6,70},{7,199},{8,72}... | collective-permute-start | bytes 786440 | tf_op jit(solution)/shard_map/ppermute | solution.py:27
  41.6 5.3 %collective-permute-done.6.refs_7_ = bf16[1024,128]{1,0:T(8,128)(2,1)S(1)} collective-permute-done((bf16[1024,128]{1,0:T(8,128)(2,1)S(1)}, bf16[1024,128]{1,0:T(8,128)(2,1)S(1)}, u32[]{:S(2)}, u32[]{:S(2)}) %collective-permute-start.6) | collective-permute-done | bytes 262176 | tf_op jit(solution)/shard_map/ppermute | solution.py:27
  46.9 0.9 %copy-done = bf16[4,256,128]{2,1,0:T(8,128)(2,1)S(1)} copy-done((bf16[4,256,128]{2,1,0:T(8,128)(2,1)S(1)}, bf16[4,256,128]{2,1,0:T(8,128)(2,1)}, u32[]{:S(2)}) %copy-start) | copy-done | bytes 262168
  47.9 0.7 %copy-done.1 = f32[7,7,128]{2,1,0:T(8,128)S(1)} copy-done((f32[7,7,128]{2,1,0:T(8,128)S(1)}, f32[7,7,128]{2,1,0:T(8,128)}, u32[]{:S(2)}) %copy-start.1) | copy-done | bytes 25112
  48.6 0.7 copy-done.2
  49.9 3.8 %early.1 = (bf16[1024,1024]{1,0:T(8,128)(2,1)S(1)}, bf16[9,1024,128]{2,1,0:T(8,128)(2,1)S(1)}, f32[3,1536,128]{2,1,0:T(8,128)S(1)}, f32[1,128]{1,0:T(1,128)S(1)}...) custom-call(bf16[1024,128]{1,0:T(8,128)(2,1)S(1)} %bitcast.8, bf16[1024,128]{1,0:T(8,128)(2,1)S(1)} %collective-permute-done.refs_1_, ...), custom_call_target="tpu_custom_call" | custom-call | flops 1811939328 | bytes 6291456 | tf_op jit(solution)/shard_map/early/pallas_call | solution.py:248
  53.8 1.1 %late.1 = (bf16[4,256,128]{2,1,0:T(8,128)(2,1)S(1)}, bf16[4,256,128]{2,1,0:T(8,128)(2,1)S(1)}, bf16[2,256,128]{2,1,0:T(8,128)(2,1)S(1)}, f32[4,256,128]{2,1,0:T(8,128)S(1)}) custom-call(bf16[1024,1024]{1,0:T(8,128)(2,1)S(1)} %get-tuple-element.15.xs, bf16[9,1024,128]{2,1,0:T(8,128)(2,1)S(1)} %get-tuple-element.16.ws_early, ...), custom_call_target="tpu_custom_call" | custom-call | flops 603979776 | bytes 4194304 | tf_op jit(solution)/shard_map/late/pallas_call | solution.py:267
  54.9 5.3 %collective-permute-start.14 = (bf16[4,256,128]{2,1,0:T(8,128)(2,1)S(1)}, bf16[4,256,128]{2,1,0:T(8,128)(2,1)S(1)}, u32[]{:S(2)}, u32[]{:S(2)}) collective-permute-start(bf16[4,256,128]{2,1,0:T(8,128)(2,1)S(1)} %get-tuple-element.21), channel_id=1, source_target_pairs={{1,2},{3,4},{5,6},{7,8},{9,10},{11,12},{13,14},{15,16},{17,18},{19... | collective-permute-start | bytes 786440 | tf_op jit(solution)/shard_map/ppermute | solution.py:291
  60.3 5.8 %collective-permute-done.14.from_outer = bf16[4,256,128]{2,1,0:T(8,128)(2,1)S(1)} collective-permute-done((bf16[4,256,128]{2,1,0:T(8,128)(2,1)S(1)}, bf16[4,256,128]{2,1,0:T(8,128)(2,1)S(1)}, u32[]{:S(2)}, u32[]{:S(2)}) %collective-permute-start.14) | collective-permute-done | bytes 262176 | tf_op jit(solution)/shard_map/ppermute | solution.py:291
  66.2 5.5 %depth.1 = bf16[4,256,128]{2,1,0:T(8,128)(2,1)} custom-call(f32[4,256,128]{2,1,0:T(8,128)S(1)} %get-tuple-element.19.own, bf16[2,256,128]{2,1,0:T(8,128)(2,1)S(1)} %get-tuple-element.20.mid, bf16[4,256,128]{2,1,0:T(8,128)(2,1)S(1)} %collective-permute-done.14.from_outer, bf16[4,256,128]{2,1,0:T(8,128)(2,1)S(1)} %collective-permute-done.15.from_inner, ...), custom_call_target="tpu_custom_call" | custom-call | flops 12845056 | bytes 2097152 | tf_op jit(solution)/shard_map/depth/pallas_call | solution.py:293
  (21 shorter events, 1.5 us)
Async XLA Ops:
  10.2 10.6 %collective-permute-start.7 = (bf16[36,32,128]{2,1,0:T(8,128)(2,1)S(1)}, bf16[36,32,128]{2,1,0:T(8,128)(2,1)S(1)}, u32[]{:S(2)}, u32[]{:S(2)}) collective-permute-start(bf16[36,32,128]{2,1,0:T(8,128)(2,1)S(1)} %all_to_all.5.refs_8_), channel_id=1, source_target_pairs={{0,2},{1,15},{2,4},{3,1},{4,6},{5,3},{6,8},{7,5},{8,10},{9,7},{10,... | collective-permute-start | bytes 884744 | tf_op jit(solution)/shard_map/ppermute | solution.py:27
  20.8 7.9 %collective-permute-start.8 = (bf16[36,32,128]{2,1,0:T(8,128)(2,1)S(1)}, bf16[36,32,128]{2,1,0:T(8,128)(2,1)S(1)}, u32[]{:S(2)}, u32[]{:S(2)}) collective-permute-start(bf16[36,32,128]{2,1,0:T(8,128)(2,1)S(1)} %collective-permute-done.7.refs_9_), channel_id=1, source_target_pairs={{0,2},{1,15},{2,4},{3,1},{4,6},{5,3},{6,8},{7,5},{8,10},{9,7},{10,... | collective-permute-start | bytes 884744 | tf_op jit(solution)/shard_map/ppermute | solution.py:27
  20.8 8.6 %collective-permute-start = (bf16[1024,128]{1,0:T(8,128)(2,1)}, bf16[1024,128]{1,0:T(8,128)(2,1)S(1)}, u32[]{:S(2)}, u32[]{:S(2)}) collective-permute-start(bf16[1024,128]{1,0:T(8,128)(2,1)} %bitcast.5), channel_id=1, source_target_pairs={{0,32},{1,33},{2,34},{3,35},{4,36},{5,37},{6,38},{7,39},{8,40},{9,... | collective-permute-start | bytes 786440 | tf_op jit(solution)/shard_map/ppermute | solution.py:27
  22.1 10.1 %collective-permute-start.1 = (bf16[1024,128]{1,0:T(8,128)(2,1)}, bf16[1024,128]{1,0:T(8,128)(2,1)S(1)}, u32[]{:S(2)}, u32[]{:S(2)}) collective-permute-start(bf16[1024,128]{1,0:T(8,128)(2,1)} %bitcast.6), channel_id=1, source_target_pairs={{0,64},{1,193},{2,66},{3,195},{4,68},{5,197},{6,70},{7,199},{8,72}... | collective-permute-start | bytes 786440 | tf_op jit(solution)/shard_map/ppermute | solution.py:27
  23.6 9.9 %collective-permute-start.2 = (bf16[1024,128]{1,0:T(8,128)(2,1)}, bf16[1024,128]{1,0:T(8,128)(2,1)S(1)}, u32[]{:S(2)}, u32[]{:S(2)}) collective-permute-start(bf16[1024,128]{1,0:T(8,128)(2,1)} %bitcast.7), channel_id=1, source_target_pairs={{0,192},{1,65},{2,194},{3,67},{4,196},{5,69},{6,198},{7,71},{8,200... | collective-permute-start | bytes 786440 | tf_op jit(solution)/shard_map/ppermute | solution.py:27
  28.7 8.3 %collective-permute-start.9 = (bf16[36,32,128]{2,1,0:T(8,128)(2,1)S(1)}, bf16[36,32,128]{2,1,0:T(8,128)(2,1)S(1)}, u32[]{:S(2)}, u32[]{:S(2)}) collective-permute-start(bf16[36,32,128]{2,1,0:T(8,128)(2,1)S(1)} %collective-permute-done.8.refs_10_), channel_id=1, source_target_pairs={{0,2},{1,15},{2,4},{3,1},{4,6},{5,3},{6,8},{7,5},{8,10},{9,7},{10,... | collective-permute-start | bytes 884744 | tf_op jit(solution)/shard_map/ppermute | solution.py:27
  29.4 7.6 %collective-permute-start.5 = (bf16[1024,128]{1,0:T(8,128)(2,1)S(1)}, bf16[1024,128]{1,0:T(8,128)(2,1)S(1)}, u32[]{:S(2)}, u32[]{:S(2)}) collective-permute-start(bf16[1024,128]{1,0:T(8,128)(2,1)S(1)} %collective-permute-done.refs_1_), channel_id=1, source_target_pairs={{0,192},{1,65},{2,194},{3,67},{4,196},{5,69},{6,198},{7,71},{8,200... | collective-permute-start | bytes 786440 | tf_op jit(solution)/shard_map/ppermute | solution.py:27
  32.2 8.3 %collective-permute-start.3 = (bf16[1024,128]{1,0:T(8,128)(2,1)S(1)}, bf16[1024,128]{1,0:T(8,128)(2,1)S(1)}, u32[]{:S(2)}, u32[]{:S(2)}) collective-permute-start(bf16[1024,128]{1,0:T(8,128)(2,1)S(1)} %collective-permute-done.1.refs_2_), channel_id=1, source_target_pairs={{0,32},{1,33},{2,34},{3,35},{4,36},{5,37},{6,38},{7,39},{8,40},{9,... | collective-permute-start | bytes 786440 | tf_op jit(solution)/shard_map/ppermute | solution.py:27
  33.5 8.1 %collective-permute-start.4 = (bf16[1024,128]{1,0:T(8,128)(2,1)S(1)}, bf16[1024,128]{1,0:T(8,128)(2,1)S(1)}, u32[]{:S(2)}, u32[]{:S(2)}) collective-permute-start(bf16[1024,128]{1,0:T(8,128)(2,1)S(1)} %collective-permute-done.2.refs_3_), channel_id=1, source_target_pairs={{0,64},{1,193},{2,66},{3,195},{4,68},{5,197},{6,70},{7,199},{8,72}... | collective-permute-start | bytes 786440 | tf_op jit(solution)/shard_map/ppermute | solution.py:27
  33.7 13.2 %collective-permute-start.10 = (bf16[36,32,128]{2,1,0:T(8,128)(2,1)S(1)}, bf16[36,32,128]{2,1,0:T(8,128)(2,1)S(1)}, u32[]{:S(2)}, u32[]{:S(2)}) collective-permute-start(bf16[36,32,128]{2,1,0:T(8,128)(2,1)S(1)} %collective-permute-done.7.refs_9_), channel_id=1, source_target_pairs={{0,1},{1,0},{2,3},{3,2},{4,5},{5,4},{6,7},{7,6},{8,9},{9,8},{10,11... | collective-permute-start | bytes 884744 | tf_op jit(solution)/shard_map/ppermute | solution.py:27
  37.0 9.9 %collective-permute-start.11 = (bf16[36,32,128]{2,1,0:T(8,128)(2,1)S(1)}, bf16[36,32,128]{2,1,0:T(8,128)(2,1)S(1)}, u32[]{:S(2)}, u32[]{:S(2)}) collective-permute-start(bf16[36,32,128]{2,1,0:T(8,128)(2,1)S(1)} %collective-permute-done.8.refs_10_), channel_id=1, source_target_pairs={{0,1},{1,0},{2,3},{3,2},{4,5},{5,4},{6,7},{7,6},{8,9},{9,8},{10,11... | collective-permute-start | bytes 884744 | tf_op jit(solution)/shard_map/ppermute | solution.py:27
  37.0 9.9 %collective-permute-start.12 = (bf16[36,32,128]{2,1,0:T(8,128)(2,1)S(1)}, bf16[36,32,128]{2,1,0:T(8,128)(2,1)S(1)}, u32[]{:S(2)}, u32[]{:S(2)}) collective-permute-start(bf16[36,32,128]{2,1,0:T(8,128)(2,1)S(1)} %collective-permute-done.9.refs_11_), channel_id=1, source_target_pairs={{0,1},{1,0},{2,3},{3,2},{4,5},{5,4},{6,7},{7,6},{8,9},{9,8},{10,11... | collective-permute-start | bytes 884744 | tf_op jit(solution)/shard_map/ppermute | solution.py:27
  40.5 6.4 %collective-permute-start.6 = (bf16[1024,128]{1,0:T(8,128)(2,1)S(1)}, bf16[1024,128]{1,0:T(8,128)(2,1)S(1)}, u32[]{:S(2)}, u32[]{:S(2)}) collective-permute-start(bf16[1024,128]{1,0:T(8,128)(2,1)S(1)} %collective-permute-done.5.refs_6_), channel_id=1, source_target_pairs={{0,64},{1,193},{2,66},{3,195},{4,68},{5,197},{6,70},{7,199},{8,72}... | collective-permute-start | bytes 786440 | tf_op jit(solution)/shard_map/ppermute | solution.py:27
  41.6 12.2 %collective-permute-start.13 = (bf16[36,32,128]{2,1,0:T(8,128)(2,1)S(1)}, bf16[36,32,128]{2,1,0:T(8,128)(2,1)S(1)}, u32[]{:S(2)}, u32[]{:S(2)}) collective-permute-start(bf16[36,32,128]{2,1,0:T(8,128)(2,1)S(1)} %collective-permute-done.9.refs_11_), channel_id=1, source_target_pairs={{0,2},{1,15},{2,4},{3,1},{4,6},{5,3},{6,8},{7,5},{8,10},{9,7},{10,... | collective-permute-start | bytes 884744 | tf_op jit(solution)/shard_map/ppermute | solution.py:27
  46.9 1.0 %copy-start = (bf16[4,256,128]{2,1,0:T(8,128)(2,1)S(1)}, bf16[4,256,128]{2,1,0:T(8,128)(2,1)}, u32[]{:S(2)}) copy-start(bf16[4,256,128]{2,1,0:T(8,128)(2,1)} %param.5) | copy-start | bytes 786436
  47.8 0.7 %copy-start.1 = (f32[7,7,128]{2,1,0:T(8,128)S(1)}, f32[7,7,128]{2,1,0:T(8,128)}, u32[]{:S(2)}) copy-start(f32[7,7,128]{2,1,0:T(8,128)} %refs_17_.1) | copy-start | bytes 75268
  48.6 0.7 copy-start.2
  49.3 0.7 copy-start.3
  54.9 11.3 %collective-permute-start.14 = (bf16[4,256,128]{2,1,0:T(8,128)(2,1)S(1)}, bf16[4,256,128]{2,1,0:T(8,128)(2,1)S(1)}, u32[]{:S(2)}, u32[]{:S(2)}) collective-permute-start(bf16[4,256,128]{2,1,0:T(8,128)(2,1)S(1)} %get-tuple-element.21), channel_id=1, source_target_pairs={{1,2},{3,4},{5,6},{7,8},{9,10},{11,12},{13,14},{15,16},{17,18},{19... | collective-permute-start | bytes 786440 | tf_op jit(solution)/shard_map/ppermute | solution.py:291
  60.2 6.0 %collective-permute-start.15 = (bf16[4,256,128]{2,1,0:T(8,128)(2,1)S(1)}, bf16[4,256,128]{2,1,0:T(8,128)(2,1)S(1)}, u32[]{:S(2)}, u32[]{:S(2)}) collective-permute-start(bf16[4,256,128]{2,1,0:T(8,128)(2,1)S(1)} %get-tuple-element.22), channel_id=1, source_target_pairs={{0,1},{1,0},{2,3},{3,2},{4,5},{5,4},{6,7},{7,6},{8,9},{9,8},{10,11... | collective-permute-start | bytes 786440 | tf_op jit(solution)/shard_map/ppermute | solution.py:292

commit v2 on v1

v2 whole, which is shorter than its diff:
```python
import jax
import jax.numpy as jnp
from jax import lax
from jax.experimental import pallas as pl
from jax.experimental.pallas import tpu as pltpu
from jax.sharding import PartitionSpec as P


ROWS, COLS, CH = 4, 256, 128
PIX = ROWS * COLS


def over_a(x):
    return x ^ 1


def over_b(x):
    return (x + 1 if x % 2 else x - 1) % 4


def move(block, partner):
    pairs = []
    for chan in range(8):
        for tile in range(32):
            x, y, hi, z, core = partner(chan // 2, chan % 2, tile // 16, (tile // 2) % 8, tile % 2)
            pairs.append((chan * 32 + tile, (2 * x + y) * 32 + (hi * 8 + z % 8) * 2 + core))
    return lax.ppermute(block, ("chan", "tile"), pairs)


def to_y(x, y, hi, z, core):
    return x, 1 - y, hi, z, core


def to_l(x, y, hi, z, core):
    return (over_b(x) if core else over_a(x)), y, hi, z, core


def to_m(x, y, hi, z, core):
    return (over_a(x) if core else over_b(x)), y, hi, z, core


def to_hi(x, y, hi, z, core):
    return x, y, 1 - hi, z, core


def to_core(x, y, hi, z, core):
    return x, y, hi, z, 1 - core


def to_next(x, y, hi, z, core):
    return x, y, hi, (z - 1 if core else z + 1), core


TAPS = (((0, 0), (0, 1)), ((0, 2), (2, 0)), ((2, 1), (2, 2)), ((1, 0), (1, 1)), ((1, 2),))
EARLY = 6 * CH


def add_taps(pixels, filters, acc):
    for taps in TAPS:
        columns = [filters(3 * a + b) for a, b in taps]
        rhs = jnp.concatenate(columns, axis=1) if len(taps) > 1 else columns[0]
        result = jnp.dot(pixels(), rhs, preferred_element_type=jnp.float32)
        for at, (a, b) in enumerate(taps):
            part = result[:, at * CH : (at + 1) * CH]
            if a == 0:
                acc[b, 512:1536, :] = part
            elif a == 2:
                acc[b, 0:512, :] = part[0:512]
                acc[b, 512:1024, :] += part[512:1024]
            else:
                acc[b, 256:1280, :] += part


class Copies:
    def __init__(self, sems):
        self.sems, self.started = sems, []

    def start(self, src, dst):
        copy = pltpu.make_async_copy(src, dst, self.sems.at[len(self.started)])
        copy.start()
        self.started.append(copy)

    def wait(self):
        for copy in self.started:
            copy.wait()


def block_at(pair, half, z):
    return 2 * ((pair - z // 2 + 5) % 4) + half


def filter_rows(z, at_z, half, at_core, first):
    row = block_at(at_z // 2, half, z) * CH + (at_z % 2) * 64 + at_core * 32 - first
    return pl.ds(pl.multiple_of(row, 32), 32)


def early_kernel(*refs):
    blocks, own_w, other_w, small = refs[:8], refs[8:12], refs[12:15], refs[15:18]
    (xs, ws, acc, *params), sems = refs[18:24], refs[24]
    chan, tile = lax.axis_index("chan"), lax.axis_index("tile")
    x, y = chan // 2, chan % 2
    y_hi, z, core = tile // 16, (tile // 2) % 8, tile % 2
    turn = 1 - 2 * ((x + core) % 2)
    xl, xm, xf = (x + turn + 4) % 4, (x - turn + 4) % 4, (x + 2) % 4
    copies = Copies(sems)
    places = ((x, y), (x, 1 - y), (xl, y), (xm, y), (xl, 1 - y), (xf, y), (xm, 1 - y), (xf, 1 - y))
    for block, (at_x, at_y) in zip(blocks, places):
        index = 2 * at_x + at_y
        at = block_at(index % 4, index // 4, z)
        copies.start(block, xs.at[:, pl.ds(pl.multiple_of(at * CH, CH), CH)])

    def place(array, at_z, at_core):
        for piece in range(array.shape[0] // 9):
            rows = filter_rows(z, at_z, (y_hi + piece // 2) % 2, (at_core + piece) % 2, 0)
            copies.start(array.at[pl.ds(9 * piece, 9)], ws.at[:, rows, :])

    back = 1 - 2 * core
    for steps, array in enumerate(own_w):
        place(array, (z - steps * back + 8) % 8, core)
    for steps, array in enumerate(other_w):
        place(array, (z + (steps + 1) * back + 8) % 8, 1 - core)
    for source, target in zip(small, params):
        copies.start(source, target)
    copies.wait()
    add_taps(lambda: xs[:, 0:EARLY], lambda tap: ws[tap, 0:EARLY, :], acc)


def late_kernel(xs, ws_early, acc_early, last, bias, outer, inner, mid, own, ws, acc, sems):
    tile = lax.axis_index("tile")
    y_hi, z, core = tile // 16, (tile // 2) % 8, tile % 2
    copies = Copies(sems)
    for half in range(2):
        rows = pl.ds(pl.multiple_of(half * CH + (1 - z % 2) * 64, 64), 64)
        early = pl.ds(pl.multiple_of(EARLY + half * CH + (1 - z % 2) * 64, 64), 64)
        copies.start(ws_early.at[:, early, :], ws.at[:, rows, :])
    for piece in range(4):
        rows = filter_rows(z, (z + 4) % 8, (y_hi + piece // 2) % 2, (core + piece) % 2, EARLY)
        copies.start(last.at[pl.ds(9 * piece, 9)], ws.at[:, rows, :])
    copies.wait()
    add_taps(lambda: xs[:, EARLY : 8 * CH], lambda tap: ws[tap], acc)

    column = lax.broadcasted_iota(jnp.int32, (COLS, CH), 0)

    def row_sum(row):
        rows = pl.ds(pl.multiple_of((row + 1 + core * (3 - 2 * row)) * COLS, COLS), COLS)
        total = [acc[b, rows, :] + acc_early[b, rows, :] for b in range(3)]
        left = jnp.where(column == 0, 0.0, pltpu.roll(total[0], 1, 0))
        right = jnp.where(column == COLS - 1, 0.0, pltpu.roll(total[2], COLS - 1, 0))
        return total[1] + left + right

    for slot, row in enumerate((-1, 0, 4, 3)):
        value = row_sum(row)
        own[slot] = value
        if slot < 2:
            outer[slot] = value.astype(jnp.bfloat16)
        else:
            inner[slot - 2] = value.astype(jnp.bfloat16)
    for slot, row in enumerate((1, 2)):
        value = jnp.maximum(row_sum(row) + bias[...], 0.0).astype(jnp.bfloat16)
        mid[slot] = value
        outer[2 + slot] = value
        inner[3 - slot] = value


def add_depth(rows, first, weight, hidden, begin, finish):
    core = lax.axis_index("tile") % 2
    pad = jnp.zeros((len(rows), 8, CH), jnp.float32)
    hidden[:, 0:8, :] = pad
    hidden[:, 264:272, :] = pad
    for at, value in enumerate(rows):
        hidden[at, 8:264, :] = value
    width = 32

    def strip(step, _):
        start = pl.multiple_of(step * width, width)
        sums = [begin(row, pl.ds(start, width)) for row in range(ROWS)]
        for at in range(len(rows)):
            for b in range(7):
                value = hidden[at, pl.ds(start + (5 + b), width), :]
                for row in range(ROWS):
                    a = first + at - row + 3
                    if 0 <= a < 7:
                        sums[row] = sums[row] + value * weight[a + core * (6 - 2 * a), b : b + 1, :]
        for row in range(ROWS):
            finish(row, pl.ds(start, width), sums[row])
        return 0

    lax.fori_loop(0, COLS // width, strip, 0)


def activate(value, bias):
    return jnp.maximum(value + bias[...], 0.0).astype(jnp.bfloat16).astype(jnp.float32)


def depth_early_kernel(own, mid, inner, bias, depth_bias, weight, part, hidden):
    f32 = jnp.float32
    rows = (
        mid[0].astype(f32),
        mid[1].astype(f32),
        activate(own[3] + inner[0].astype(f32), bias),
        activate(inner[1].astype(f32) + own[2], bias),
        inner[2].astype(f32),
        inner[3].astype(f32),
    )

    def finish(row, columns, value):
        part[row, columns, :] = value

    add_depth(
        rows, 1, weight, hidden,
        lambda row, columns: jnp.zeros((columns.size, CH), f32) + depth_bias[...], finish,
    )


def depth_late_kernel(part, own, outer, bias, weight, out, hidden):
    f32 = jnp.float32
    tile = lax.axis_index("tile")
    core = tile % 2
    inside = jnp.logical_and(tile > 0, tile < 31).astype(f32)
    rows = (
        outer[3].astype(f32) * inside,
        outer[2].astype(f32) * inside,
        activate(outer[1].astype(f32) + own[0], bias) * inside,
        activate(own[1] + outer[0].astype(f32), bias),
    )

    def finish(row, columns, value):
        out[row + core * (3 - 2 * row), columns, :] = value.astype(jnp.bfloat16)

    add_depth(rows, -3, weight, hidden, lambda row, columns: part[row, columns, :], finish)


def gather_all(pixels, weight):
    p0 = pixels.reshape(PIX, CH)
    w0 = weight.reshape(9, 32, CH)
    h0 = move(w0, to_hi)
    w0_other = move(w0, to_core)
    p_y, p_l, p_m = move(p0, to_y), move(p0, to_l), move(p0, to_m)
    w0 = jnp.concatenate([w0, w0_other, h0, move(h0, to_core)])
    w1 = move(w0, to_next)
    w2 = move(w1, to_next)
    o1 = move(w1, to_core)
    p_ly, p_ml, p_ym = move(p_l, to_y), move(p_m, to_l), move(p_y, to_m)
    w3 = move(w2, to_next)
    o2 = move(w2, to_core)
    p_far = move(p_ym, to_l)
    w4 = move(w3, to_next)
    o3 = move(w3, to_core)
    return (in_hbm(p0), p_y, p_l, p_m, p_ly, p_ml, p_ym, p_far, w0, w1, w2, w3, o1, o2, o3), w4


def in_hbm(array):
    return pltpu.with_memory_space_constraint(array, pltpu.HBM)


def body(pixels, conv_weight, conv_bias, depth_weight, depth_bias):
    anywhere, vmem = pl.BlockSpec(memory_space=pl.ANY), pl.BlockSpec(memory_space=pltpu.VMEM)
    hbm = pl.BlockSpec(memory_space=pltpu.HBM)
    f32, bf16 = jnp.float32, jnp.bfloat16
    message = jax.ShapeDtypeStruct((4, COLS, CH), bf16)
    gathered, last = gather_all(pixels, conv_weight)
    xs, ws, acc, *params = pl.pallas_call(
        early_kernel,
        out_shape=(
            jax.ShapeDtypeStruct((PIX, 8 * CH), bf16),
            jax.ShapeDtypeStruct((9, 8 * CH, CH), bf16),
            jax.ShapeDtypeStruct((3, 6 * COLS, CH), f32),
            jax.ShapeDtypeStruct((1, CH), f32),
            jax.ShapeDtypeStruct((1, CH), f32),
            jax.ShapeDtypeStruct((7, 7, CH), f32),
        ),
        in_specs=[hbm] + [anywhere] * 14 + [hbm] * 3,
        out_specs=(vmem,) * 6,
        scratch_shapes=[pltpu.SemaphoreType.DMA((39,))],
        compiler_params=pltpu.CompilerParams(vmem_limit_bytes=30 << 20),
        cost_estimate=pl.CostEstimate(
            flops=2 * PIX * 9 * EARLY * CH, bytes_accessed=6 << 20, transcendentals=0
        ),
        name="early",
    )(
        *gathered,
        in_hbm(conv_bias.reshape(1, CH)),
        in_hbm(depth_bias.reshape(1, CH)),
        in_hbm(depth_weight),
    )
    outer, inner, mid, own = pl.pallas_call(
        late_kernel,
        out_shape=(
            message,
            message,
            jax.ShapeDtypeStruct((2, COLS, CH), bf16),
            jax.ShapeDtypeStruct((4, COLS, CH), f32),
        ),
        in_specs=[vmem, anywhere, vmem, anywhere, vmem],
        out_specs=(vmem,) * 4,
        scratch_shapes=[
            pltpu.VMEM((9, 2 * CH, CH), bf16),
            pltpu.VMEM((3, 6 * COLS, CH), f32),
            pltpu.SemaphoreType.DMA((6,)),
        ],
        compiler_params=pltpu.CompilerParams(vmem_limit_bytes=30 << 20),
        cost_estimate=pl.CostEstimate(
            flops=2 * PIX * 9 * 2 * CH * CH, bytes_accessed=4 << 20, transcendentals=0
        ),
        name="late",
    )(xs, ws, acc, last, params[0])
    bias, depth_bias, weight = params
    across = [(i, i + 1) for i in range(1, 31, 2)]
    from_outer = lax.ppermute(outer, "tile", across + [(j, i) for i, j in across])
    from_inner = lax.ppermute(inner, "tile", [(i, i ^ 1) for i in range(32)])
    part = depth(depth_early_kernel, f32, 6, own, mid, from_inner, bias, depth_bias, weight)
    return depth(depth_late_kernel, bf16, 4, part, own, from_outer, bias, weight)


def depth(kernel, dtype, rows, *operands):
    vmem = pl.BlockSpec(memory_space=pltpu.VMEM)
    return pl.pallas_call(
        kernel,
        out_shape=jax.ShapeDtypeStruct((ROWS, COLS, CH), dtype),
        in_specs=[vmem] * len(operands),
        out_specs=vmem,
        scratch_shapes=[pltpu.VMEM((rows, COLS + 16, CH), jnp.float32)],
        compiler_params=pltpu.CompilerParams(vmem_limit_bytes=20 << 20),
        cost_estimate=pl.CostEstimate(flops=5 * rows * COLS * 49 * CH, bytes_accessed=2 << 20, transcendentals=0),
        name="depth",
    )(*operands)


def solution(mesh):
    in_specs = (
        P("tile", None, "chan"),
        P(None, None, "tile", "chan"),
        P("chan"),
        P(None, None, "chan"),
        P("chan"),
    )
    out_specs = P("tile", None, "chan")
    return jax.shard_map(body, mesh=mesh, in_specs=in_specs, out_specs=out_specs, check_vma=False)
```

time: 72 us -> 64.9 us (0.901)
  blocking collectives: 9.32 us -> 0 us
  waiting for transfers between devices: 27.6 us -> 35.4 us
  local copies, waits for them, and re-layouts: 3.92 us -> 0 us
  Pallas kernels: 10.5 us -> 8.91 us
  other arithmetic: 0 us -> 0.92 us
  starting transfers between devices: 20.3 us -> 19.4 us
    all_to_all x1 -> x0, blocking collectives: 9.32 us -> none  [gather_all(): lax.all_to_all(four, 'tile', 0, 0, tiled=True, axis_index_groups=groups)]
    ppermute x14 -> x17, waiting for transfers between devices: 21.8 us -> 28 us  [move(): return lax.ppermute(block, ('chan', 'tile'), pairs)]
    unnamed x8 -> x0, local copies, waits for them, and re-layouts: 3 us -> none
    pallas_call x1 -> x2, Pallas kernels: 5.55 us -> 2.86 us  [depth(): pl.pallas_call(kernel, out_shape=jax.ShapeDtypeStruct((ROWS, COLS, CH), d...]
    ppermute x1, starting transfers between devices: 5.35 us -> 2.67 us  [body(): lax.ppermute(outer, 'tile', across + [(j, i) for i, j in across])]
    ppermute x14 -> x17, starting transfers between devices: 14.9 us -> 16.4 us  [move(): return lax.ppermute(block, ('chan', 'tile'), pairs)]
    ppermute x1, waiting for transfers between devices: 5.85 us -> 7.36 us  [body(): lax.ppermute(outer, 'tile', across + [(j, i) for i, j in across])]
    concatenate x0 -> x1, other arithmetic: none -> 0.92 us  [gather_all(): w0 = jnp.concatenate([w0, w0_other, h0, move(h0, to_core)])]
  transfers between devices with their start and end apart: 16 -> 19, of which waited for: 7 -> 10; matrix products, arithmetic and copies ran while one was open for 0% -> 0% of each run, Pallas kernels for 5% -> 9%
where the time goes in v2:
time: 64.9 us; the launch traced here: 64.7 us
  waiting for transfers between devices  35.4 us (55%)
  starting transfers between devices  19.4 us (30%)
  Pallas kernels  8.91 us (14%)
  other arithmetic  0.92 us (1%)
    ppermute x17, waiting for transfers between devices, move(): return lax.ppermute(block, ('chan', 'tile'), pairs)  28 us
    ppermute x17, starting transfers between devices, move(): return lax.ppermute(block, ('chan', 'tile'), pairs)  16.4 us
    ppermute x1, waiting for transfers between devices, body(): lax.ppermute(outer, 'tile', across + [(j, i) for i, j in across])  7.36 us
    pallas_call x1, Pallas kernels, body(): pl.pallas_call(early_kernel, out_shape=(jax.ShapeDtypeStruct((PIX, 8 * CH...  4.54 us
    pallas_call x2, Pallas kernels, depth(): pl.pallas_call(kernel, out_shape=jax.ShapeDtypeStruct((ROWS, COLS, CH), d...  2.86 us
    ppermute x1, starting transfers between devices, body(): lax.ppermute(outer, 'tile', across + [(j, i) for i, j in across])  2.67 us
    pallas_call x1, Pallas kernels, body(): pl.pallas_call(late_kernel, out_shape=(message, message, jax.ShapeDtypeSt...  1.51 us
  transfers between devices with their start and end apart: 19, of which 10 were waited for; matrix products, arithmetic and copies ran while one was open for 0% of the time, Pallas kernels for 9%

profile of v2, /device:TPU:16, one launch (start us, length us, event | category | flops | bytes accessed | tf_op | source)
XLA Modules:
  0.0 64.7 jit_solution(8871048169358867678)
XLA Ops:
  0.0 2.0 %collective-permute-start.8 = (bf16[9,32,128]{2,1,0:T(8,128)(2,1)}, bf16[9,32,128]{2,1,0:T(8,128)(2,1)S(1)}, u32[]{:S(2)}, u32[]{:S(2)}) collective-permute-start(bf16[9,32,128]{2,1,0:T(8,128)(2,1)} %bitcast.4), channel_id=1, source_target_pairs={{0,16},{1,17},{2,18},{3,19},{4,20},{5,21},{6,22},{7,23},{8,24},{9,... | collective-permute-start | bytes 221192 | tf_op jit(solution)/shard_map/ppermute | solution.py:27
  2.0 4.0 %collective-permute-done.8 = bf16[9,32,128]{2,1,0:T(8,128)(2,1)S(1)} collective-permute-done((bf16[9,32,128]{2,1,0:T(8,128)(2,1)}, bf16[9,32,128]{2,1,0:T(8,128)(2,1)S(1)}, u32[]{:S(2)}, u32[]{:S(2)}) %collective-permute-start.8) | collective-permute-done | bytes 73760 | tf_op jit(solution)/shard_map/ppermute | solution.py:27
  6.1 1.3 %collective-permute-done.9 = bf16[9,32,128]{2,1,0:T(8,128)(2,1)S(1)} collective-permute-done((bf16[9,32,128]{2,1,0:T(8,128)(2,1)S(1)}, bf16[9,32,128]{2,1,0:T(8,128)(2,1)S(1)}, u32[]{:S(2)}, u32[]{:S(2)}) %collective-permute-start.9) | collective-permute-done | bytes 73760 | tf_op jit(solution)/shard_map/ppermute | solution.py:27
  7.3 0.9 %pad_maximum_fusion.refs_8_ = bf16[36,32,128]{2,1,0:T(8,128)(2,1)S(1)} fusion(bf16[9,32,128]{2,1,0:T(8,128)(2,1)S(1)} %collective-permute-done.9, bf16[9,32,128]{2,1,0:T(8,128)(2,1)S(1)} %collective-permute-done.8, bf16[9,32,128]{2,1,0:T(8,128)(2,1)S(1)} %collective-permute-done.7, bf16[9,32,128]{2,1,0:T(8,128)(2,1)} %bitcast.6), kind=kLoop, calls=%fused_computation | loop fusion | flops 442368 | bytes 589824 | tf_op jit(solution)/shard_map/concatenate | solution.py:239
  8.3 2.0 %collective-permute-start.10 = (bf16[36,32,128]{2,1,0:T(8,128)(2,1)S(1)}, bf16[36,32,128]{2,1,0:T(8,128)(2,1)S(1)}, u32[]{:S(2)}, u32[]{:S(2)}) collective-permute-start(bf16[36,32,128]{2,1,0:T(8,128)(2,1)S(1)} %pad_maximum_fusion.refs_8_), channel_id=1, source_target_pairs={{0,2},{1,15},{2,4},{3,1},{4,6},{5,3},{6,8},{7,5},{8,10},{9,7},{10,... | collective-permute-start | bytes 884744 | tf_op jit(solution)/shard_map/ppermute | solution.py:27
  10.3 8.6 %collective-permute-done.10.refs_9_ = bf16[36,32,128]{2,1,0:T(8,128)(2,1)S(1)} collective-permute-done((bf16[36,32,128]{2,1,0:T(8,128)(2,1)S(1)}, bf16[36,32,128]{2,1,0:T(8,128)(2,1)S(1)}, u32[]{:S(2)}, u32[]{:S(2)}) %collective-permute-start.10) | collective-permute-done | bytes 294944 | tf_op jit(solution)/shard_map/ppermute | solution.py:27
  18.9 1.3 %collective-permute-start = (bf16[1024,128]{1,0:T(8,128)(2,1)}, bf16[1024,128]{1,0:T(8,128)(2,1)S(1)}, u32[]{:S(2)}, u32[]{:S(2)}) collective-permute-start(bf16[1024,128]{1,0:T(8,128)(2,1)} %bitcast.7), channel_id=1, source_target_pairs={{0,32},{1,33},{2,34},{3,35},{4,36},{5,37},{6,38},{7,39},{8,40},{9,... | collective-permute-start | bytes 786440 | tf_op jit(solution)/shard_map/ppermute | solution.py:27
  20.2 1.5 %collective-permute-start.1 = (bf16[1024,128]{1,0:T(8,128)(2,1)}, bf16[1024,128]{1,0:T(8,128)(2,1)S(1)}, u32[]{:S(2)}, u32[]{:S(2)}) collective-permute-start(bf16[1024,128]{1,0:T(8,128)(2,1)} %bitcast.8), channel_id=1, source_target_pairs={{0,64},{1,193},{2,66},{3,195},{4,68},{5,197},{6,70},{7,199},{8,72}... | collective-permute-start | bytes 786440 | tf_op jit(solution)/shard_map/ppermute | solution.py:27
  21.7 2.1 %collective-permute-start.2 = (bf16[1024,128]{1,0:T(8,128)(2,1)}, bf16[1024,128]{1,0:T(8,128)(2,1)S(1)}, u32[]{:S(2)}, u32[]{:S(2)}) collective-permute-start(bf16[1024,128]{1,0:T(8,128)(2,1)} %bitcast.9), channel_id=1, source_target_pairs={{0,192},{1,65},{2,194},{3,67},{4,196},{5,69},{6,198},{7,71},{8,200... | collective-permute-start | bytes 786440 | tf_op jit(solution)/shard_map/ppermute | solution.py:27
  23.8 3.1 %collective-permute-done.11.refs_10_ = bf16[36,32,128]{2,1,0:T(8,128)(2,1)S(1)} collective-permute-done((bf16[36,32,128]{2,1,0:T(8,128)(2,1)S(1)}, bf16[36,32,128]{2,1,0:T(8,128)(2,1)S(1)}, u32[]{:S(2)}, u32[]{:S(2)}) %collective-permute-start.11) | collective-permute-done | bytes 294944 | tf_op jit(solution)/shard_map/ppermute | solution.py:27
  26.8 0.5 collective-permute-done.refs_1_
  27.3 2.8 %collective-permute-start.5 = (bf16[1024,128]{1,0:T(8,128)(2,1)S(1)}, bf16[1024,128]{1,0:T(8,128)(2,1)S(1)}, u32[]{:S(2)}, u32[]{:S(2)}) collective-permute-start(bf16[1024,128]{1,0:T(8,128)(2,1)S(1)} %collective-permute-done.refs_1_), channel_id=1, source_target_pairs={{0,192},{1,65},{2,194},{3,67},{4,196},{5,69},{6,198},{7,71},{8,200... | collective-permute-start | bytes 786440 | tf_op jit(solution)/shard_map/ppermute | solution.py:27
  30.1 1.3 %collective-permute-start.3 = (bf16[1024,128]{1,0:T(8,128)(2,1)S(1)}, bf16[1024,128]{1,0:T(8,128)(2,1)S(1)}, u32[]{:S(2)}, u32[]{:S(2)}) collective-permute-start(bf16[1024,128]{1,0:T(8,128)(2,1)S(1)} %collective-permute-done.1.refs_2_), channel_id=1, source_target_pairs={{0,32},{1,33},{2,34},{3,35},{4,36},{5,37},{6,38},{7,39},{8,40},{9,... | collective-permute-start | bytes 786440 | tf_op jit(solution)/shard_map/ppermute | solution.py:27
  31.8 2.7 %collective-permute-start.13 = (bf16[36,32,128]{2,1,0:T(8,128)(2,1)S(1)}, bf16[36,32,128]{2,1,0:T(8,128)(2,1)S(1)}, u32[]{:S(2)}, u32[]{:S(2)}) collective-permute-start(bf16[36,32,128]{2,1,0:T(8,128)(2,1)S(1)} %collective-permute-done.10.refs_9_), channel_id=1, source_target_pairs={{0,1},{1,0},{2,3},{3,2},{4,5},{5,4},{6,7},{7,6},{8,9},{9,8},{10,11... | collective-permute-start | bytes 884744 | tf_op jit(solution)/shard_map/ppermute | solution.py:27
  34.4 0.5 collective-permute-done.5.refs_6_
  34.9 0.5 collective-permute-start.15
  35.4 3.6 %collective-permute-done.3.refs_4_ = bf16[1024,128]{1,0:T(8,128)(2,1)S(1)} collective-permute-done((bf16[1024,128]{1,0:T(8,128)(2,1)S(1)}, bf16[1024,128]{1,0:T(8,128)(2,1)S(1)}, u32[]{:S(2)}, u32[]{:S(2)}) %collective-permute-start.3) | collective-permute-done | bytes 262176 | tf_op jit(solution)/shard_map/ppermute | solution.py:27
  39.1 6.3 %collective-permute-done.6.refs_7_ = bf16[1024,128]{1,0:T(8,128)(2,1)S(1)} collective-permute-done((bf16[1024,128]{1,0:T(8,128)(2,1)S(1)}, bf16[1024,128]{1,0:T(8,128)(2,1)S(1)}, u32[]{:S(2)}, u32[]{:S(2)}) %collective-permute-start.6) | collective-permute-done | bytes 262176 | tf_op jit(solution)/shard_map/ppermute | solution.py:27
  45.4 4.5 %early.1 = (bf16[1024,1024]{1,0:T(8,128)(2,1)S(1)}, bf16[9,1024,128]{2,1,0:T(8,128)(2,1)S(1)}, f32[3,1536,128]{2,1,0:T(8,128)S(1)}, f32[1,128]{1,0:T(1,128)S(1)}...) custom-call(bf16[1024,128]{1,0:T(8,128)(2,1)} %bitcast.10, bf16[1024,128]{1,0:T(8,128)(2,1)S(1)} %collective-permute-done.refs_1_, ...), custom_call_target="tpu_custom_call" | custom-call | flops 1811939328 | bytes 6291456 | tf_op jit(solution)/shard_map/early/pallas_call | solution.py:262
  50.0 1.5 %late.1 = (bf16[4,256,128]{2,1,0:T(8,128)(2,1)S(1)}, bf16[4,256,128]{2,1,0:T(8,128)(2,1)S(1)}, bf16[2,256,128]{2,1,0:T(8,128)(2,1)S(1)}, f32[4,256,128]{2,1,0:T(8,128)S(1)}) custom-call(bf16[1024,1024]{1,0:T(8,128)(2,1)S(1)} %get-tuple-element.15.xs, bf16[9,1024,128]{2,1,0:T(8,128)(2,1)S(1)} %get-tuple-element.16.ws_early, ...), custom_call_target="tpu_custom_call" | custom-call | flops 603979776 | bytes 4194304 | tf_op jit(solution)/shard_map/late/pallas_call | solution.py:286
  51.8 2.7 %collective-permute-start.18 = (bf16[4,256,128]{2,1,0:T(8,128)(2,1)S(1)}, bf16[4,256,128]{2,1,0:T(8,128)(2,1)S(1)}, u32[]{:S(2)}, u32[]{:S(2)}) collective-permute-start(bf16[4,256,128]{2,1,0:T(8,128)(2,1)S(1)} %get-tuple-element.24), channel_id=1, source_target_pairs={{1,2},{3,4},{5,6},{7,8},{9,10},{11,12},{13,14},{15,16},{17,18},{19... | collective-permute-start | bytes 786440 | tf_op jit(solution)/shard_map/ppermute | solution.py:309
  54.5 1.2 %depth.2.part = f32[4,256,128]{2,1,0:T(8,128)S(1)} custom-call(f32[4,256,128]{2,1,0:T(8,128)S(1)} %get-tuple-element.19.own, bf16[2,256,128]{2,1,0:T(8,128)(2,1)S(1)} %get-tuple-element.20.mid, bf16[4,256,128]{2,1,0:T(8,128)(2,1)S(1)} %collective-permute-done.17.inner, f32[1,128]{1,0:T(1,128)S(1)} %get-tuple-element.18.bias, ...), custom_call_target="tpu_custom_call" | custom-call | flops 48168960 | bytes 2097152 | tf_op jit(solution)/shard_map/depth/pallas_call | solution.py:317
  55.8 7.4 %collective-permute-done.18.outer = bf16[4,256,128]{2,1,0:T(8,128)(2,1)S(1)} collective-permute-done((bf16[4,256,128]{2,1,0:T(8,128)(2,1)S(1)}, bf16[4,256,128]{2,1,0:T(8,128)(2,1)S(1)}, u32[]{:S(2)}, u32[]{:S(2)}) %collective-permute-start.18) | collective-permute-done | bytes 262176 | tf_op jit(solution)/shard_map/ppermute | solution.py:309
  63.1 1.6 %depth.3 = bf16[4,256,128]{2,1,0:T(8,128)(2,1)} custom-call(f32[4,256,128]{2,1,0:T(8,128)S(1)} %depth.2.part, f32[4,256,128]{2,1,0:T(8,128)S(1)} %get-tuple-element.19.own, bf16[4,256,128]{2,1,0:T(8,128)(2,1)S(1)} %collective-permute-done.18.outer, f32[1,128]{1,0:T(1,128)S(1)} %get-tuple-element.18.bias, f32[7,7,128]{2,1,0:T(8,128)S(1)} %get-tuple-element.23.weight), custom_call_target="tpu_custom_call" | custom-call | flops 32112640 | bytes 2097152 | tf_op jit(solution)/shard_map/depth/pallas_call | solution.py:317
  (19 shorter events, 0.8 us)
Async XLA Ops:
  0.0 6.1 %collective-permute-start.8 = (bf16[9,32,128]{2,1,0:T(8,128)(2,1)}, bf16[9,32,128]{2,1,0:T(8,128)(2,1)S(1)}, u32[]{:S(2)}, u32[]{:S(2)}) collective-permute-start(bf16[9,32,128]{2,1,0:T(8,128)(2,1)} %bitcast.4), channel_id=1, source_target_pairs={{0,16},{1,17},{2,18},{3,19},{4,20},{5,21},{6,22},{7,23},{8,24},{9,... | collective-permute-start | bytes 221192 | tf_op jit(solution)/shard_map/ppermute | solution.py:27
  2.0 4.0 %collective-permute-start.7 = (bf16[9,32,128]{2,1,0:T(8,128)(2,1)}, bf16[9,32,128]{2,1,0:T(8,128)(2,1)S(1)}, u32[]{:S(2)}, u32[]{:S(2)}) collective-permute-start(bf16[9,32,128]{2,1,0:T(8,128)(2,1)} %bitcast.5), channel_id=1, source_target_pairs={{0,1},{1,0},{2,3},{3,2},{4,5},{5,4},{6,7},{7,6},{8,9},{9,8},{10,11... | collective-permute-start | bytes 221192 | tf_op jit(solution)/shard_map/ppermute | solution.py:27
  6.1 1.3 %collective-permute-start.9 = (bf16[9,32,128]{2,1,0:T(8,128)(2,1)S(1)}, bf16[9,32,128]{2,1,0:T(8,128)(2,1)S(1)}, u32[]{:S(2)}, u32[]{:S(2)}) collective-permute-start(bf16[9,32,128]{2,1,0:T(8,128)(2,1)S(1)} %collective-permute-done.8), channel_id=1, source_target_pairs={{0,1},{1,0},{2,3},{3,2},{4,5},{5,4},{6,7},{7,6},{8,9},{9,8},{10,11... | collective-permute-start | bytes 221192 | tf_op jit(solution)/shard_map/ppermute | solution.py:27
  8.3 10.6 %collective-permute-start.10 = (bf16[36,32,128]{2,1,0:T(8,128)(2,1)S(1)}, bf16[36,32,128]{2,1,0:T(8,128)(2,1)S(1)}, u32[]{:S(2)}, u32[]{:S(2)}) collective-permute-start(bf16[36,32,128]{2,1,0:T(8,128)(2,1)S(1)} %pad_maximum_fusion.refs_8_), channel_id=1, source_target_pairs={{0,2},{1,15},{2,4},{3,1},{4,6},{5,3},{6,8},{7,5},{8,10},{9,7},{10,... | collective-permute-start | bytes 884744 | tf_op jit(solution)/shard_map/ppermute | solution.py:27
  18.9 7.9 %collective-permute-start.11 = (bf16[36,32,128]{2,1,0:T(8,128)(2,1)S(1)}, bf16[36,32,128]{2,1,0:T(8,128)(2,1)S(1)}, u32[]{:S(2)}, u32[]{:S(2)}) collective-permute-start(bf16[36,32,128]{2,1,0:T(8,128)(2,1)S(1)} %collective-permute-done.10.refs_9_), channel_id=1, source_target_pairs={{0,2},{1,15},{2,4},{3,1},{4,6},{5,3},{6,8},{7,5},{8,10},{9,7},{10,... | collective-permute-start | bytes 884744 | tf_op jit(solution)/shard_map/ppermute | solution.py:27
  18.9 8.4 %collective-permute-start = (bf16[1024,128]{1,0:T(8,128)(2,1)}, bf16[1024,128]{1,0:T(8,128)(2,1)S(1)}, u32[]{:S(2)}, u32[]{:S(2)}) collective-permute-start(bf16[1024,128]{1,0:T(8,128)(2,1)} %bitcast.7), channel_id=1, source_target_pairs={{0,32},{1,33},{2,34},{3,35},{4,36},{5,37},{6,38},{7,39},{8,40},{9,... | collective-permute-start | bytes 786440 | tf_op jit(solution)/shard_map/ppermute | solution.py:27
  20.2 9.9 %collective-permute-start.1 = (bf16[1024,128]{1,0:T(8,128)(2,1)}, bf16[1024,128]{1,0:T(8,128)(2,1)S(1)}, u32[]{:S(2)}, u32[]{:S(2)}) collective-permute-start(bf16[1024,128]{1,0:T(8,128)(2,1)} %bitcast.8), channel_id=1, source_target_pairs={{0,64},{1,193},{2,66},{3,195},{4,68},{5,197},{6,70},{7,199},{8,72}... | collective-permute-start | bytes 786440 | tf_op jit(solution)/shard_map/ppermute | solution.py:27
  21.7 9.8 %collective-permute-start.2 = (bf16[1024,128]{1,0:T(8,128)(2,1)}, bf16[1024,128]{1,0:T(8,128)(2,1)S(1)}, u32[]{:S(2)}, u32[]{:S(2)}) collective-permute-start(bf16[1024,128]{1,0:T(8,128)(2,1)} %bitcast.9), channel_id=1, source_target_pairs={{0,192},{1,65},{2,194},{3,67},{4,196},{5,69},{6,198},{7,71},{8,200... | collective-permute-start | bytes 786440 | tf_op jit(solution)/shard_map/ppermute | solution.py:27
  26.8 8.1 %collective-permute-start.12 = (bf16[36,32,128]{2,1,0:T(8,128)(2,1)S(1)}, bf16[36,32,128]{2,1,0:T(8,128)(2,1)S(1)}, u32[]{:S(2)}, u32[]{:S(2)}) collective-permute-start(bf16[36,32,128]{2,1,0:T(8,128)(2,1)S(1)} %collective-permute-done.11.refs_10_), channel_id=1, source_target_pairs={{0,2},{1,15},{2,4},{3,1},{4,6},{5,3},{6,8},{7,5},{8,10},{9,7},{10,... | collective-permute-start | bytes 884744 | tf_op jit(solution)/shard_map/ppermute | solution.py:27
  27.3 7.6 %collective-permute-start.5 = (bf16[1024,128]{1,0:T(8,128)(2,1)S(1)}, bf16[1024,128]{1,0:T(8,128)(2,1)S(1)}, u32[]{:S(2)}, u32[]{:S(2)}) collective-permute-start(bf16[1024,128]{1,0:T(8,128)(2,1)S(1)} %collective-permute-done.refs_1_), channel_id=1, source_target_pairs={{0,192},{1,65},{2,194},{3,67},{4,196},{5,69},{6,198},{7,71},{8,200... | collective-permute-start | bytes 786440 | tf_op jit(solution)/shard_map/ppermute | solution.py:27
  30.1 9.0 %collective-permute-start.3 = (bf16[1024,128]{1,0:T(8,128)(2,1)S(1)}, bf16[1024,128]{1,0:T(8,128)(2,1)S(1)}, u32[]{:S(2)}, u32[]{:S(2)}) collective-permute-start(bf16[1024,128]{1,0:T(8,128)(2,1)S(1)} %collective-permute-done.1.refs_2_), channel_id=1, source_target_pairs={{0,32},{1,33},{2,34},{3,35},{4,36},{5,37},{6,38},{7,39},{8,40},{9,... | collective-permute-start | bytes 786440 | tf_op jit(solution)/shard_map/ppermute | solution.py:27
  31.5 7.5 %collective-permute-start.4 = (bf16[1024,128]{1,0:T(8,128)(2,1)S(1)}, bf16[1024,128]{1,0:T(8,128)(2,1)S(1)}, u32[]{:S(2)}, u32[]{:S(2)}) collective-permute-start(bf16[1024,128]{1,0:T(8,128)(2,1)S(1)} %collective-permute-done.2.refs_3_), channel_id=1, source_target_pairs={{0,64},{1,193},{2,66},{3,195},{4,68},{5,197},{6,70},{7,199},{8,72}... | collective-permute-start | bytes 786440 | tf_op jit(solution)/shard_map/ppermute | solution.py:27
  31.8 7.3 %collective-permute-start.13 = (bf16[36,32,128]{2,1,0:T(8,128)(2,1)S(1)}, bf16[36,32,128]{2,1,0:T(8,128)(2,1)S(1)}, u32[]{:S(2)}, u32[]{:S(2)}) collective-permute-start(bf16[36,32,128]{2,1,0:T(8,128)(2,1)S(1)} %collective-permute-done.10.refs_9_), channel_id=1, source_target_pairs={{0,1},{1,0},{2,3},{3,2},{4,5},{5,4},{6,7},{7,6},{8,9},{9,8},{10,11... | collective-permute-start | bytes 884744 | tf_op jit(solution)/shard_map/ppermute | solution.py:27
  34.9 10.5 %collective-permute-start.14 = (bf16[36,32,128]{2,1,0:T(8,128)(2,1)S(1)}, bf16[36,32,128]{2,1,0:T(8,128)(2,1)S(1)}, u32[]{:S(2)}, u32[]{:S(2)}) collective-permute-start(bf16[36,32,128]{2,1,0:T(8,128)(2,1)S(1)} %collective-permute-done.11.refs_10_), channel_id=1, source_target_pairs={{0,1},{1,0},{2,3},{3,2},{4,5},{5,4},{6,7},{7,6},{8,9},{9,8},{10,11... | collective-permute-start | bytes 884744 | tf_op jit(solution)/shard_map/ppermute | solution.py:27
  34.9 10.5 %collective-permute-start.15 = (bf16[36,32,128]{2,1,0:T(8,128)(2,1)S(1)}, bf16[36,32,128]{2,1,0:T(8,128)(2,1)S(1)}, u32[]{:S(2)}, u32[]{:S(2)}) collective-permute-start(bf16[36,32,128]{2,1,0:T(8,128)(2,1)S(1)} %collective-permute-done.12.refs_11_), channel_id=1, source_target_pairs={{0,1},{1,0},{2,3},{3,2},{4,5},{5,4},{6,7},{7,6},{8,9},{9,8},{10,11... | collective-permute-start | bytes 884744 | tf_op jit(solution)/shard_map/ppermute | solution.py:27
  39.0 6.4 %collective-permute-start.6 = (bf16[1024,128]{1,0:T(8,128)(2,1)S(1)}, bf16[1024,128]{1,0:T(8,128)(2,1)S(1)}, u32[]{:S(2)}, u32[]{:S(2)}) collective-permute-start(bf16[1024,128]{1,0:T(8,128)(2,1)S(1)} %collective-permute-done.5.refs_6_), channel_id=1, source_target_pairs={{0,64},{1,193},{2,66},{3,195},{4,68},{5,197},{6,70},{7,199},{8,72}... | collective-permute-start | bytes 786440 | tf_op jit(solution)/shard_map/ppermute | solution.py:27
  39.0 10.9 %collective-permute-start.16 = (bf16[36,32,128]{2,1,0:T(8,128)(2,1)S(1)}, bf16[36,32,128]{2,1,0:T(8,128)(2,1)S(1)}, u32[]{:S(2)}, u32[]{:S(2)}) collective-permute-start(bf16[36,32,128]{2,1,0:T(8,128)(2,1)S(1)} %collective-permute-done.12.refs_11_), channel_id=1, source_target_pairs={{0,2},{1,15},{2,4},{3,1},{4,6},{5,3},{6,8},{7,5},{8,10},{9,7},{10,... | collective-permute-start | bytes 884744 | tf_op jit(solution)/shard_map/ppermute | solution.py:27
  51.5 3.0 %collective-permute-start.17 = (bf16[4,256,128]{2,1,0:T(8,128)(2,1)S(1)}, bf16[4,256,128]{2,1,0:T(8,128)(2,1)S(1)}, u32[]{:S(2)}, u32[]{:S(2)}) collective-permute-start(bf16[4,256,128]{2,1,0:T(8,128)(2,1)S(1)} %get-tuple-element.21), channel_id=1, source_target_pairs={{0,1},{1,0},{2,3},{3,2},{4,5},{5,4},{6,7},{7,6},{8,9},{9,8},{10,11... | collective-permute-start | bytes 786440 | tf_op jit(solution)/shard_map/ppermute | solution.py:310
  51.8 11.3 %collective-permute-start.18 = (bf16[4,256,128]{2,1,0:T(8,128)(2,1)S(1)}, bf16[4,256,128]{2,1,0:T(8,128)(2,1)S(1)}, u32[]{:S(2)}, u32[]{:S(2)}) collective-permute-start(bf16[4,256,128]{2,1,0:T(8,128)(2,1)S(1)} %get-tuple-element.24), channel_id=1, source_target_pairs={{1,2},{3,4},{5,6},{7,8},{9,10},{11,12},{13,14},{15,16},{17,18},{19... | collective-permute-start | bytes 786440 | tf_op jit(solution)/shard_map/ppermute | solution.py:309

commit v3 on v2

--- a/solution.py
+++ b/solution.py
@@ -52,23 +52,27 @@
 
 
 TAPS = (((0, 0), (0, 1)), ((0, 2), (2, 0)), ((2, 1), (2, 2)), ((1, 0), (1, 1)), ((1, 2),))
-EARLY = 6 * CH
-
-
-def add_taps(pixels, filters, acc):
+
+
+def add_taps(pixels, filters, acc, base=None):
+    def put(b, begin, value, add):
+        rows = slice(begin, begin + value.shape[0])
+        before = acc if add else base
+        acc[b, rows, :] = value if before is None else before[b, rows, :] + value
+
     for taps in TAPS:
-        columns = [filters(3 * a + b) for a, b in taps]
+        columns = [filters[3 * a + b] for a, b in taps]
         rhs = jnp.concatenate(columns, axis=1) if len(taps) > 1 else columns[0]
         result = jnp.dot(pixels(), rhs, preferred_element_type=jnp.float32)
         for at, (a, b) in enumerate(taps):
             part = result[:, at * CH : (at + 1) * CH]
             if a == 0:
-                acc[b, 512:1536, :] = part
+                put(b, 512, part, False)
             elif a == 2:
-                acc[b, 0:512, :] = part[0:512]
-                acc[b, 512:1024, :] += part[512:1024]
+                put(b, 0, part[0:512], False)
+                put(b, 512, part[512:1024], True)
             else:
-                acc[b, 256:1280, :] += part
+                put(b, 256, part, True)
 
 
 class Copies:
@@ -85,65 +89,97 @@
             copy.wait()
 
 
-def block_at(pair, half, z):
-    return 2 * ((pair - z // 2 + 5) % 4) + half
-
-
-def filter_rows(z, at_z, half, at_core, first):
-    row = block_at(at_z // 2, half, z) * CH + (at_z % 2) * 64 + at_core * 32 - first
-    return pl.ds(pl.multiple_of(row, 32), 32)
-
-
-def early_kernel(*refs):
-    blocks, own_w, other_w, small = refs[:8], refs[8:12], refs[12:15], refs[15:18]
-    (xs, ws, acc, *params), sems = refs[18:24], refs[24]
-    chan, tile = lax.axis_index("chan"), lax.axis_index("tile")
+def pair_at(pair, z):
+    ahead = ((pair - z // 2) * (1 - 2 * (z % 2)) + 8) % 4
+    return (ahead % 3 + 1) * ((ahead + 3) // 4)
+
+
+class Filters:
+    def __init__(self, copies, target):
+        self.copies, self.target = copies, target
+        tile = lax.axis_index("tile")
+        self.y_hi, self.z, self.core = tile // 16, (tile // 2) % 8, tile % 2
+        self.partner_back = (self.core + self.z) % 2 == 1
+
+    def each_piece(self, array, odd, first, core):
+        for piece in range(4):
+            half, at_core = (self.y_hi + piece // 2) % 2, (core + piece) % 2
+            source, at = (array[piece // 2], piece % 2) if isinstance(array, tuple) else (array, piece)
+            row = first + half * CH + odd * 64 + at_core * 32
+            rows = pl.ds(pl.multiple_of(row, 32), 32)
+            yield source.at[pl.ds(9 * at, 9)], self.target.at[:, rows, :]
+
+    def place(self, array, odd, first, core):
+        for src, dst in self.each_piece(array, odd, first, core):
+            self.copies.start(src, dst)
+
+    def place_one(self, mine, others, towards_partner, odd, first):
+        use_mine = self.partner_back == towards_partner
+        sems = [self.copies.sems.at[len(self.copies.started) + piece] for piece in range(4)]
+
+        def start(array, core):
+            for (src, dst), sem in zip(self.each_piece(array, odd, first, core), sems):
+                pltpu.make_async_copy(src, dst, sem).start()
+
+        pl.when(use_mine)(lambda: start(mine, self.core))
+        pl.when(jnp.logical_not(use_mine))(lambda: start(others, 1 - self.core))
+        for sem in sems:
+            same_size = pltpu.make_async_copy(mine[0].at[pl.ds(0, 9)], self.target.at[:, pl.ds(0, 32), :], sem)
+            self.copies.started.append(same_size)
+
+
+def first_kernel(*refs):
+    blocks, w0, w1, w2, (o1, o2), small = refs[:8], refs[8:10], refs[10:12], refs[12:14], refs[14:16], refs[16:19]
+    (xs, acc, *params), (ws, sems) = refs[19:24], refs[24:]
+    chan = lax.axis_index("chan")
     x, y = chan // 2, chan % 2
-    y_hi, z, core = tile // 16, (tile // 2) % 8, tile % 2
+    copies = Copies(sems)
+    filters = Filters(copies, ws)
+    z, core = filters.z, filters.core
     turn = 1 - 2 * ((x + core) % 2)
     xl, xm, xf = (x + turn + 4) % 4, (x - turn + 4) % 4, (x + 2) % 4
-    copies = Copies(sems)
     places = ((x, y), (x, 1 - y), (xl, y), (xm, y), (xl, 1 - y), (xf, y), (xm, 1 - y), (xf, 1 - y))
     for block, (at_x, at_y) in zip(blocks, places):
         index = 2 * at_x + at_y
-        at = block_at(index % 4, index // 4, z)
+        at = 2 * pair_at(index % 4, z) + index // 4
         copies.start(block, xs.at[:, pl.ds(pl.multiple_of(at * CH, CH), CH)])
-
-    def place(array, at_z, at_core):
-        for piece in range(array.shape[0] // 9):
-            rows = filter_rows(z, at_z, (y_hi + piece // 2) % 2, (at_core + piece) % 2, 0)
-            copies.start(array.at[pl.ds(9 * piece, 9)], ws.at[:, rows, :])
-
-    back = 1 - 2 * core
-    for steps, array in enumerate(own_w):
-        place(array, (z - steps * back + 8) % 8, core)
-    for steps, array in enumerate(other_w):
-        place(array, (z + (steps + 1) * back + 8) % 8, 1 - core)
+    even, odd = z % 2, 1 - z % 2
+    filters.place(w0, even, 0, core)
+    filters.place_one(w1, o1, True, odd, 0)
+    filters.place_one(w1, o1, False, odd, 2 * CH)
+    filters.place_one(w2, o2, False, even, 2 * CH)
     for source, target in zip(small, params):
         copies.start(source, target)
     copies.wait()
-    add_taps(lambda: xs[:, 0:EARLY], lambda tap: ws[tap, 0:EARLY, :], acc)
-
-
-def late_kernel(xs, ws_early, acc_early, last, bias, outer, inner, mid, own, ws, acc, sems):
-    tile = lax.axis_index("tile")
-    y_hi, z, core = tile // 16, (tile // 2) % 8, tile % 2
+    add_taps(lambda: xs[:, 0 : 4 * CH], ws, acc)
+
+
+def second_kernel(xs, base, a2, g2, a3, g3, o2, o3, acc, ws, sems):
+    w2, w3 = (a2, g2), (a3, g3)
     copies = Copies(sems)
-    for half in range(2):
-        rows = pl.ds(pl.multiple_of(half * CH + (1 - z % 2) * 64, 64), 64)
-        early = pl.ds(pl.multiple_of(EARLY + half * CH + (1 - z % 2) * 64, 64), 64)
-        copies.start(ws_early.at[:, early, :], ws.at[:, rows, :])
-    for piece in range(4):
-        rows = filter_rows(z, (z + 4) % 8, (y_hi + piece // 2) % 2, (core + piece) % 2, EARLY)
-        copies.start(last.at[pl.ds(9 * piece, 9)], ws.at[:, rows, :])
+    filters = Filters(copies, ws)
+    even, odd = filters.z % 2, 1 - filters.z % 2
+    filters.place_one(w2, o2, True, even, 0)
+    filters.place_one(w3, o3, True, odd, 0)
     copies.wait()
-    add_taps(lambda: xs[:, EARLY : 8 * CH], lambda tap: ws[tap], acc)
+    add_taps(lambda: xs[:, 4 * CH : 6 * CH], ws, acc, base)
+
+
+def third_kernel(xs, base, a3, g3, o3, a4, g4, bias, outer, inner, mid, own, ws, acc, sems):
+    w3, w4 = (a3, g3), (a4, g4)
+    copies = Copies(sems)
+    filters = Filters(copies, ws)
+    core, even, odd = filters.core, filters.z % 2, 1 - filters.z % 2
+    filters.place_one(w3, o3, False, odd, 0)
+    filters.place(w4, even, 0, core)
+    copies.wait()
+    add_taps(lambda: xs[:, 6 * CH : 8 * CH], ws, acc, base)
 
     column = lax.broadcasted_iota(jnp.int32, (COLS, CH), 0)
 
     def row_sum(row):
         rows = pl.ds(pl.multiple_of((row + 1 + core * (3 - 2 * row)) * COLS, COLS), COLS)
-        total = [acc[b, rows, :] + acc_early[b, rows, :] for b in range(3)]
+        total = [acc[b, rows, :] for b in range(3)]
         left = jnp.where(column == 0, 0.0, pltpu.roll(total[0], 1, 0))
         right = jnp.where(column == COLS - 1, 0.0, pltpu.roll(total[2], COLS - 1, 0))
         return total[1] + left + right
@@ -236,17 +272,23 @@
     h0 = move(w0, to_hi)
     w0_other = move(w0, to_core)
     p_y, p_l, p_m = move(p0, to_y), move(p0, to_l), move(p0, to_m)
-    w0 = jnp.concatenate([w0, w0_other, h0, move(h0, to_core)])
-    w1 = move(w0, to_next)
-    w2 = move(w1, to_next)
-    o1 = move(w1, to_core)
+    a0 = jnp.concatenate([w0, w0_other])
+    a1 = move(a0, to_next)
+    g0 = jnp.concatenate([h0, move(h0, to_core)])
+    g1 = move(g0, to_next)
+    a2, g2 = move(a1, to_next), move(g1, to_next)
+    both = jnp.concatenate([a1, g1])
+    o1 = move(both, to_core)
     p_ly, p_ml, p_ym = move(p_l, to_y), move(p_m, to_l), move(p_y, to_m)
-    w3 = move(w2, to_next)
-    o2 = move(w2, to_core)
+    a3, g3 = move(a2, to_next), move(g2, to_next)
+    both = jnp.concatenate([a2, g2])
+    o2 = move(both, to_core)
     p_far = move(p_ym, to_l)
-    w4 = move(w3, to_next)
-    o3 = move(w3, to_core)
-    return (in_hbm(p0), p_y, p_l, p_m, p_ly, p_ml, p_ym, p_far, w0, w1, w2, w3, o1, o2, o3), w4
+    a4, g4 = move(a3, to_next), move(g3, to_next)
+    both = jnp.concatenate([a3, g3])
+    o3 = move(both, to_core)
+    blocks = (in_hbm(p0), p_y, p_l, p_m, p_ly, p_ml, p_ym, p_far)
+    return blocks, ((a0, g0), (a1, g1), (a2, g2), (a3, g3), (a4, g4)), (o1, o2, o3)
 
 
 def in_hbm(array):
@@ -258,52 +300,64 @@
     hbm = pl.BlockSpec(memory_space=pltpu.HBM)
     f32, bf16 = jnp.float32, jnp.bfloat16
     message = jax.ShapeDtypeStruct((4, COLS, CH), bf16)
-    gathered, last = gather_all(pixels, conv_weight)
-    xs, ws, acc, *params = pl.pallas_call(
-        early_kernel,
+    sums = jax.ShapeDtypeStruct((3, 6 * COLS, CH), f32)
+
+    def settings(blocks):
+        return dict(
+            compiler_params=pltpu.CompilerParams(vmem_limit_bytes=30 << 20),
+            cost_estimate=pl.CostEstimate(
+                flops=2 * PIX * 9 * blocks * CH * CH, bytes_accessed=4 << 20, transcendentals=0
+            ),
+        )
+
+    blocks, (w0, w1, w2, w3, w4), (o1, o2, o3) = gather_all(pixels, conv_weight)
+    xs, acc, *params = pl.pallas_call(
+        first_kernel,
         out_shape=(
             jax.ShapeDtypeStruct((PIX, 8 * CH), bf16),
-            jax.ShapeDtypeStruct((9, 8 * CH, CH), bf16),
-            jax.ShapeDtypeStruct((3, 6 * COLS, CH), f32),
+            sums,
             jax.ShapeDtypeStruct((1, CH), f32),
             jax.ShapeDtypeStruct((1, CH), f32),
             jax.ShapeDtypeStruct((7, 7, CH), f32),
         ),
-        in_specs=[hbm] + [anywhere] * 14 + [hbm] * 3,
-        out_specs=(vmem,) * 6,
-        scratch_shapes=[pltpu.SemaphoreType.DMA((39,))],
-        compiler_params=pltpu.CompilerParams(vmem_limit_bytes=30 << 20),
-        cost_estimate=pl.CostEstimate(
-            flops=2 * PIX * 9 * EARLY * CH, bytes_accessed=6 << 20, transcendentals=0
-        ),
-        name="early",
+        in_specs=[hbm] + [anywhere] * 15 + [hbm] * 3,
+        out_specs=(vmem,) * 5,
+        scratch_shapes=[pltpu.VMEM((9, 4 * CH, CH), bf16), pltpu.SemaphoreType.DMA((27,))],
+        name="first",
+        **settings(4),
     )(
-        *gathered,
+        *blocks, *w0, *w1, *w2, o1, o2,
         in_hbm(conv_bias.reshape(1, CH)),
         in_hbm(depth_bias.reshape(1, CH)),
         in_hbm(depth_weight),
     )
+    acc = pl.pallas_call(
+        second_kernel,
+        out_shape=sums,
+        in_specs=[vmem] * 2 + [anywhere] * 6,
+        out_specs=vmem,
+        scratch_shapes=[pltpu.VMEM((9, 2 * CH, CH), bf16), pltpu.SemaphoreType.DMA((8,))],
+        name="second",
+        **settings(2),
+    )(xs, acc, *w2, *w3, o2, o3)
     outer, inner, mid, own = pl.pallas_call(
-        late_kernel,
+        third_kernel,
         out_shape=(
             message,
             message,
             jax.ShapeDtypeStruct((2, COLS, CH), bf16),
             jax.ShapeDtypeStruct((4, COLS, CH), f32),
         ),
-        in_specs=[vmem, anywhere, vmem, anywhere, vmem],
+        in_specs=[vmem] * 2 + [anywhere] * 5 + [vmem],
         out_specs=(vmem,) * 4,
         scratch_shapes=[
             pltpu.VMEM((9, 2 * CH, CH), bf16),
             pltpu.VMEM((3, 6 * COLS, CH), f32),
-            pltpu.SemaphoreType.DMA((6,)),
+            pltpu.SemaphoreType.DMA((8,)),
         ],
-        compiler_params=pltpu.CompilerParams(vmem_limit_bytes=30 << 20),
-        cost_estimate=pl.CostEstimate(
-            flops=2 * PIX * 9 * 2 * CH * CH, bytes_accessed=4 << 20, transcendentals=0
-        ),
-        name="late",
-    )(xs, ws, acc, last, params[0])
+        name="third",
+        **settings(2),
+    )(xs, acc, *w3, o3, *w4, params[0])
     bias, depth_bias, weight = params
     across = [(i, i + 1) for i in range(1, 31, 2)]
     from_outer = lax.ppermute(outer, "tile", across + [(j, i) for i, j in across])

time: 64.9 us -> 57.9 us (0.89)
  the two profiles are of different devices: /device:TPU:16 before, /device:TPU:24 now
where the time goes in v3:
time: 57.9 us; the launch traced here: 57.7 us
  starting transfers between devices  28.7 us (50%)
  waiting for transfers between devices  19.1 us (33%)
  Pallas kernels  8.82 us (15%)
  other arithmetic  0.98 us (2%)
    ppermute x21, starting transfers between devices, move(): return lax.ppermute(block, ('chan', 'tile'), pairs)  24 us
    ppermute x21, waiting for transfers between devices, move(): return lax.ppermute(block, ('chan', 'tile'), pairs)  12.7 us
    ppermute x1, waiting for transfers between devices, body(): lax.ppermute(outer, 'tile', across + [(j, i) for i, j in across])  6.36 us
    ppermute x1, starting transfers between devices, body(): lax.ppermute(outer, 'tile', across + [(j, i) for i, j in across])  3.71 us
    pallas_call x1, Pallas kernels, body(): pl.pallas_call(first_kernel, out_shape=(jax.ShapeDtypeStruct((PIX, 8 * CH...  3.6 us
    pallas_call x2, Pallas kernels, depth(): pl.pallas_call(kernel, out_shape=jax.ShapeDtypeStruct((ROWS, COLS, CH), d...  2.76 us
    pallas_call x1, Pallas kernels, body(): pl.pallas_call(third_kernel, out_shape=(message, message, jax.ShapeDtypeS...  1.36 us
  transfers between devices with their start and end apart: 23, of which 9 were waited for; matrix products, arithmetic and copies ran while one was open for 2% of the time, Pallas kernels for 10%

profile of v3, /device:TPU:24, one launch (start us, length us, event | category | flops | bytes accessed | tf_op | source)
XLA Modules:
  0.0 57.7 jit_solution(5257898311949354000)
XLA Ops:
  0.0 1.2 %collective-permute-start.8 = (bf16[9,32,128]{2,1,0:T(8,128)(2,1)}, bf16[9,32,128]{2,1,0:T(8,128)(2,1)S(1)}, u32[]{:S(2)}, u32[]{:S(2)}) collective-permute-start(bf16[9,32,128]{2,1,0:T(8,128)(2,1)} %bitcast.5), channel_id=1, source_target_pairs={{0,16},{1,17},{2,18},{3,19},{4,20},{5,21},{6,22},{7,23},{8,24},{9,... | collective-permute-start | bytes 221192 | tf_op jit(solution)/shard_map/ppermute | solution.py:27
  2.4 2.0 %collective-permute-start.10 = (bf16[18,32,128]{2,1,0:T(8,128)(2,1)S(1)}, bf16[18,32,128]{2,1,0:T(8,128)(2,1)S(1)}, u32[]{:S(2)}, u32[]{:S(2)}) collective-permute-start(bf16[18,32,128]{2,1,0:T(8,128)(2,1)S(1)} %pad_maximum_fusion.3.refs_8_), channel_id=1, source_target_pairs={{0,2},{1,15},{2,4},{3,1},{4,6},{5,3},{6,8},{7,5},{8,10},{9,7},{10,... | collective-permute-start | bytes 442376 | tf_op jit(solution)/shard_map/ppermute | solution.py:27
  4.4 2.0 %collective-permute-done.8 = bf16[9,32,128]{2,1,0:T(8,128)(2,1)S(1)} collective-permute-done((bf16[9,32,128]{2,1,0:T(8,128)(2,1)}, bf16[9,32,128]{2,1,0:T(8,128)(2,1)S(1)}, u32[]{:S(2)}, u32[]{:S(2)}) %collective-permute-start.8) | collective-permute-done | bytes 73760 | tf_op jit(solution)/shard_map/ppermute | solution.py:27
  6.4 1.8 %collective-permute-start.9 = (bf16[9,32,128]{2,1,0:T(8,128)(2,1)S(1)}, bf16[9,32,128]{2,1,0:T(8,128)(2,1)S(1)}, u32[]{:S(2)}, u32[]{:S(2)}) collective-permute-start(bf16[9,32,128]{2,1,0:T(8,128)(2,1)S(1)} %collective-permute-done.8), channel_id=1, source_target_pairs={{0,1},{1,0},{2,3},{3,2},{4,5},{5,4},{6,7},{7,6},{8,9},{9,8},{10,11... | collective-permute-start | bytes 221192 | tf_op jit(solution)/shard_map/ppermute | solution.py:27
  8.2 0.9 %collective-permute-done.9 = bf16[9,32,128]{2,1,0:T(8,128)(2,1)S(1)} collective-permute-done((bf16[9,32,128]{2,1,0:T(8,128)(2,1)S(1)}, bf16[9,32,128]{2,1,0:T(8,128)(2,1)S(1)}, u32[]{:S(2)}, u32[]{:S(2)}) %collective-permute-start.9) | collective-permute-done | bytes 73760 | tf_op jit(solution)/shard_map/ppermute | solution.py:27
  10.4 1.5 %collective-permute-start.1 = (bf16[1024,128]{1,0:T(8,128)(2,1)}, bf16[1024,128]{1,0:T(8,128)(2,1)S(1)}, u32[]{:S(2)}, u32[]{:S(2)}) collective-permute-start(bf16[1024,128]{1,0:T(8,128)(2,1)} %bitcast.8), channel_id=1, source_target_pairs={{0,64},{1,193},{2,66},{3,195},{4,68},{5,197},{6,70},{7,199},{8,72}... | collective-permute-start | bytes 786440 | tf_op jit(solution)/shard_map/ppermute | solution.py:27
  11.9 2.1 %collective-permute-start.2 = (bf16[1024,128]{1,0:T(8,128)(2,1)}, bf16[1024,128]{1,0:T(8,128)(2,1)S(1)}, u32[]{:S(2)}, u32[]{:S(2)}) collective-permute-start(bf16[1024,128]{1,0:T(8,128)(2,1)} %bitcast.9), channel_id=1, source_target_pairs={{0,192},{1,65},{2,194},{3,67},{4,196},{5,69},{6,198},{7,71},{8,200... | collective-permute-start | bytes 786440 | tf_op jit(solution)/shard_map/ppermute | solution.py:27
  14.0 1.9 %collective-permute-start.12 = (bf16[18,32,128]{2,1,0:T(8,128)(2,1)S(1)}, bf16[18,32,128]{2,1,0:T(8,128)(2,1)S(1)}, u32[]{:S(2)}, u32[]{:S(2)}) collective-permute-start(bf16[18,32,128]{2,1,0:T(8,128)(2,1)S(1)} %collective-permute-done.10.refs_10_), channel_id=1, source_target_pairs={{0,2},{1,15},{2,4},{3,1},{4,6},{5,3},{6,8},{7,5},{8,10},{9,7},{10,... | collective-permute-start | bytes 442376 | tf_op jit(solution)/shard_map/ppermute | solution.py:27
  16.7 1.1 %collective-permute-start.13 = (bf16[18,32,128]{2,1,0:T(8,128)(2,1)S(1)}, bf16[18,32,128]{2,1,0:T(8,128)(2,1)S(1)}, u32[]{:S(2)}, u32[]{:S(2)}) collective-permute-start(bf16[18,32,128]{2,1,0:T(8,128)(2,1)S(1)} %collective-permute-done.11.refs_11_), channel_id=1, source_target_pairs={{0,2},{1,15},{2,4},{3,1},{4,6},{5,3},{6,8},{7,5},{8,10},{9,7},{10,... | collective-permute-start | bytes 442376 | tf_op jit(solution)/shard_map/ppermute | solution.py:27
  17.9 1.7 %collective-permute-start.5 = (bf16[1024,128]{1,0:T(8,128)(2,1)S(1)}, bf16[1024,128]{1,0:T(8,128)(2,1)S(1)}, u32[]{:S(2)}, u32[]{:S(2)}) collective-permute-start(bf16[1024,128]{1,0:T(8,128)(2,1)S(1)} %collective-permute-done.refs_1_), channel_id=1, source_target_pairs={{0,192},{1,65},{2,194},{3,67},{4,196},{5,69},{6,198},{7,71},{8,200... | collective-permute-start | bytes 786440 | tf_op jit(solution)/shard_map/ppermute | solution.py:27
  20.3 1.2 %collective-permute-done.2.refs_3_ = bf16[1024,128]{1,0:T(8,128)(2,1)S(1)} collective-permute-done((bf16[1024,128]{1,0:T(8,128)(2,1)}, bf16[1024,128]{1,0:T(8,128)(2,1)S(1)}, u32[]{:S(2)}, u32[]{:S(2)}) %collective-permute-start.2) | collective-permute-done | bytes 262176 | tf_op jit(solution)/shard_map/ppermute | solution.py:27
  21.4 2.8 %collective-permute-start.16 = (bf16[18,32,128]{2,1,0:T(8,128)(2,1)S(1)}, bf16[18,32,128]{2,1,0:T(8,128)(2,1)S(1)}, u32[]{:S(2)}, u32[]{:S(2)}) collective-permute-start(bf16[18,32,128]{2,1,0:T(8,128)(2,1)S(1)} %collective-permute-done.12.refs_12_.a2), channel_id=1, source_target_pairs={{0,2},{1,15},{2,4},{3,1},{4,6},{5,3},{6,8},{7,5},{8,10},{9,7},{10,... | collective-permute-start | bytes 442376 | tf_op jit(solution)/shard_map/ppermute | solution.py:27
  25.1 4.7 %collective-permute-done.16.a3 = bf16[18,32,128]{2,1,0:T(8,128)(2,1)S(1)} collective-permute-done((bf16[18,32,128]{2,1,0:T(8,128)(2,1)S(1)}, bf16[18,32,128]{2,1,0:T(8,128)(2,1)S(1)}, u32[]{:S(2)}, u32[]{:S(2)}) %collective-permute-start.16) | collective-permute-done | bytes 147488 | tf_op jit(solution)/shard_map/ppermute | solution.py:27
  31.4 1.8 %collective-permute-start.6 = (bf16[1024,128]{1,0:T(8,128)(2,1)S(1)}, bf16[1024,128]{1,0:T(8,128)(2,1)S(1)}, u32[]{:S(2)}, u32[]{:S(2)}) collective-permute-start(bf16[1024,128]{1,0:T(8,128)(2,1)S(1)} %collective-permute-done.5.refs_6_), channel_id=1, source_target_pairs={{0,64},{1,193},{2,66},{3,195},{4,68},{5,197},{6,70},{7,199},{8,72}... | collective-permute-start | bytes 786440 | tf_op jit(solution)/shard_map/ppermute | solution.py:27
  33.6 2.1 %collective-permute-start.20 = (bf16[18,32,128]{2,1,0:T(8,128)(2,1)S(1)}, bf16[18,32,128]{2,1,0:T(8,128)(2,1)S(1)}, u32[]{:S(2)}, u32[]{:S(2)}) collective-permute-start(bf16[18,32,128]{2,1,0:T(8,128)(2,1)S(1)} %collective-permute-done.17.g3), channel_id=1, source_target_pairs={{0,2},{1,15},{2,4},{3,1},{4,6},{5,3},{6,8},{7,5},{8,10},{9,7},{10,... | collective-permute-start | bytes 442376 | tf_op jit(solution)/shard_map/ppermute | solution.py:27
  35.7 2.1 %collective-permute-done.6.refs_7_ = bf16[1024,128]{1,0:T(8,128)(2,1)S(1)} collective-permute-done((bf16[1024,128]{1,0:T(8,128)(2,1)S(1)}, bf16[1024,128]{1,0:T(8,128)(2,1)S(1)}, u32[]{:S(2)}, u32[]{:S(2)}) %collective-permute-start.6) | collective-permute-done | bytes 262176 | tf_op jit(solution)/shard_map/ppermute | solution.py:27
  37.7 3.6 %first.1 = (bf16[1024,1024]{1,0:T(8,128)(2,1)S(1)}, f32[3,1536,128]{2,1,0:T(8,128)S(1)}, f32[1,128]{1,0:T(1,128)S(1)}, f32[1,128]{1,0:T(1,128)S(1)}, f32[7,7,128]{2,1,0:T(8,128)S(1)}) custom-call(bf16[1024,128]{1,0:T(8,128)(2,1)} %bitcast.10, bf16[1024,128]{1,0:T(8,128)(2,1)S(1)} %collective-permute-done.refs_1_, ...), custom_call_target="tpu_custom_call" | custom-call | flops 1207959552 | bytes 4194304 | tf_op jit(solution)/shard_map/first/pallas_call | solution.py:314
  41.4 1.1 %second.1.base = f32[3,1536,128]{2,1,0:T(8,128)S(1)} custom-call(bf16[1024,1024]{1,0:T(8,128)(2,1)S(1)} %get-tuple-element.14.xs, f32[3,1536,128]{2,1,0:T(8,128)S(1)} %get-tuple-element.15.base, bf16[18,32,128]{2,1,0:T(8,128)(2,1)S(1)} %collective-permute-done.12.refs_12_.a2, bf16[18,32,128]{2,1,0:T(8,128)(2,1)S(1)} %collective-permute-done.13.refs_13_.g2, ...), custom_call_target="tpu_custom_call" | custom-call | flops 603979776 | bytes 4194304 | tf_op jit(solution)/shard_map/second/pallas_call | solution.py:334
  42.5 1.4 %third.1 = (bf16[4,256,128]{2,1,0:T(8,128)(2,1)S(1)}, bf16[4,256,128]{2,1,0:T(8,128)(2,1)S(1)}, bf16[2,256,128]{2,1,0:T(8,128)(2,1)S(1)}, f32[4,256,128]{2,1,0:T(8,128)S(1)}) custom-call(bf16[1024,1024]{1,0:T(8,128)(2,1)S(1)} %get-tuple-element.14.xs, f32[3,1536,128]{2,1,0:T(8,128)S(1)} %second.1.base, bf16[18,32,128]{2,1,0:T(8,128)(2,1)S(1)} %collective-permute-done.16.a3, ...), custom_call_target="tpu_custom_call" | custom-call | flops 603979776 | bytes 4194304 | tf_op jit(solution)/shard_map/third/pallas_call | solution.py:343
  43.8 1.0 %collective-permute-start.21 = (bf16[4,256,128]{2,1,0:T(8,128)(2,1)S(1)}, bf16[4,256,128]{2,1,0:T(8,128)(2,1)S(1)}, u32[]{:S(2)}, u32[]{:S(2)}) collective-permute-start(bf16[4,256,128]{2,1,0:T(8,128)(2,1)S(1)} %get-tuple-element.19), channel_id=1, source_target_pairs={{0,1},{1,0},{2,3},{3,2},{4,5},{5,4},{6,7},{7,6},{8,9},{9,8},{10,11... | collective-permute-start | bytes 786440 | tf_op jit(solution)/shard_map/ppermute | solution.py:364
  44.8 3.7 %collective-permute-start.22 = (bf16[4,256,128]{2,1,0:T(8,128)(2,1)S(1)}, bf16[4,256,128]{2,1,0:T(8,128)(2,1)S(1)}, u32[]{:S(2)}, u32[]{:S(2)}) collective-permute-start(bf16[4,256,128]{2,1,0:T(8,128)(2,1)S(1)} %get-tuple-element.22), channel_id=1, source_target_pairs={{1,2},{3,4},{5,6},{7,8},{9,10},{11,12},{13,14},{15,16},{17,18},{19... | collective-permute-start | bytes 786440 | tf_op jit(solution)/shard_map/ppermute | solution.py:363
  48.6 1.2 %depth.2.part = f32[4,256,128]{2,1,0:T(8,128)S(1)} custom-call(f32[4,256,128]{2,1,0:T(8,128)S(1)} %get-tuple-element.17.own, bf16[2,256,128]{2,1,0:T(8,128)(2,1)S(1)} %get-tuple-element.18.mid, bf16[4,256,128]{2,1,0:T(8,128)(2,1)S(1)} %collective-permute-done.21.inner, f32[1,128]{1,0:T(1,128)S(1)} %get-tuple-element.16.bias, ...), custom_call_target="tpu_custom_call" | custom-call | flops 48168960 | bytes 2097152 | tf_op jit(solution)/shard_map/depth/pallas_call | solution.py:371
  49.8 6.4 %collective-permute-done.22.outer = bf16[4,256,128]{2,1,0:T(8,128)(2,1)S(1)} collective-permute-done((bf16[4,256,128]{2,1,0:T(8,128)(2,1)S(1)}, bf16[4,256,128]{2,1,0:T(8,128)(2,1)S(1)}, u32[]{:S(2)}, u32[]{:S(2)}) %collective-permute-start.22) | collective-permute-done | bytes 262176 | tf_op jit(solution)/shard_map/ppermute | solution.py:363
  56.1 1.6 %depth.3 = bf16[4,256,128]{2,1,0:T(8,128)(2,1)} custom-call(f32[4,256,128]{2,1,0:T(8,128)S(1)} %depth.2.part, f32[4,256,128]{2,1,0:T(8,128)S(1)} %get-tuple-element.17.own, bf16[4,256,128]{2,1,0:T(8,128)(2,1)S(1)} %collective-permute-done.22.outer, f32[1,128]{1,0:T(1,128)S(1)} %get-tuple-element.16.bias, f32[7,7,128]{2,1,0:T(8,128)S(1)} %get-tuple-element.21.weight), custom_call_target="tpu_custom_call" | custom-call | flops 32112640 | bytes 2097152 | tf_op jit(solution)/shard_map/depth/pallas_call | solution.py:371
  (33 shorter events, 6.8 us)
Async XLA Ops:
  0.0 1.5 %collective-permute-start.7 = (bf16[9,32,128]{2,1,0:T(8,128)(2,1)}, bf16[9,32,128]{2,1,0:T(8,128)(2,1)S(1)}, u32[]{:S(2)}, u32[]{:S(2)}) collective-permute-start(bf16[9,32,128]{2,1,0:T(8,128)(2,1)} %bitcast.4), channel_id=1, source_target_pairs={{0,1},{1,0},{2,3},{3,2},{4,5},{5,4},{6,7},{7,6},{8,9},{9,8},{10,11... | collective-permute-start | bytes 221192 | tf_op jit(solution)/shard_map/ppermute | solution.py:27
  0.0 6.4 %collective-permute-start.8 = (bf16[9,32,128]{2,1,0:T(8,128)(2,1)}, bf16[9,32,128]{2,1,0:T(8,128)(2,1)S(1)}, u32[]{:S(2)}, u32[]{:S(2)}) collective-permute-start(bf16[9,32,128]{2,1,0:T(8,128)(2,1)} %bitcast.5), channel_id=1, source_target_pairs={{0,16},{1,17},{2,18},{3,19},{4,20},{5,21},{6,22},{7,23},{8,24},{9,... | collective-permute-start | bytes 221192 | tf_op jit(solution)/shard_map/ppermute | solution.py:27
  2.4 11.6 %collective-permute-start.10 = (bf16[18,32,128]{2,1,0:T(8,128)(2,1)S(1)}, bf16[18,32,128]{2,1,0:T(8,128)(2,1)S(1)}, u32[]{:S(2)}, u32[]{:S(2)}) collective-permute-start(bf16[18,32,128]{2,1,0:T(8,128)(2,1)S(1)} %pad_maximum_fusion.3.refs_8_), channel_id=1, source_target_pairs={{0,2},{1,15},{2,4},{3,1},{4,6},{5,3},{6,8},{7,5},{8,10},{9,7},{10,... | collective-permute-start | bytes 442376 | tf_op jit(solution)/shard_map/ppermute | solution.py:27
  6.4 2.7 %collective-permute-start.9 = (bf16[9,32,128]{2,1,0:T(8,128)(2,1)S(1)}, bf16[9,32,128]{2,1,0:T(8,128)(2,1)S(1)}, u32[]{:S(2)}, u32[]{:S(2)}) collective-permute-start(bf16[9,32,128]{2,1,0:T(8,128)(2,1)S(1)} %collective-permute-done.8), channel_id=1, source_target_pairs={{0,1},{1,0},{2,3},{3,2},{4,5},{5,4},{6,7},{7,6},{8,9},{9,8},{10,11... | collective-permute-start | bytes 221192 | tf_op jit(solution)/shard_map/ppermute | solution.py:27
  9.1 7.6 %collective-permute-start.11 = (bf16[18,32,128]{2,1,0:T(8,128)(2,1)S(1)}, bf16[18,32,128]{2,1,0:T(8,128)(2,1)S(1)}, u32[]{:S(2)}, u32[]{:S(2)}) collective-permute-start(bf16[18,32,128]{2,1,0:T(8,128)(2,1)S(1)} %constant_dynamic-update-slice_fusion.refs_9_), channel_id=1, source_target_pairs={{0,2},{1,15},{2,4},{3,1},{4,6},{5,3},{6,8},{7,5},{8,10},{9,7},{10,... | collective-permute-start | bytes 442376 | tf_op jit(solution)/shard_map/ppermute | solution.py:27
  9.7 8.2 %collective-permute-start = (bf16[1024,128]{1,0:T(8,128)(2,1)}, bf16[1024,128]{1,0:T(8,128)(2,1)S(1)}, u32[]{:S(2)}, u32[]{:S(2)}) collective-permute-start(bf16[1024,128]{1,0:T(8,128)(2,1)} %bitcast.7), channel_id=1, source_target_pairs={{0,32},{1,33},{2,34},{3,35},{4,36},{5,37},{6,38},{7,39},{8,40},{9,... | collective-permute-start | bytes 786440 | tf_op jit(solution)/shard_map/ppermute | solution.py:27
  10.4 9.1 %collective-permute-start.1 = (bf16[1024,128]{1,0:T(8,128)(2,1)}, bf16[1024,128]{1,0:T(8,128)(2,1)S(1)}, u32[]{:S(2)}, u32[]{:S(2)}) collective-permute-start(bf16[1024,128]{1,0:T(8,128)(2,1)} %bitcast.8), channel_id=1, source_target_pairs={{0,64},{1,193},{2,66},{3,195},{4,68},{5,197},{6,70},{7,199},{8,72}... | collective-permute-start | bytes 786440 | tf_op jit(solution)/shard_map/ppermute | solution.py:27
  11.9 9.5 %collective-permute-start.2 = (bf16[1024,128]{1,0:T(8,128)(2,1)}, bf16[1024,128]{1,0:T(8,128)(2,1)S(1)}, u32[]{:S(2)}, u32[]{:S(2)}) collective-permute-start(bf16[1024,128]{1,0:T(8,128)(2,1)} %bitcast.9), channel_id=1, source_target_pairs={{0,192},{1,65},{2,194},{3,67},{4,196},{5,69},{6,198},{7,71},{8,200... | collective-permute-start | bytes 786440 | tf_op jit(solution)/shard_map/ppermute | solution.py:27
  14.0 7.4 %collective-permute-start.12 = (bf16[18,32,128]{2,1,0:T(8,128)(2,1)S(1)}, bf16[18,32,128]{2,1,0:T(8,128)(2,1)S(1)}, u32[]{:S(2)}, u32[]{:S(2)}) collective-permute-start(bf16[18,32,128]{2,1,0:T(8,128)(2,1)S(1)} %collective-permute-done.10.refs_10_), channel_id=1, source_target_pairs={{0,2},{1,15},{2,4},{3,1},{4,6},{5,3},{6,8},{7,5},{8,10},{9,7},{10,... | collective-permute-start | bytes 442376 | tf_op jit(solution)/shard_map/ppermute | solution.py:27
  16.7 7.5 %collective-permute-start.13 = (bf16[18,32,128]{2,1,0:T(8,128)(2,1)S(1)}, bf16[18,32,128]{2,1,0:T(8,128)(2,1)S(1)}, u32[]{:S(2)}, u32[]{:S(2)}) collective-permute-start(bf16[18,32,128]{2,1,0:T(8,128)(2,1)S(1)} %collective-permute-done.11.refs_11_), channel_id=1, source_target_pairs={{0,2},{1,15},{2,4},{3,1},{4,6},{5,3},{6,8},{7,5},{8,10},{9,7},{10,... | collective-permute-start | bytes 442376 | tf_op jit(solution)/shard_map/ppermute | solution.py:27
  17.9 12.7 %collective-permute-start.5 = (bf16[1024,128]{1,0:T(8,128)(2,1)S(1)}, bf16[1024,128]{1,0:T(8,128)(2,1)S(1)}, u32[]{:S(2)}, u32[]{:S(2)}) collective-permute-start(bf16[1024,128]{1,0:T(8,128)(2,1)S(1)} %collective-permute-done.refs_1_), channel_id=1, source_target_pairs={{0,192},{1,65},{2,194},{3,67},{4,196},{5,69},{6,198},{7,71},{8,200... | collective-permute-start | bytes 786440 | tf_op jit(solution)/shard_map/ppermute | solution.py:27
  19.5 13.7 %collective-permute-start.3 = (bf16[1024,128]{1,0:T(8,128)(2,1)S(1)}, bf16[1024,128]{1,0:T(8,128)(2,1)S(1)}, u32[]{:S(2)}, u32[]{:S(2)}) collective-permute-start(bf16[1024,128]{1,0:T(8,128)(2,1)S(1)} %collective-permute-done.1.refs_2_), channel_id=1, source_target_pairs={{0,32},{1,33},{2,34},{3,35},{4,36},{5,37},{6,38},{7,39},{8,40},{9,... | collective-permute-start | bytes 786440 | tf_op jit(solution)/shard_map/ppermute | solution.py:27
  21.4 11.9 %collective-permute-start.4 = (bf16[1024,128]{1,0:T(8,128)(2,1)S(1)}, bf16[1024,128]{1,0:T(8,128)(2,1)S(1)}, u32[]{:S(2)}, u32[]{:S(2)}) collective-permute-start(bf16[1024,128]{1,0:T(8,128)(2,1)S(1)} %collective-permute-done.2.refs_3_), channel_id=1, source_target_pairs={{0,64},{1,193},{2,66},{3,195},{4,68},{5,197},{6,70},{7,199},{8,72}... | collective-permute-start | bytes 786440 | tf_op jit(solution)/shard_map/ppermute | solution.py:27
  21.4 8.3 %collective-permute-start.16 = (bf16[18,32,128]{2,1,0:T(8,128)(2,1)S(1)}, bf16[18,32,128]{2,1,0:T(8,128)(2,1)S(1)}, u32[]{:S(2)}, u32[]{:S(2)}) collective-permute-start(bf16[18,32,128]{2,1,0:T(8,128)(2,1)S(1)} %collective-permute-done.12.refs_12_.a2), channel_id=1, source_target_pairs={{0,2},{1,15},{2,4},{3,1},{4,6},{5,3},{6,8},{7,5},{8,10},{9,7},{10,... | collective-permute-start | bytes 442376 | tf_op jit(solution)/shard_map/ppermute | solution.py:27
  24.3 7.1 %collective-permute-start.17 = (bf16[18,32,128]{2,1,0:T(8,128)(2,1)S(1)}, bf16[18,32,128]{2,1,0:T(8,128)(2,1)S(1)}, u32[]{:S(2)}, u32[]{:S(2)}) collective-permute-start(bf16[18,32,128]{2,1,0:T(8,128)(2,1)S(1)} %collective-permute-done.13.refs_13_.g2), channel_id=1, source_target_pairs={{0,2},{1,15},{2,4},{3,1},{4,6},{5,3},{6,8},{7,5},{8,10},{9,7},{10,... | collective-permute-start | bytes 442376 | tf_op jit(solution)/shard_map/ppermute | solution.py:27
  29.8 3.8 %collective-permute-start.14 = (bf16[36,32,128]{2,1,0:T(8,128)(2,1)S(1)}, bf16[36,32,128]{2,1,0:T(8,128)(2,1)S(1)}, u32[]{:S(2)}, u32[]{:S(2)}) collective-permute-start(bf16[36,32,128]{2,1,0:T(8,128)(2,1)S(1)} %pad_maximum_fusion), channel_id=1, source_target_pairs={{0,1},{1,0},{2,3},{3,2},{4,5},{5,4},{6,7},{7,6},{8,9},{9,8},{10,11... | collective-permute-start | bytes 884744 | tf_op jit(solution)/shard_map/ppermute | solution.py:27
  30.6 5.1 %collective-permute-start.15 = (bf16[36,32,128]{2,1,0:T(8,128)(2,1)S(1)}, bf16[36,32,128]{2,1,0:T(8,128)(2,1)S(1)}, u32[]{:S(2)}, u32[]{:S(2)}) collective-permute-start(bf16[36,32,128]{2,1,0:T(8,128)(2,1)S(1)} %pad_maximum_fusion.1), channel_id=1, source_target_pairs={{0,1},{1,0},{2,3},{3,2},{4,5},{5,4},{6,7},{7,6},{8,9},{9,8},{10,11... | collective-permute-start | bytes 884744 | tf_op jit(solution)/shard_map/ppermute | solution.py:27
  31.4 6.4 %collective-permute-start.6 = (bf16[1024,128]{1,0:T(8,128)(2,1)S(1)}, bf16[1024,128]{1,0:T(8,128)(2,1)S(1)}, u32[]{:S(2)}, u32[]{:S(2)}) collective-permute-start(bf16[1024,128]{1,0:T(8,128)(2,1)S(1)} %collective-permute-done.5.refs_6_), channel_id=1, source_target_pairs={{0,64},{1,193},{2,66},{3,195},{4,68},{5,197},{6,70},{7,199},{8,72}... | collective-permute-start | bytes 786440 | tf_op jit(solution)/shard_map/ppermute | solution.py:27
  33.2 8.1 %collective-permute-start.18 = (bf16[36,32,128]{2,1,0:T(8,128)(2,1)S(1)}, bf16[36,32,128]{2,1,0:T(8,128)(2,1)S(1)}, u32[]{:S(2)}, u32[]{:S(2)}) collective-permute-start(bf16[36,32,128]{2,1,0:T(8,128)(2,1)S(1)} %pad_maximum_fusion.2), channel_id=1, source_target_pairs={{0,1},{1,0},{2,3},{3,2},{4,5},{5,4},{6,7},{7,6},{8,9},{9,8},{10,11... | collective-permute-start | bytes 884744 | tf_op jit(solution)/shard_map/ppermute | solution.py:27
  33.3 9.1 %collective-permute-start.19 = (bf16[18,32,128]{2,1,0:T(8,128)(2,1)S(1)}, bf16[18,32,128]{2,1,0:T(8,128)(2,1)S(1)}, u32[]{:S(2)}, u32[]{:S(2)}) collective-permute-start(bf16[18,32,128]{2,1,0:T(8,128)(2,1)S(1)} %collective-permute-done.16.a3), channel_id=1, source_target_pairs={{0,2},{1,15},{2,4},{3,1},{4,6},{5,3},{6,8},{7,5},{8,10},{9,7},{10,... | collective-permute-start | bytes 442376 | tf_op jit(solution)/shard_map/ppermute | solution.py:27
  33.6 8.9 %collective-permute-start.20 = (bf16[18,32,128]{2,1,0:T(8,128)(2,1)S(1)}, bf16[18,32,128]{2,1,0:T(8,128)(2,1)S(1)}, u32[]{:S(2)}, u32[]{:S(2)}) collective-permute-start(bf16[18,32,128]{2,1,0:T(8,128)(2,1)S(1)} %collective-permute-done.17.g3), channel_id=1, source_target_pairs={{0,2},{1,15},{2,4},{3,1},{4,6},{5,3},{6,8},{7,5},{8,10},{9,7},{10,... | collective-permute-start | bytes 442376 | tf_op jit(solution)/shard_map/ppermute | solution.py:27
  43.8 4.7 %collective-permute-start.21 = (bf16[4,256,128]{2,1,0:T(8,128)(2,1)S(1)}, bf16[4,256,128]{2,1,0:T(8,128)(2,1)S(1)}, u32[]{:S(2)}, u32[]{:S(2)}) collective-permute-start(bf16[4,256,128]{2,1,0:T(8,128)(2,1)S(1)} %get-tuple-element.19), channel_id=1, source_target_pairs={{0,1},{1,0},{2,3},{3,2},{4,5},{5,4},{6,7},{7,6},{8,9},{9,8},{10,11... | collective-permute-start | bytes 786440 | tf_op jit(solution)/shard_map/ppermute | solution.py:364
  44.8 11.3 %collective-permute-start.22 = (bf16[4,256,128]{2,1,0:T(8,128)(2,1)S(1)}, bf16[4,256,128]{2,1,0:T(8,128)(2,1)S(1)}, u32[]{:S(2)}, u32[]{:S(2)}) collective-permute-start(bf16[4,256,128]{2,1,0:T(8,128)(2,1)S(1)} %get-tuple-element.22), channel_id=1, source_target_pairs={{1,2},{3,4},{5,6},{7,8},{9,10},{11,12},{13,14},{15,16},{17,18},{19... | collective-permute-start | bytes 786440 | tf_op jit(solution)/shard_map/ppermute | solution.py:363

commit v4 on v3

--- a/solution.py
+++ b/solution.py
@@ -95,46 +95,42 @@
 
 
 class Filters:
-    def __init__(self, copies, target):
-        self.copies, self.target = copies, target
+    def __init__(self, target):
+        self.target = target
         tile = lax.axis_index("tile")
         self.y_hi, self.z, self.core = tile // 16, (tile // 2) % 8, tile % 2
         self.partner_back = (self.core + self.z) % 2 == 1
 
-    def each_piece(self, array, odd, first, core):
+    def place(self, arrays, odd, first, core):
         for piece in range(4):
             half, at_core = (self.y_hi + piece // 2) % 2, (core + piece) % 2
-            source, at = (array[piece // 2], piece % 2) if isinstance(array, tuple) else (array, piece)
             row = first + half * CH + odd * 64 + at_core * 32
             rows = pl.ds(pl.multiple_of(row, 32), 32)
-            yield source.at[pl.ds(9 * at, 9)], self.target.at[:, rows, :]
-
-    def place(self, array, odd, first, core):
-        for src, dst in self.each_piece(array, odd, first, core):
-            self.copies.start(src, dst)
+            array, offset = arrays[piece // 2]
+            begin = offset + 9 * (piece % 2)
+            self.target[:, rows, :] = array[begin : begin + 9]
 
     def place_one(self, mine, others, towards_partner, odd, first):
         use_mine = self.partner_back == towards_partner
-        sems = [self.copies.sems.at[len(self.copies.started) + piece] for piece in range(4)]
-
-        def start(array, core):
-            for (src, dst), sem in zip(self.each_piece(array, odd, first, core), sems):
-                pltpu.make_async_copy(src, dst, sem).start()
-
-        pl.when(use_mine)(lambda: start(mine, self.core))
-        pl.when(jnp.logical_not(use_mine))(lambda: start(others, 1 - self.core))
-        for sem in sems:
-            same_size = pltpu.make_async_copy(mine[0].at[pl.ds(0, 9)], self.target.at[:, pl.ds(0, 32), :], sem)
-            self.copies.started.append(same_size)
+        pl.when(use_mine)(lambda: self.place(mine, odd, first, self.core))
+        pl.when(jnp.logical_not(use_mine))(lambda: self.place(others, odd, first, 1 - self.core))
+
+
+def rows_of(first, second, at=0):
+    return (first, at), (second, at)
+
+
+def of_pack(pack, slot):
+    return (pack, 36 * slot), (pack, 36 * slot + 18)
 
 
 def first_kernel(*refs):
-    blocks, w0, w1, w2, (o1, o2), small = refs[:8], refs[8:10], refs[10:12], refs[12:14], refs[14:16], refs[16:19]
-    (xs, acc, *params), (ws, sems) = refs[19:24], refs[24:]
+    blocks, (a0, g0, a1, g1, a2, g2, o12), small = refs[:8], refs[8:15], refs[15:18]
+    (xs, acc, *params), (ws, sems) = refs[18:23], refs[23:]
     chan = lax.axis_index("chan")
     x, y = chan // 2, chan % 2
     copies = Copies(sems)
-    filters = Filters(copies, ws)
+    filters = Filters(ws)
     z, core = filters.z, filters.core
     turn = 1 - 2 * ((x + core) % 2)
     xl, xm, xf = (x + turn + 4) % 4, (x - turn + 4) % 4, (x + 2) % 4
@@ -142,37 +138,35 @@
     for block, (at_x, at_y) in zip(blocks, places):
         index = 2 * at_x + at_y
         at = 2 * pair_at(index % 4, z) + index // 4
-        copies.start(block, xs.at[:, pl.ds(pl.multiple_of(at * CH, CH), CH)])
+        columns = pl.ds(pl.multiple_of(at * CH, CH), CH)
+        if block is blocks[0]:
+            copies.start(block, xs.at[:, columns])
+            for source, target in zip(small, params):
+                copies.start(source, target)
+        else:
+            xs[:, columns] = block[...]
     even, odd = z % 2, 1 - z % 2
-    filters.place(w0, even, 0, core)
-    filters.place_one(w1, o1, True, odd, 0)
-    filters.place_one(w1, o1, False, odd, 2 * CH)
-    filters.place_one(w2, o2, False, even, 2 * CH)
-    for source, target in zip(small, params):
-        copies.start(source, target)
+    filters.place(rows_of(a0, g0), even, 0, core)
+    filters.place_one(rows_of(a1, g1), of_pack(o12, 0), True, odd, 0)
+    filters.place_one(rows_of(a1, g1), of_pack(o12, 0), False, odd, 2 * CH)
+    filters.place_one(rows_of(a2, g2), of_pack(o12, 1), False, even, 2 * CH)
     copies.wait()
     add_taps(lambda: xs[:, 0 : 4 * CH], ws, acc)
 
 
-def second_kernel(xs, base, a2, g2, a3, g3, o2, o3, acc, ws, sems):
-    w2, w3 = (a2, g2), (a3, g3)
-    copies = Copies(sems)
-    filters = Filters(copies, ws)
+def second_kernel(xs, base, a2, g2, a3, g3, o12, o3, acc, ws):
+    filters = Filters(ws)
     even, odd = filters.z % 2, 1 - filters.z % 2
-    filters.place_one(w2, o2, True, even, 0)
-    filters.place_one(w3, o3, True, odd, 0)
-    copies.wait()
+    filters.place_one(rows_of(a2, g2), of_pack(o12, 1), True, even, 0)
+    filters.place_one(rows_of(a3, g3), of_pack(o3, 0), True, odd, 0)
     add_taps(lambda: xs[:, 4 * CH : 6 * CH], ws, acc, base)
 
 
-def third_kernel(xs, base, a3, g3, o3, a4, g4, bias, outer, inner, mid, own, ws, acc, sems):
-    w3, w4 = (a3, g3), (a4, g4)
-    copies = Copies(sems)
-    filters = Filters(copies, ws)
+def third_kernel(xs, base, a3, g3, o3, a4, g4, bias, outer, inner, mid, own, ws, acc):
+    filters = Filters(ws)
     core, even, odd = filters.core, filters.z % 2, 1 - filters.z % 2
-    filters.place_one(w3, o3, False, odd, 0)
-    filters.place(w4, even, 0, core)
-    copies.wait()
+    filters.place_one(rows_of(a3, g3), of_pack(o3, 0), False, odd, 0)
+    filters.place(rows_of(a4, g4), even, 0, core)
     add_taps(lambda: xs[:, 6 * CH : 8 * CH], ws, acc, base)
 
     column = lax.broadcasted_iota(jnp.int32, (COLS, CH), 0)
@@ -277,18 +271,16 @@
     g0 = jnp.concatenate([h0, move(h0, to_core)])
     g1 = move(g0, to_next)
     a2, g2 = move(a1, to_next), move(g1, to_next)
-    both = jnp.concatenate([a1, g1])
-    o1 = move(both, to_core)
     p_ly, p_ml, p_ym = move(p_l, to_y), move(p_m, to_l), move(p_y, to_m)
     a3, g3 = move(a2, to_next), move(g2, to_next)
-    both = jnp.concatenate([a2, g2])
-    o2 = move(both, to_core)
+    both = jnp.concatenate([a1, g1, a2, g2])
+    o12 = move(both, to_core)
     p_far = move(p_ym, to_l)
     a4, g4 = move(a3, to_next), move(g3, to_next)
     both = jnp.concatenate([a3, g3])
     o3 = move(both, to_core)
     blocks = (in_hbm(p0), p_y, p_l, p_m, p_ly, p_ml, p_ym, p_far)
-    return blocks, ((a0, g0), (a1, g1), (a2, g2), (a3, g3), (a4, g4)), (o1, o2, o3)
+    return blocks, (a0, g0, a1, g1, a2, g2, a3, g3, a4, g4), o12, o3
 
 
 def in_hbm(array):
@@ -296,7 +288,7 @@
 
 
 def body(pixels, conv_weight, conv_bias, depth_weight, depth_bias):
-    anywhere, vmem = pl.BlockSpec(memory_space=pl.ANY), pl.BlockSpec(memory_space=pltpu.VMEM)
+    vmem = pl.BlockSpec(memory_space=pltpu.VMEM)
     hbm = pl.BlockSpec(memory_space=pltpu.HBM)
     f32, bf16 = jnp.float32, jnp.bfloat16
     message = jax.ShapeDtypeStruct((4, COLS, CH), bf16)
@@ -310,7 +302,7 @@
             ),
         )
 
-    blocks, (w0, w1, w2, w3, w4), (o1, o2, o3) = gather_all(pixels, conv_weight)
+    blocks, filters, o12, o3 = gather_all(pixels, conv_weight)
     xs, acc, *params = pl.pallas_call(
         first_kernel,
         out_shape=(
@@ -320,13 +312,13 @@
             jax.ShapeDtypeStruct((1, CH), f32),
             jax.ShapeDtypeStruct((7, 7, CH), f32),
         ),
-        in_specs=[hbm] + [anywhere] * 15 + [hbm] * 3,
+        in_specs=[hbm] + [vmem] * 14 + [hbm] * 3,
         out_specs=(vmem,) * 5,
-        scratch_shapes=[pltpu.VMEM((9, 4 * CH, CH), bf16), pltpu.SemaphoreType.DMA((27,))],
+        scratch_shapes=[pltpu.VMEM((9, 4 * CH, CH), bf16), pltpu.SemaphoreType.DMA((4,))],
         name="first",
         **settings(4),
     )(
-        *blocks, *w0, *w1, *w2, o1, o2,
+        *blocks, *filters[:6], o12,
         in_hbm(conv_bias.reshape(1, CH)),
         in_hbm(depth_bias.reshape(1, CH)),
         in_hbm(depth_weight),
@@ -334,12 +326,12 @@
     acc = pl.pallas_call(
         second_kernel,
         out_shape=sums,
-        in_specs=[vmem] * 2 + [anywhere] * 6,
+        in_specs=[vmem] * 8,
         out_specs=vmem,
-        scratch_shapes=[pltpu.VMEM((9, 2 * CH, CH), bf16), pltpu.SemaphoreType.DMA((8,))],
+        scratch_shapes=[pltpu.VMEM((9, 2 * CH, CH), bf16)],
         name="second",
         **settings(2),
-    )(xs, acc, *w2, *w3, o2, o3)
+    )(xs, acc, *filters[4:8], o12, o3)
     outer, inner, mid, own = pl.pallas_call(
         third_kernel,
         out_shape=(
@@ -348,16 +340,15 @@
             jax.ShapeDtypeStruct((2, COLS, CH), bf16),
             jax.ShapeDtypeStruct((4, COLS, CH), f32),
         ),
-        in_specs=[vmem] * 2 + [anywhere] * 5 + [vmem],
+        in_specs=[vmem] * 8,
         out_specs=(vmem,) * 4,
         scratch_shapes=[
             pltpu.VMEM((9, 2 * CH, CH), bf16),
             pltpu.VMEM((3, 6 * COLS, CH), f32),
-            pltpu.SemaphoreType.DMA((8,)),
         ],
         name="third",
         **settings(2),
-    )(xs, acc, *w3, o3, *w4, params[0])
+    )(xs, acc, *filters[6:8], o3, *filters[8:], params[0])
     bias, depth_bias, weight = params
     across = [(i, i + 1) for i in range(1, 31, 2)]
     from_outer = lax.ppermute(outer, "tile", across + [(j, i) for i, j in across])

time: 57.9 us -> 61.7 us (1.066)
  the two profiles are of different devices: /device:TPU:24 before, /device:TPU:1 now
where the time goes in v4:
time: 61.7 us; the launch traced here: 60.7 us
  starting transfers between devices  39 us (63%)
  waiting for transfers between devices  12.7 us (21%)
  Pallas kernels  7.84 us (13%)
  other arithmetic  1.03 us (2%)
    ppermute x20, starting transfers between devices, move(): return lax.ppermute(block, ('chan', 'tile'), pairs)  33.1 us
    ppermute x20, waiting for transfers between devices, move(): return lax.ppermute(block, ('chan', 'tile'), pairs)  8.16 us
    ppermute x1, waiting for transfers between devices, body(): lax.ppermute(outer, 'tile', across + [(j, i) for i, j in across])  4.54 us
    ppermute x1, starting transfers between devices, body(): from_inner = lax.ppermute(inner, 'tile', [(i, i ^ 1) for i in range(32)])  3.98 us
    pallas_call x1, Pallas kernels, body(): pl.pallas_call(first_kernel, out_shape=(jax.ShapeDtypeStruct((PIX, 8 * CH...  2.92 us
    pallas_call x2, Pallas kernels, depth(): pl.pallas_call(kernel, out_shape=jax.ShapeDtypeStruct((ROWS, COLS, CH), d...  2.78 us
    ppermute x1, starting transfers between devices, body(): lax.ppermute(outer, 'tile', across + [(j, i) for i, j in across])  1.91 us
  transfers between devices with their start and end apart: 22, of which 8 were waited for; matrix products, arithmetic and copies ran while one was open for 2% of the time, Pallas kernels for 8%

profile of v4, /device:TPU:1, one launch (start us, length us, event | category | flops | bytes accessed | tf_op | source)
XLA Modules:
  0.0 60.7 jit_solution(5355609894255623544)
XLA Ops:
  0.0 3.2 %collective-permute-start.7 = (bf16[9,32,128]{2,1,0:T(8,128)(2,1)}, bf16[9,32,128]{2,1,0:T(8,128)(2,1)S(1)}, u32[]{:S(2)}, u32[]{:S(2)}) collective-permute-start(bf16[9,32,128]{2,1,0:T(8,128)(2,1)} %bitcast.4), channel_id=1, source_target_pairs={{0,1},{1,0},{2,3},{3,2},{4,5},{5,4},{6,7},{7,6},{8,9},{9,8},{10,11... | collective-permute-start | bytes 221192 | tf_op jit(solution)/shard_map/ppermute | solution.py:27
  3.2 1.2 %collective-permute-start.8 = (bf16[9,32,128]{2,1,0:T(8,128)(2,1)}, bf16[9,32,128]{2,1,0:T(8,128)(2,1)S(1)}, u32[]{:S(2)}, u32[]{:S(2)}) collective-permute-start(bf16[9,32,128]{2,1,0:T(8,128)(2,1)} %bitcast.5), channel_id=1, source_target_pairs={{0,16},{1,17},{2,18},{3,19},{4,20},{5,21},{6,22},{7,23},{8,24},{9,... | collective-permute-start | bytes 221192 | tf_op jit(solution)/shard_map/ppermute | solution.py:27
  5.3 5.7 %collective-permute-start.10 = (bf16[18,32,128]{2,1,0:T(8,128)(2,1)S(1)}, bf16[18,32,128]{2,1,0:T(8,128)(2,1)S(1)}, u32[]{:S(2)}, u32[]{:S(2)}) collective-permute-start(bf16[18,32,128]{2,1,0:T(8,128)(2,1)S(1)} %pad_maximum_fusion.2.refs_8_), channel_id=1, source_target_pairs={{0,2},{1,15},{2,4},{3,1},{4,6},{5,3},{6,8},{7,5},{8,10},{9,7},{10,... | collective-permute-start | bytes 442376 | tf_op jit(solution)/shard_map/ppermute | solution.py:27
  11.0 1.3 %collective-permute-done.9 = bf16[9,32,128]{2,1,0:T(8,128)(2,1)S(1)} collective-permute-done((bf16[9,32,128]{2,1,0:T(8,128)(2,1)S(1)}, bf16[9,32,128]{2,1,0:T(8,128)(2,1)S(1)}, u32[]{:S(2)}, u32[]{:S(2)}) %collective-permute-start.9) | collective-permute-done | bytes 73760 | tf_op jit(solution)/shard_map/ppermute | solution.py:27
  12.3 2.2 %collective-permute-start.11 = (bf16[18,32,128]{2,1,0:T(8,128)(2,1)S(1)}, bf16[18,32,128]{2,1,0:T(8,128)(2,1)S(1)}, u32[]{:S(2)}, u32[]{:S(2)}) collective-permute-start(bf16[18,32,128]{2,1,0:T(8,128)(2,1)S(1)} %constant_dynamic-update-slice_fusion.refs_9_), channel_id=1, source_target_pairs={{0,2},{1,15},{2,4},{3,1},{4,6},{5,3},{6,8},{7,5},{8,10},{9,7},{10,... | collective-permute-start | bytes 442376 | tf_op jit(solution)/shard_map/ppermute | solution.py:27
  14.5 1.7 %collective-permute-start.12 = (bf16[18,32,128]{2,1,0:T(8,128)(2,1)S(1)}, bf16[18,32,128]{2,1,0:T(8,128)(2,1)S(1)}, u32[]{:S(2)}, u32[]{:S(2)}) collective-permute-start(bf16[18,32,128]{2,1,0:T(8,128)(2,1)S(1)} %collective-permute-done.10.refs_10_), channel_id=1, source_target_pairs={{0,2},{1,15},{2,4},{3,1},{4,6},{5,3},{6,8},{7,5},{8,10},{9,7},{10,... | collective-permute-start | bytes 442376 | tf_op jit(solution)/shard_map/ppermute | solution.py:27
  16.6 3.1 %collective-permute-start.13 = (bf16[18,32,128]{2,1,0:T(8,128)(2,1)S(1)}, bf16[18,32,128]{2,1,0:T(8,128)(2,1)S(1)}, u32[]{:S(2)}, u32[]{:S(2)}) collective-permute-start(bf16[18,32,128]{2,1,0:T(8,128)(2,1)S(1)} %collective-permute-done.11.refs_11_), channel_id=1, source_target_pairs={{0,2},{1,15},{2,4},{3,1},{4,6},{5,3},{6,8},{7,5},{8,10},{9,7},{10,... | collective-permute-start | bytes 442376 | tf_op jit(solution)/shard_map/ppermute | solution.py:27
  19.7 1.3 %collective-permute-start = (bf16[1024,128]{1,0:T(8,128)(2,1)}, bf16[1024,128]{1,0:T(8,128)(2,1)S(1)}, u32[]{:S(2)}, u32[]{:S(2)}) collective-permute-start(bf16[1024,128]{1,0:T(8,128)(2,1)} %bitcast.7), channel_id=1, source_target_pairs={{0,32},{1,33},{2,34},{3,35},{4,36},{5,37},{6,38},{7,39},{8,40},{9,... | collective-permute-start | bytes 786440 | tf_op jit(solution)/shard_map/ppermute | solution.py:27
  21.0 2.5 %collective-permute-start.1 = (bf16[1024,128]{1,0:T(8,128)(2,1)}, bf16[1024,128]{1,0:T(8,128)(2,1)S(1)}, u32[]{:S(2)}, u32[]{:S(2)}) collective-permute-start(bf16[1024,128]{1,0:T(8,128)(2,1)} %bitcast.8), channel_id=1, source_target_pairs={{0,64},{1,193},{2,66},{3,195},{4,68},{5,197},{6,70},{7,199},{8,72}... | collective-permute-start | bytes 786440 | tf_op jit(solution)/shard_map/ppermute | solution.py:27
  23.5 1.8 %collective-permute-start.14 = (bf16[72,32,128]{2,1,0:T(8,128)(2,1)S(1)}, bf16[72,32,128]{2,1,0:T(8,128)(2,1)S(1)}, u32[]{:S(2)}, u32[]{:S(2)}) collective-permute-start(bf16[72,32,128]{2,1,0:T(8,128)(2,1)S(1)} %pad_maximum_fusion), channel_id=1, source_target_pairs={{0,1},{1,0},{2,3},{3,2},{4,5},{5,4},{6,7},{7,6},{8,9},{9,8},{10,11... | collective-permute-start | bytes 1769480 | tf_op jit(solution)/shard_map/ppermute | solution.py:27
  25.4 1.2 %collective-permute-start.2 = (bf16[1024,128]{1,0:T(8,128)(2,1)}, bf16[1024,128]{1,0:T(8,128)(2,1)S(1)}, u32[]{:S(2)}, u32[]{:S(2)}) collective-permute-start(bf16[1024,128]{1,0:T(8,128)(2,1)} %bitcast.9), channel_id=1, source_target_pairs={{0,192},{1,65},{2,194},{3,67},{4,196},{5,69},{6,198},{7,71},{8,200... | collective-permute-start | bytes 786440 | tf_op jit(solution)/shard_map/ppermute | solution.py:27
  27.6 1.2 %collective-permute-start.5 = (bf16[1024,128]{1,0:T(8,128)(2,1)S(1)}, bf16[1024,128]{1,0:T(8,128)(2,1)S(1)}, u32[]{:S(2)}, u32[]{:S(2)}) collective-permute-start(bf16[1024,128]{1,0:T(8,128)(2,1)S(1)} %collective-permute-done.refs_1_), channel_id=1, source_target_pairs={{0,192},{1,65},{2,194},{3,67},{4,196},{5,69},{6,198},{7,71},{8,200... | collective-permute-start | bytes 786440 | tf_op jit(solution)/shard_map/ppermute | solution.py:27
  28.8 2.3 %collective-permute-done.2.refs_3_ = bf16[1024,128]{1,0:T(8,128)(2,1)S(1)} collective-permute-done((bf16[1024,128]{1,0:T(8,128)(2,1)}, bf16[1024,128]{1,0:T(8,128)(2,1)S(1)}, u32[]{:S(2)}, u32[]{:S(2)}) %collective-permute-start.2) | collective-permute-done | bytes 262176 | tf_op jit(solution)/shard_map/ppermute | solution.py:27
  31.8 1.3 %collective-permute-done.15.a3 = bf16[18,32,128]{2,1,0:T(8,128)(2,1)S(1)} collective-permute-done((bf16[18,32,128]{2,1,0:T(8,128)(2,1)S(1)}, bf16[18,32,128]{2,1,0:T(8,128)(2,1)S(1)}, u32[]{:S(2)}, u32[]{:S(2)}) %collective-permute-start.15) | collective-permute-done | bytes 147488 | tf_op jit(solution)/shard_map/ppermute | solution.py:27
  33.1 1.8 %collective-permute-start.4 = (bf16[1024,128]{1,0:T(8,128)(2,1)S(1)}, bf16[1024,128]{1,0:T(8,128)(2,1)S(1)}, u32[]{:S(2)}, u32[]{:S(2)}) collective-permute-start(bf16[1024,128]{1,0:T(8,128)(2,1)S(1)} %collective-permute-done.2.refs_3_), channel_id=1, source_target_pairs={{0,64},{1,193},{2,66},{3,195},{4,68},{5,197},{6,70},{7,199},{8,72}... | collective-permute-start | bytes 786440 | tf_op jit(solution)/shard_map/ppermute | solution.py:27
  34.9 1.5 %collective-permute-start.6 = (bf16[1024,128]{1,0:T(8,128)(2,1)S(1)}, bf16[1024,128]{1,0:T(8,128)(2,1)S(1)}, u32[]{:S(2)}, u32[]{:S(2)}) collective-permute-start(bf16[1024,128]{1,0:T(8,128)(2,1)S(1)} %collective-permute-done.5.refs_6_), channel_id=1, source_target_pairs={{0,64},{1,193},{2,66},{3,195},{4,68},{5,197},{6,70},{7,199},{8,72}... | collective-permute-start | bytes 786440 | tf_op jit(solution)/shard_map/ppermute | solution.py:27
  36.4 2.7 %collective-permute-start.17 = (bf16[36,32,128]{2,1,0:T(8,128)(2,1)S(1)}, bf16[36,32,128]{2,1,0:T(8,128)(2,1)S(1)}, u32[]{:S(2)}, u32[]{:S(2)}) collective-permute-start(bf16[36,32,128]{2,1,0:T(8,128)(2,1)S(1)} %pad_maximum_fusion.1), channel_id=1, source_target_pairs={{0,1},{1,0},{2,3},{3,2},{4,5},{5,4},{6,7},{7,6},{8,9},{9,8},{10,11... | collective-permute-start | bytes 884744 | tf_op jit(solution)/shard_map/ppermute | solution.py:27
  39.5 1.2 %collective-permute-start.19 = (bf16[18,32,128]{2,1,0:T(8,128)(2,1)S(1)}, bf16[18,32,128]{2,1,0:T(8,128)(2,1)S(1)}, u32[]{:S(2)}, u32[]{:S(2)}) collective-permute-start(bf16[18,32,128]{2,1,0:T(8,128)(2,1)S(1)} %collective-permute-done.16.g3), channel_id=1, source_target_pairs={{0,2},{1,15},{2,4},{3,1},{4,6},{5,3},{6,8},{7,5},{8,10},{9,7},{10,... | collective-permute-start | bytes 442376 | tf_op jit(solution)/shard_map/ppermute | solution.py:27
  40.7 1.6 %collective-permute-done.6.refs_7_ = bf16[1024,128]{1,0:T(8,128)(2,1)S(1)} collective-permute-done((bf16[1024,128]{1,0:T(8,128)(2,1)S(1)}, bf16[1024,128]{1,0:T(8,128)(2,1)S(1)}, u32[]{:S(2)}, u32[]{:S(2)}) %collective-permute-start.6) | collective-permute-done | bytes 262176 | tf_op jit(solution)/shard_map/ppermute | solution.py:27
  42.3 2.9 %first.1 = (bf16[1024,1024]{1,0:T(8,128)(2,1)S(1)}, f32[3,1536,128]{2,1,0:T(8,128)S(1)}, f32[1,128]{1,0:T(1,128)S(1)}, f32[1,128]{1,0:T(1,128)S(1)}, f32[7,7,128]{2,1,0:T(8,128)S(1)}) custom-call(bf16[1024,128]{1,0:T(8,128)(2,1)} %bitcast.10, bf16[1024,128]{1,0:T(8,128)(2,1)S(1)} %collective-permute-done.refs_1_, ...), custom_call_target="tpu_custom_call" | custom-call | flops 1207959552 | bytes 4194304 | tf_op jit(solution)/shard_map/first/pallas_call | solution.py:306
  47.4 4.0 %collective-permute-start.20 = (bf16[4,256,128]{2,1,0:T(8,128)(2,1)S(1)}, bf16[4,256,128]{2,1,0:T(8,128)(2,1)S(1)}, u32[]{:S(2)}, u32[]{:S(2)}) collective-permute-start(bf16[4,256,128]{2,1,0:T(8,128)(2,1)S(1)} %get-tuple-element.19), channel_id=1, source_target_pairs={{0,1},{1,0},{2,3},{3,2},{4,5},{5,4},{6,7},{7,6},{8,9},{9,8},{10,11... | collective-permute-start | bytes 786440 | tf_op jit(solution)/shard_map/ppermute | solution.py:355
  51.4 1.9 %collective-permute-start.21 = (bf16[4,256,128]{2,1,0:T(8,128)(2,1)S(1)}, bf16[4,256,128]{2,1,0:T(8,128)(2,1)S(1)}, u32[]{:S(2)}, u32[]{:S(2)}) collective-permute-start(bf16[4,256,128]{2,1,0:T(8,128)(2,1)S(1)} %get-tuple-element.22), channel_id=1, source_target_pairs={{1,2},{3,4},{5,6},{7,8},{9,10},{11,12},{13,14},{15,16},{17,18},{19... | collective-permute-start | bytes 786440 | tf_op jit(solution)/shard_map/ppermute | solution.py:354
  54.6 4.5 %collective-permute-done.21.outer = bf16[4,256,128]{2,1,0:T(8,128)(2,1)S(1)} collective-permute-done((bf16[4,256,128]{2,1,0:T(8,128)(2,1)S(1)}, bf16[4,256,128]{2,1,0:T(8,128)(2,1)S(1)}, u32[]{:S(2)}, u32[]{:S(2)}) %collective-permute-start.21) | collective-permute-done | bytes 262176 | tf_op jit(solution)/shard_map/ppermute | solution.py:354
  59.1 1.6 %depth.3 = bf16[4,256,128]{2,1,0:T(8,128)(2,1)} custom-call(f32[4,256,128]{2,1,0:T(8,128)S(1)} %depth.2.part, f32[4,256,128]{2,1,0:T(8,128)S(1)} %get-tuple-element.17.own, bf16[4,256,128]{2,1,0:T(8,128)(2,1)S(1)} %collective-permute-done.21.outer, f32[1,128]{1,0:T(1,128)S(1)} %get-tuple-element.16.bias, f32[7,7,128]{2,1,0:T(8,128)S(1)} %get-tuple-element.21.weight), custom_call_target="tpu_custom_call" | custom-call | flops 32112640 | bytes 2097152 | tf_op jit(solution)/shard_map/depth/pallas_call | solution.py:362
  (30 shorter events, 6.8 us)
Async XLA Ops:
  0.0 4.4 %collective-permute-start.7 = (bf16[9,32,128]{2,1,0:T(8,128)(2,1)}, bf16[9,32,128]{2,1,0:T(8,128)(2,1)S(1)}, u32[]{:S(2)}, u32[]{:S(2)}) collective-permute-start(bf16[9,32,128]{2,1,0:T(8,128)(2,1)} %bitcast.4), channel_id=1, source_target_pairs={{0,1},{1,0},{2,3},{3,2},{4,5},{5,4},{6,7},{7,6},{8,9},{9,8},{10,11... | collective-permute-start | bytes 221192 | tf_op jit(solution)/shard_map/ppermute | solution.py:27
  3.2 7.8 %collective-permute-start.8 = (bf16[9,32,128]{2,1,0:T(8,128)(2,1)}, bf16[9,32,128]{2,1,0:T(8,128)(2,1)S(1)}, u32[]{:S(2)}, u32[]{:S(2)}) collective-permute-start(bf16[9,32,128]{2,1,0:T(8,128)(2,1)} %bitcast.5), channel_id=1, source_target_pairs={{0,16},{1,17},{2,18},{3,19},{4,20},{5,21},{6,22},{7,23},{8,24},{9,... | collective-permute-start | bytes 221192 | tf_op jit(solution)/shard_map/ppermute | solution.py:27
  5.3 9.1 %collective-permute-start.10 = (bf16[18,32,128]{2,1,0:T(8,128)(2,1)S(1)}, bf16[18,32,128]{2,1,0:T(8,128)(2,1)S(1)}, u32[]{:S(2)}, u32[]{:S(2)}) collective-permute-start(bf16[18,32,128]{2,1,0:T(8,128)(2,1)S(1)} %pad_maximum_fusion.2.refs_8_), channel_id=1, source_target_pairs={{0,2},{1,15},{2,4},{3,1},{4,6},{5,3},{6,8},{7,5},{8,10},{9,7},{10,... | collective-permute-start | bytes 442376 | tf_op jit(solution)/shard_map/ppermute | solution.py:27
  11.0 1.3 %collective-permute-start.9 = (bf16[9,32,128]{2,1,0:T(8,128)(2,1)S(1)}, bf16[9,32,128]{2,1,0:T(8,128)(2,1)S(1)}, u32[]{:S(2)}, u32[]{:S(2)}) collective-permute-start(bf16[9,32,128]{2,1,0:T(8,128)(2,1)S(1)} %collective-permute-done.8), channel_id=1, source_target_pairs={{0,1},{1,0},{2,3},{3,2},{4,5},{5,4},{6,7},{7,6},{8,9},{9,8},{10,11... | collective-permute-start | bytes 221192 | tf_op jit(solution)/shard_map/ppermute | solution.py:27
  12.3 4.3 %collective-permute-start.11 = (bf16[18,32,128]{2,1,0:T(8,128)(2,1)S(1)}, bf16[18,32,128]{2,1,0:T(8,128)(2,1)S(1)}, u32[]{:S(2)}, u32[]{:S(2)}) collective-permute-start(bf16[18,32,128]{2,1,0:T(8,128)(2,1)S(1)} %constant_dynamic-update-slice_fusion.refs_9_), channel_id=1, source_target_pairs={{0,2},{1,15},{2,4},{3,1},{4,6},{5,3},{6,8},{7,5},{8,10},{9,7},{10,... | collective-permute-start | bytes 442376 | tf_op jit(solution)/shard_map/ppermute | solution.py:27
  14.5 9.0 %collective-permute-start.12 = (bf16[18,32,128]{2,1,0:T(8,128)(2,1)S(1)}, bf16[18,32,128]{2,1,0:T(8,128)(2,1)S(1)}, u32[]{:S(2)}, u32[]{:S(2)}) collective-permute-start(bf16[18,32,128]{2,1,0:T(8,128)(2,1)S(1)} %collective-permute-done.10.refs_10_), channel_id=1, source_target_pairs={{0,2},{1,15},{2,4},{3,1},{4,6},{5,3},{6,8},{7,5},{8,10},{9,7},{10,... | collective-permute-start | bytes 442376 | tf_op jit(solution)/shard_map/ppermute | solution.py:27
  16.6 6.9 %collective-permute-start.13 = (bf16[18,32,128]{2,1,0:T(8,128)(2,1)S(1)}, bf16[18,32,128]{2,1,0:T(8,128)(2,1)S(1)}, u32[]{:S(2)}, u32[]{:S(2)}) collective-permute-start(bf16[18,32,128]{2,1,0:T(8,128)(2,1)S(1)} %collective-permute-done.11.refs_11_), channel_id=1, source_target_pairs={{0,2},{1,15},{2,4},{3,1},{4,6},{5,3},{6,8},{7,5},{8,10},{9,7},{10,... | collective-permute-start | bytes 442376 | tf_op jit(solution)/shard_map/ppermute | solution.py:27
  19.7 7.9 %collective-permute-start = (bf16[1024,128]{1,0:T(8,128)(2,1)}, bf16[1024,128]{1,0:T(8,128)(2,1)S(1)}, u32[]{:S(2)}, u32[]{:S(2)}) collective-permute-start(bf16[1024,128]{1,0:T(8,128)(2,1)} %bitcast.7), channel_id=1, source_target_pairs={{0,32},{1,33},{2,34},{3,35},{4,36},{5,37},{6,38},{7,39},{8,40},{9,... | collective-permute-start | bytes 786440 | tf_op jit(solution)/shard_map/ppermute | solution.py:27
  21.0 7.8 %collective-permute-start.1 = (bf16[1024,128]{1,0:T(8,128)(2,1)}, bf16[1024,128]{1,0:T(8,128)(2,1)S(1)}, u32[]{:S(2)}, u32[]{:S(2)}) collective-permute-start(bf16[1024,128]{1,0:T(8,128)(2,1)} %bitcast.8), channel_id=1, source_target_pairs={{0,64},{1,193},{2,66},{3,195},{4,68},{5,197},{6,70},{7,199},{8,72}... | collective-permute-start | bytes 786440 | tf_op jit(solution)/shard_map/ppermute | solution.py:27
  23.5 18.8 %collective-permute-start.14 = (bf16[72,32,128]{2,1,0:T(8,128)(2,1)S(1)}, bf16[72,32,128]{2,1,0:T(8,128)(2,1)S(1)}, u32[]{:S(2)}, u32[]{:S(2)}) collective-permute-start(bf16[72,32,128]{2,1,0:T(8,128)(2,1)S(1)} %pad_maximum_fusion), channel_id=1, source_target_pairs={{0,1},{1,0},{2,3},{3,2},{4,5},{5,4},{6,7},{7,6},{8,9},{9,8},{10,11... | collective-permute-start | bytes 1769480 | tf_op jit(solution)/shard_map/ppermute | solution.py:27
  25.4 5.7 %collective-permute-start.2 = (bf16[1024,128]{1,0:T(8,128)(2,1)}, bf16[1024,128]{1,0:T(8,128)(2,1)S(1)}, u32[]{:S(2)}, u32[]{:S(2)}) collective-permute-start(bf16[1024,128]{1,0:T(8,128)(2,1)} %bitcast.9), channel_id=1, source_target_pairs={{0,192},{1,65},{2,194},{3,67},{4,196},{5,69},{6,198},{7,71},{8,200... | collective-permute-start | bytes 786440 | tf_op jit(solution)/shard_map/ppermute | solution.py:27
  27.6 7.3 %collective-permute-start.5 = (bf16[1024,128]{1,0:T(8,128)(2,1)S(1)}, bf16[1024,128]{1,0:T(8,128)(2,1)S(1)}, u32[]{:S(2)}, u32[]{:S(2)}) collective-permute-start(bf16[1024,128]{1,0:T(8,128)(2,1)S(1)} %collective-permute-done.refs_1_), channel_id=1, source_target_pairs={{0,192},{1,65},{2,194},{3,67},{4,196},{5,69},{6,198},{7,71},{8,200... | collective-permute-start | bytes 786440 | tf_op jit(solution)/shard_map/ppermute | solution.py:27
  28.8 4.3 %collective-permute-start.15 = (bf16[18,32,128]{2,1,0:T(8,128)(2,1)S(1)}, bf16[18,32,128]{2,1,0:T(8,128)(2,1)S(1)}, u32[]{:S(2)}, u32[]{:S(2)}) collective-permute-start(bf16[18,32,128]{2,1,0:T(8,128)(2,1)S(1)} %collective-permute-done.12.refs_12_.a2), channel_id=1, source_target_pairs={{0,2},{1,15},{2,4},{3,1},{4,6},{5,3},{6,8},{7,5},{8,10},{9,7},{10,... | collective-permute-start | bytes 442376 | tf_op jit(solution)/shard_map/ppermute | solution.py:27
  28.8 7.6 %collective-permute-start.16 = (bf16[18,32,128]{2,1,0:T(8,128)(2,1)S(1)}, bf16[18,32,128]{2,1,0:T(8,128)(2,1)S(1)}, u32[]{:S(2)}, u32[]{:S(2)}) collective-permute-start(bf16[18,32,128]{2,1,0:T(8,128)(2,1)S(1)} %collective-permute-done.13.refs_13_.g2), channel_id=1, source_target_pairs={{0,2},{1,15},{2,4},{3,1},{4,6},{5,3},{6,8},{7,5},{8,10},{9,7},{10,... | collective-permute-start | bytes 442376 | tf_op jit(solution)/shard_map/ppermute | solution.py:27
  31.1 8.1 %collective-permute-start.3 = (bf16[1024,128]{1,0:T(8,128)(2,1)S(1)}, bf16[1024,128]{1,0:T(8,128)(2,1)S(1)}, u32[]{:S(2)}, u32[]{:S(2)}) collective-permute-start(bf16[1024,128]{1,0:T(8,128)(2,1)S(1)} %collective-permute-done.1.refs_2_), channel_id=1, source_target_pairs={{0,32},{1,33},{2,34},{3,35},{4,36},{5,37},{6,38},{7,39},{8,40},{9,... | collective-permute-start | bytes 786440 | tf_op jit(solution)/shard_map/ppermute | solution.py:27
  33.1 6.4 %collective-permute-start.4 = (bf16[1024,128]{1,0:T(8,128)(2,1)S(1)}, bf16[1024,128]{1,0:T(8,128)(2,1)S(1)}, u32[]{:S(2)}, u32[]{:S(2)}) collective-permute-start(bf16[1024,128]{1,0:T(8,128)(2,1)S(1)} %collective-permute-done.2.refs_3_), channel_id=1, source_target_pairs={{0,64},{1,193},{2,66},{3,195},{4,68},{5,197},{6,70},{7,199},{8,72}... | collective-permute-start | bytes 786440 | tf_op jit(solution)/shard_map/ppermute | solution.py:27
  34.9 7.4 %collective-permute-start.6 = (bf16[1024,128]{1,0:T(8,128)(2,1)S(1)}, bf16[1024,128]{1,0:T(8,128)(2,1)S(1)}, u32[]{:S(2)}, u32[]{:S(2)}) collective-permute-start(bf16[1024,128]{1,0:T(8,128)(2,1)S(1)} %collective-permute-done.5.refs_6_), channel_id=1, source_target_pairs={{0,64},{1,193},{2,66},{3,195},{4,68},{5,197},{6,70},{7,199},{8,72}... | collective-permute-start | bytes 786440 | tf_op jit(solution)/shard_map/ppermute | solution.py:27
  36.4 8.8 %collective-permute-start.17 = (bf16[36,32,128]{2,1,0:T(8,128)(2,1)S(1)}, bf16[36,32,128]{2,1,0:T(8,128)(2,1)S(1)}, u32[]{:S(2)}, u32[]{:S(2)}) collective-permute-start(bf16[36,32,128]{2,1,0:T(8,128)(2,1)S(1)} %pad_maximum_fusion.1), channel_id=1, source_target_pairs={{0,1},{1,0},{2,3},{3,2},{4,5},{5,4},{6,7},{7,6},{8,9},{9,8},{10,11... | collective-permute-start | bytes 884744 | tf_op jit(solution)/shard_map/ppermute | solution.py:27
  39.2 7.0 %collective-permute-start.18 = (bf16[18,32,128]{2,1,0:T(8,128)(2,1)S(1)}, bf16[18,32,128]{2,1,0:T(8,128)(2,1)S(1)}, u32[]{:S(2)}, u32[]{:S(2)}) collective-permute-start(bf16[18,32,128]{2,1,0:T(8,128)(2,1)S(1)} %collective-permute-done.15.a3), channel_id=1, source_target_pairs={{0,2},{1,15},{2,4},{3,1},{4,6},{5,3},{6,8},{7,5},{8,10},{9,7},{10,... | collective-permute-start | bytes 442376 | tf_op jit(solution)/shard_map/ppermute | solution.py:27
  39.5 6.7 %collective-permute-start.19 = (bf16[18,32,128]{2,1,0:T(8,128)(2,1)S(1)}, bf16[18,32,128]{2,1,0:T(8,128)(2,1)S(1)}, u32[]{:S(2)}, u32[]{:S(2)}) collective-permute-start(bf16[18,32,128]{2,1,0:T(8,128)(2,1)S(1)} %collective-permute-done.16.g3), channel_id=1, source_target_pairs={{0,2},{1,15},{2,4},{3,1},{4,6},{5,3},{6,8},{7,5},{8,10},{9,7},{10,... | collective-permute-start | bytes 442376 | tf_op jit(solution)/shard_map/ppermute | solution.py:27
  47.4 5.9 %collective-permute-start.20 = (bf16[4,256,128]{2,1,0:T(8,128)(2,1)S(1)}, bf16[4,256,128]{2,1,0:T(8,128)(2,1)S(1)}, u32[]{:S(2)}, u32[]{:S(2)}) collective-permute-start(bf16[4,256,128]{2,1,0:T(8,128)(2,1)S(1)} %get-tuple-element.19), channel_id=1, source_target_pairs={{0,1},{1,0},{2,3},{3,2},{4,5},{5,4},{6,7},{7,6},{8,9},{9,8},{10,11... | collective-permute-start | bytes 786440 | tf_op jit(solution)/shard_map/ppermute | solution.py:355
  51.4 7.7 %collective-permute-start.21 = (bf16[4,256,128]{2,1,0:T(8,128)(2,1)S(1)}, bf16[4,256,128]{2,1,0:T(8,128)(2,1)S(1)}, u32[]{:S(2)}, u32[]{:S(2)}) collective-permute-start(bf16[4,256,128]{2,1,0:T(8,128)(2,1)S(1)} %get-tuple-element.22), channel_id=1, source_target_pairs={{1,2},{3,4},{5,6},{7,8},{9,10},{11,12},{13,14},{15,16},{17,18},{19... | collective-permute-start | bytes 786440 | tf_op jit(solution)/shard_map/ppermute | solution.py:354

commit v5 on v4

--- a/solution.py
+++ b/solution.py
@@ -130,6 +130,8 @@
     chan = lax.axis_index("chan")
     x, y = chan // 2, chan % 2
     copies = Copies(sems)
+    for source, target in zip(small, params):
+        copies.start(source, target)
     filters = Filters(ws)
     z, core = filters.z, filters.core
     turn = 1 - 2 * ((x + core) % 2)
@@ -139,19 +141,14 @@
         index = 2 * at_x + at_y
         at = 2 * pair_at(index % 4, z) + index // 4
         columns = pl.ds(pl.multiple_of(at * CH, CH), CH)
-        if block is blocks[0]:
-            copies.start(block, xs.at[:, columns])
-            for source, target in zip(small, params):
-                copies.start(source, target)
-        else:
-            xs[:, columns] = block[...]
+        xs[:, columns] = block[...]
     even, odd = z % 2, 1 - z % 2
     filters.place(rows_of(a0, g0), even, 0, core)
     filters.place_one(rows_of(a1, g1), of_pack(o12, 0), True, odd, 0)
     filters.place_one(rows_of(a1, g1), of_pack(o12, 0), False, odd, 2 * CH)
     filters.place_one(rows_of(a2, g2), of_pack(o12, 1), False, even, 2 * CH)
+    add_taps(lambda: xs[:, 0 : 4 * CH], ws, acc)
     copies.wait()
-    add_taps(lambda: xs[:, 0 : 4 * CH], ws, acc)
 
 
 def second_kernel(xs, base, a2, g2, a3, g3, o12, o3, acc, ws):
@@ -260,13 +257,25 @@
     add_depth(rows, -3, weight, hidden, lambda row, columns: part[row, columns, :], finish)
 
 
+def pack_kernel(mine, others, both):
+    both[0:9] = mine[...]
+    both[9:18] = others[...]
+
+
 def gather_all(pixels, weight):
     p0 = pixels.reshape(PIX, CH)
     w0 = weight.reshape(9, 32, CH)
     h0 = move(w0, to_hi)
     w0_other = move(w0, to_core)
     p_y, p_l, p_m = move(p0, to_y), move(p0, to_l), move(p0, to_m)
-    a0 = jnp.concatenate([w0, w0_other])
+    a0 = pl.pallas_call(
+        pack_kernel,
+        out_shape=jax.ShapeDtypeStruct((18, 32, CH), jnp.bfloat16),
+        in_specs=[pl.BlockSpec(memory_space=pltpu.VMEM)] * 2,
+        out_specs=pl.BlockSpec(memory_space=pltpu.VMEM),
+        compiler_params=pltpu.CompilerParams(vmem_limit_bytes=2 << 20),
+        name="pack",
+    )(w0, w0_other)
     a1 = move(a0, to_next)
     g0 = jnp.concatenate([h0, move(h0, to_core)])
     g1 = move(g0, to_next)
@@ -279,7 +288,7 @@
     a4, g4 = move(a3, to_next), move(g3, to_next)
     both = jnp.concatenate([a3, g3])
     o3 = move(both, to_core)
-    blocks = (in_hbm(p0), p_y, p_l, p_m, p_ly, p_ml, p_ym, p_far)
+    blocks = (p0, p_y, p_l, p_m, p_ly, p_ml, p_ym, p_far)
     return blocks, (a0, g0, a1, g1, a2, g2, a3, g3, a4, g4), o12, o3
 
 
@@ -312,9 +321,9 @@
             jax.ShapeDtypeStruct((1, CH), f32),
             jax.ShapeDtypeStruct((7, 7, CH), f32),
         ),
-        in_specs=[hbm] + [vmem] * 14 + [hbm] * 3,
+        in_specs=[vmem] * 15 + [hbm] * 3,
         out_specs=(vmem,) * 5,
-        scratch_shapes=[pltpu.VMEM((9, 4 * CH, CH), bf16), pltpu.SemaphoreType.DMA((4,))],
+        scratch_shapes=[pltpu.VMEM((9, 4 * CH, CH), bf16), pltpu.SemaphoreType.DMA((3,))],
         name="first",
         **settings(4),
     )(

time: 61.7 us -> 61.3 us (level)
  other arithmetic: 1.03 us -> 0.1 us
  local copies, waits for them, and re-layouts: 0.02 us -> 0.94 us
    concatenate x1 -> x0, other arithmetic: 0.93 us -> none  [gather_all(): a0 = jnp.concatenate([w0, w0_other])]
    unnamed x1 -> x5, local copies, waits for them, and re-layouts: 0.01 us -> 0.92 us
    pallas_call x1, Pallas kernels: 2.92 us -> 2.3 us  [body(): pl.pallas_call(first_kernel, out_shape=(jax.ShapeDtypeStruct((PIX, 8 * CH...]
  transfers between devices with their start and end apart: 22 -> 22, of which waited for: 8 -> 8; matrix products, arithmetic and copies ran while one was open for 2% -> 0% of each run, Pallas kernels for 8% -> 7%
where the time goes in v5:
time: 61.3 us; the launch traced here: 60.3 us
  starting transfers between devices  39.2 us (64%)
  waiting for transfers between devices  12.7 us (21%)
  Pallas kernels  7.23 us (12%)
  local copies, waits for them, and re-layouts  0.94 us (2%)
    ppermute x20, starting transfers between devices, move(): return lax.ppermute(block, ('chan', 'tile'), pairs)  33.1 us
    ppermute x20, waiting for transfers between devices, move(): return lax.ppermute(block, ('chan', 'tile'), pairs)  8.16 us
    ppermute x1, waiting for transfers between devices, body(): lax.ppermute(outer, 'tile', across + [(j, i) for i, j in across])  4.54 us
    ppermute x1, starting transfers between devices, body(): from_inner = lax.ppermute(inner, 'tile', [(i, i ^ 1) for i in range(32)])  4.19 us
    pallas_call x2, Pallas kernels, depth(): pl.pallas_call(kernel, out_shape=jax.ShapeDtypeStruct((ROWS, COLS, CH), d...  2.78 us
    pallas_call x1, Pallas kernels, body(): pl.pallas_call(first_kernel, out_shape=(jax.ShapeDtypeStruct((PIX, 8 * CH...  2.3 us
    ppermute x1, starting transfers between devices, body(): lax.ppermute(outer, 'tile', across + [(j, i) for i, j in across])  1.91 us
  transfers between devices with their start and end apart: 22, of which 8 were waited for; matrix products, arithmetic and copies ran while one was open for 0% of the time, Pallas kernels for 7%

profile of v5, /device:TPU:1, one launch (start us, length us, event | category | flops | bytes accessed | tf_op | source)
XLA Modules:
  0.0 60.3 jit_solution(14521366350282544932)
XLA Ops:
  0.0 3.2 %collective-permute-start.7 = (bf16[9,32,128]{2,1,0:T(8,128)(2,1)}, bf16[9,32,128]{2,1,0:T(8,128)(2,1)S(1)}, u32[]{:S(2)}, u32[]{:S(2)}) collective-permute-start(bf16[9,32,128]{2,1,0:T(8,128)(2,1)} %bitcast.4), channel_id=1, source_target_pairs={{0,1},{1,0},{2,3},{3,2},{4,5},{5,4},{6,7},{7,6},{8,9},{9,8},{10,11... | collective-permute-start | bytes 221192 | tf_op jit(solution)/shard_map/ppermute | solution.py:27
  3.2 1.2 %collective-permute-start.8 = (bf16[9,32,128]{2,1,0:T(8,128)(2,1)}, bf16[9,32,128]{2,1,0:T(8,128)(2,1)S(1)}, u32[]{:S(2)}, u32[]{:S(2)}) collective-permute-start(bf16[9,32,128]{2,1,0:T(8,128)(2,1)} %bitcast.5), channel_id=1, source_target_pairs={{0,16},{1,17},{2,18},{3,19},{4,20},{5,21},{6,22},{7,23},{8,24},{9,... | collective-permute-start | bytes 221192 | tf_op jit(solution)/shard_map/ppermute | solution.py:27
  5.3 5.7 %collective-permute-start.10 = (bf16[18,32,128]{2,1,0:T(8,128)(2,1)S(1)}, bf16[18,32,128]{2,1,0:T(8,128)(2,1)S(1)}, u32[]{:S(2)}, u32[]{:S(2)}) collective-permute-start(bf16[18,32,128]{2,1,0:T(8,128)(2,1)S(1)} %pack.1.refs_8_), channel_id=1, source_target_pairs={{0,2},{1,15},{2,4},{3,1},{4,6},{5,3},{6,8},{7,5},{8,10},{9,7},{10,... | collective-permute-start | bytes 442376 | tf_op jit(solution)/shard_map/ppermute | solution.py:27
  11.0 1.3 %collective-permute-done.9 = bf16[9,32,128]{2,1,0:T(8,128)(2,1)S(1)} collective-permute-done((bf16[9,32,128]{2,1,0:T(8,128)(2,1)S(1)}, bf16[9,32,128]{2,1,0:T(8,128)(2,1)S(1)}, u32[]{:S(2)}, u32[]{:S(2)}) %collective-permute-start.9) | collective-permute-done | bytes 73760 | tf_op jit(solution)/shard_map/ppermute | solution.py:27
  12.3 2.2 %collective-permute-start.11 = (bf16[18,32,128]{2,1,0:T(8,128)(2,1)S(1)}, bf16[18,32,128]{2,1,0:T(8,128)(2,1)S(1)}, u32[]{:S(2)}, u32[]{:S(2)}) collective-permute-start(bf16[18,32,128]{2,1,0:T(8,128)(2,1)S(1)} %constant_dynamic-update-slice_fusion.refs_9_), channel_id=1, source_target_pairs={{0,2},{1,15},{2,4},{3,1},{4,6},{5,3},{6,8},{7,5},{8,10},{9,7},{10,... | collective-permute-start | bytes 442376 | tf_op jit(solution)/shard_map/ppermute | solution.py:27
  14.5 1.7 %collective-permute-start.12 = (bf16[18,32,128]{2,1,0:T(8,128)(2,1)S(1)}, bf16[18,32,128]{2,1,0:T(8,128)(2,1)S(1)}, u32[]{:S(2)}, u32[]{:S(2)}) collective-permute-start(bf16[18,32,128]{2,1,0:T(8,128)(2,1)S(1)} %collective-permute-done.10.refs_10_), channel_id=1, source_target_pairs={{0,2},{1,15},{2,4},{3,1},{4,6},{5,3},{6,8},{7,5},{8,10},{9,7},{10,... | collective-permute-start | bytes 442376 | tf_op jit(solution)/shard_map/ppermute | solution.py:27
  16.6 3.1 %collective-permute-start.13 = (bf16[18,32,128]{2,1,0:T(8,128)(2,1)S(1)}, bf16[18,32,128]{2,1,0:T(8,128)(2,1)S(1)}, u32[]{:S(2)}, u32[]{:S(2)}) collective-permute-start(bf16[18,32,128]{2,1,0:T(8,128)(2,1)S(1)} %collective-permute-done.11.refs_11_), channel_id=1, source_target_pairs={{0,2},{1,15},{2,4},{3,1},{4,6},{5,3},{6,8},{7,5},{8,10},{9,7},{10,... | collective-permute-start | bytes 442376 | tf_op jit(solution)/shard_map/ppermute | solution.py:27
  19.7 1.3 %collective-permute-start = (bf16[1024,128]{1,0:T(8,128)(2,1)}, bf16[1024,128]{1,0:T(8,128)(2,1)S(1)}, u32[]{:S(2)}, u32[]{:S(2)}) collective-permute-start(bf16[1024,128]{1,0:T(8,128)(2,1)} %bitcast.7), channel_id=1, source_target_pairs={{0,32},{1,33},{2,34},{3,35},{4,36},{5,37},{6,38},{7,39},{8,40},{9,... | collective-permute-start | bytes 786440 | tf_op jit(solution)/shard_map/ppermute | solution.py:27
  21.0 2.5 %collective-permute-start.1 = (bf16[1024,128]{1,0:T(8,128)(2,1)}, bf16[1024,128]{1,0:T(8,128)(2,1)S(1)}, u32[]{:S(2)}, u32[]{:S(2)}) collective-permute-start(bf16[1024,128]{1,0:T(8,128)(2,1)} %bitcast.8), channel_id=1, source_target_pairs={{0,64},{1,193},{2,66},{3,195},{4,68},{5,197},{6,70},{7,199},{8,72}... | collective-permute-start | bytes 786440 | tf_op jit(solution)/shard_map/ppermute | solution.py:27
  23.5 1.8 %collective-permute-start.14 = (bf16[72,32,128]{2,1,0:T(8,128)(2,1)S(1)}, bf16[72,32,128]{2,1,0:T(8,128)(2,1)S(1)}, u32[]{:S(2)}, u32[]{:S(2)}) collective-permute-start(bf16[72,32,128]{2,1,0:T(8,128)(2,1)S(1)} %pad_maximum_fusion), channel_id=1, source_target_pairs={{0,1},{1,0},{2,3},{3,2},{4,5},{5,4},{6,7},{7,6},{8,9},{9,8},{10,11... | collective-permute-start | bytes 1769480 | tf_op jit(solution)/shard_map/ppermute | solution.py:27
  25.4 1.2 %collective-permute-start.2 = (bf16[1024,128]{1,0:T(8,128)(2,1)}, bf16[1024,128]{1,0:T(8,128)(2,1)S(1)}, u32[]{:S(2)}, u32[]{:S(2)}) collective-permute-start(bf16[1024,128]{1,0:T(8,128)(2,1)} %bitcast.9), channel_id=1, source_target_pairs={{0,192},{1,65},{2,194},{3,67},{4,196},{5,69},{6,198},{7,71},{8,200... | collective-permute-start | bytes 786440 | tf_op jit(solution)/shard_map/ppermute | solution.py:27
  27.6 1.2 %collective-permute-start.5 = (bf16[1024,128]{1,0:T(8,128)(2,1)S(1)}, bf16[1024,128]{1,0:T(8,128)(2,1)S(1)}, u32[]{:S(2)}, u32[]{:S(2)}) collective-permute-start(bf16[1024,128]{1,0:T(8,128)(2,1)S(1)} %collective-permute-done.refs_1_), channel_id=1, source_target_pairs={{0,192},{1,65},{2,194},{3,67},{4,196},{5,69},{6,198},{7,71},{8,200... | collective-permute-start | bytes 786440 | tf_op jit(solution)/shard_map/ppermute | solution.py:27
  28.8 2.3 %collective-permute-done.2.refs_3_ = bf16[1024,128]{1,0:T(8,128)(2,1)S(1)} collective-permute-done((bf16[1024,128]{1,0:T(8,128)(2,1)}, bf16[1024,128]{1,0:T(8,128)(2,1)S(1)}, u32[]{:S(2)}, u32[]{:S(2)}) %collective-permute-start.2) | collective-permute-done | bytes 262176 | tf_op jit(solution)/shard_map/ppermute | solution.py:27
  31.8 1.3 %collective-permute-done.15.a3 = bf16[18,32,128]{2,1,0:T(8,128)(2,1)S(1)} collective-permute-done((bf16[18,32,128]{2,1,0:T(8,128)(2,1)S(1)}, bf16[18,32,128]{2,1,0:T(8,128)(2,1)S(1)}, u32[]{:S(2)}, u32[]{:S(2)}) %collective-permute-start.15) | collective-permute-done | bytes 147488 | tf_op jit(solution)/shard_map/ppermute | solution.py:27
  33.1 1.8 %collective-permute-start.4 = (bf16[1024,128]{1,0:T(8,128)(2,1)S(1)}, bf16[1024,128]{1,0:T(8,128)(2,1)S(1)}, u32[]{:S(2)}, u32[]{:S(2)}) collective-permute-start(bf16[1024,128]{1,0:T(8,128)(2,1)S(1)} %collective-permute-done.2.refs_3_), channel_id=1, source_target_pairs={{0,64},{1,193},{2,66},{3,195},{4,68},{5,197},{6,70},{7,199},{8,72}... | collective-permute-start | bytes 786440 | tf_op jit(solution)/shard_map/ppermute | solution.py:27
  34.9 1.5 %collective-permute-start.6 = (bf16[1024,128]{1,0:T(8,128)(2,1)S(1)}, bf16[1024,128]{1,0:T(8,128)(2,1)S(1)}, u32[]{:S(2)}, u32[]{:S(2)}) collective-permute-start(bf16[1024,128]{1,0:T(8,128)(2,1)S(1)} %collective-permute-done.5.refs_6_), channel_id=1, source_target_pairs={{0,64},{1,193},{2,66},{3,195},{4,68},{5,197},{6,70},{7,199},{8,72}... | collective-permute-start | bytes 786440 | tf_op jit(solution)/shard_map/ppermute | solution.py:27
  36.4 2.7 %collective-permute-start.17 = (bf16[36,32,128]{2,1,0:T(8,128)(2,1)S(1)}, bf16[36,32,128]{2,1,0:T(8,128)(2,1)S(1)}, u32[]{:S(2)}, u32[]{:S(2)}) collective-permute-start(bf16[36,32,128]{2,1,0:T(8,128)(2,1)S(1)} %pad_maximum_fusion.1), channel_id=1, source_target_pairs={{0,1},{1,0},{2,3},{3,2},{4,5},{5,4},{6,7},{7,6},{8,9},{9,8},{10,11... | collective-permute-start | bytes 884744 | tf_op jit(solution)/shard_map/ppermute | solution.py:27
  39.5 1.2 %collective-permute-start.19 = (bf16[18,32,128]{2,1,0:T(8,128)(2,1)S(1)}, bf16[18,32,128]{2,1,0:T(8,128)(2,1)S(1)}, u32[]{:S(2)}, u32[]{:S(2)}) collective-permute-start(bf16[18,32,128]{2,1,0:T(8,128)(2,1)S(1)} %collective-permute-done.16.g3), channel_id=1, source_target_pairs={{0,2},{1,15},{2,4},{3,1},{4,6},{5,3},{6,8},{7,5},{8,10},{9,7},{10,... | collective-permute-start | bytes 442376 | tf_op jit(solution)/shard_map/ppermute | solution.py:27
  40.7 1.6 %collective-permute-done.6.refs_7_ = bf16[1024,128]{1,0:T(8,128)(2,1)S(1)} collective-permute-done((bf16[1024,128]{1,0:T(8,128)(2,1)S(1)}, bf16[1024,128]{1,0:T(8,128)(2,1)S(1)}, u32[]{:S(2)}, u32[]{:S(2)}) %collective-permute-start.6) | collective-permute-done | bytes 262176 | tf_op jit(solution)/shard_map/ppermute | solution.py:27
  42.3 2.3 %first.1 = (bf16[1024,1024]{1,0:T(8,128)(2,1)S(1)}, f32[3,1536,128]{2,1,0:T(8,128)S(1)}, f32[1,128]{1,0:T(1,128)S(1)}, f32[1,128]{1,0:T(1,128)S(1)}, f32[7,7,128]{2,1,0:T(8,128)S(1)}) custom-call(bf16[1024,128]{1,0:T(8,128)(2,1)S(1)} %bitcast.10, bf16[1024,128]{1,0:T(8,128)(2,1)S(1)} %collective-permute-done.refs_1_, ...), custom_call_target="tpu_custom_call" | custom-call | flops 1207959552 | bytes 4194304 | tf_op jit(solution)/shard_map/first/pallas_call | solution.py:315
  46.8 4.2 %collective-permute-start.20 = (bf16[4,256,128]{2,1,0:T(8,128)(2,1)S(1)}, bf16[4,256,128]{2,1,0:T(8,128)(2,1)S(1)}, u32[]{:S(2)}, u32[]{:S(2)}) collective-permute-start(bf16[4,256,128]{2,1,0:T(8,128)(2,1)S(1)} %get-tuple-element.19), channel_id=1, source_target_pairs={{0,1},{1,0},{2,3},{3,2},{4,5},{5,4},{6,7},{7,6},{8,9},{9,8},{10,11... | collective-permute-start | bytes 786440 | tf_op jit(solution)/shard_map/ppermute | solution.py:364
  51.0 1.9 %collective-permute-start.21 = (bf16[4,256,128]{2,1,0:T(8,128)(2,1)S(1)}, bf16[4,256,128]{2,1,0:T(8,128)(2,1)S(1)}, u32[]{:S(2)}, u32[]{:S(2)}) collective-permute-start(bf16[4,256,128]{2,1,0:T(8,128)(2,1)S(1)} %get-tuple-element.22), channel_id=1, source_target_pairs={{1,2},{3,4},{5,6},{7,8},{9,10},{11,12},{13,14},{15,16},{17,18},{19... | collective-permute-start | bytes 786440 | tf_op jit(solution)/shard_map/ppermute | solution.py:363
  54.1 4.5 %collective-permute-done.21.outer = bf16[4,256,128]{2,1,0:T(8,128)(2,1)S(1)} collective-permute-done((bf16[4,256,128]{2,1,0:T(8,128)(2,1)S(1)}, bf16[4,256,128]{2,1,0:T(8,128)(2,1)S(1)}, u32[]{:S(2)}, u32[]{:S(2)}) %collective-permute-start.21) | collective-permute-done | bytes 262176 | tf_op jit(solution)/shard_map/ppermute | solution.py:363
  58.7 1.6 %depth.3 = bf16[4,256,128]{2,1,0:T(8,128)(2,1)} custom-call(f32[4,256,128]{2,1,0:T(8,128)S(1)} %depth.2.part, f32[4,256,128]{2,1,0:T(8,128)S(1)} %get-tuple-element.17.own, bf16[4,256,128]{2,1,0:T(8,128)(2,1)S(1)} %collective-permute-done.21.outer, f32[1,128]{1,0:T(1,128)S(1)} %get-tuple-element.16.bias, f32[7,7,128]{2,1,0:T(8,128)S(1)} %get-tuple-element.21.weight), custom_call_target="tpu_custom_call" | custom-call | flops 32112640 | bytes 2097152 | tf_op jit(solution)/shard_map/depth/pallas_call | solution.py:371
  (34 shorter events, 6.8 us)
Async XLA Ops:
  0.0 4.4 %collective-permute-start.7 = (bf16[9,32,128]{2,1,0:T(8,128)(2,1)}, bf16[9,32,128]{2,1,0:T(8,128)(2,1)S(1)}, u32[]{:S(2)}, u32[]{:S(2)}) collective-permute-start(bf16[9,32,128]{2,1,0:T(8,128)(2,1)} %bitcast.4), channel_id=1, source_target_pairs={{0,1},{1,0},{2,3},{3,2},{4,5},{5,4},{6,7},{7,6},{8,9},{9,8},{10,11... | collective-permute-start | bytes 221192 | tf_op jit(solution)/shard_map/ppermute | solution.py:27
  3.2 7.8 %collective-permute-start.8 = (bf16[9,32,128]{2,1,0:T(8,128)(2,1)}, bf16[9,32,128]{2,1,0:T(8,128)(2,1)S(1)}, u32[]{:S(2)}, u32[]{:S(2)}) collective-permute-start(bf16[9,32,128]{2,1,0:T(8,128)(2,1)} %bitcast.5), channel_id=1, source_target_pairs={{0,16},{1,17},{2,18},{3,19},{4,20},{5,21},{6,22},{7,23},{8,24},{9,... | collective-permute-start | bytes 221192 | tf_op jit(solution)/shard_map/ppermute | solution.py:27
  4.4 0.9 %copy-start = (bf16[3,3,32,128]{3,2,1,0:T(8,128)(2,1)S(1)}, bf16[3,3,32,128]{3,2,1,0:T(8,128)(2,1)}, u32[]{:S(2)}) copy-start(bf16[3,3,32,128]{3,2,1,0:T(8,128)(2,1)} %param.6) | copy-start | bytes 221188
  5.3 37.0 %copy-start.1 = (bf16[4,256,128]{2,1,0:T(8,128)(2,1)S(1)}, bf16[4,256,128]{2,1,0:T(8,128)(2,1)}, u32[]{:S(2)}) copy-start(bf16[4,256,128]{2,1,0:T(8,128)(2,1)} %param.5) | copy-start | bytes 786436
  5.3 9.1 %collective-permute-start.10 = (bf16[18,32,128]{2,1,0:T(8,128)(2,1)S(1)}, bf16[18,32,128]{2,1,0:T(8,128)(2,1)S(1)}, u32[]{:S(2)}, u32[]{:S(2)}) collective-permute-start(bf16[18,32,128]{2,1,0:T(8,128)(2,1)S(1)} %pack.1.refs_8_), channel_id=1, source_target_pairs={{0,2},{1,15},{2,4},{3,1},{4,6},{5,3},{6,8},{7,5},{8,10},{9,7},{10,... | collective-permute-start | bytes 442376 | tf_op jit(solution)/shard_map/ppermute | solution.py:27
  11.0 1.3 %collective-permute-start.9 = (bf16[9,32,128]{2,1,0:T(8,128)(2,1)S(1)}, bf16[9,32,128]{2,1,0:T(8,128)(2,1)S(1)}, u32[]{:S(2)}, u32[]{:S(2)}) collective-permute-start(bf16[9,32,128]{2,1,0:T(8,128)(2,1)S(1)} %collective-permute-done.8), channel_id=1, source_target_pairs={{0,1},{1,0},{2,3},{3,2},{4,5},{5,4},{6,7},{7,6},{8,9},{9,8},{10,11... | collective-permute-start | bytes 221192 | tf_op jit(solution)/shard_map/ppermute | solution.py:27
  12.3 4.3 %collective-permute-start.11 = (bf16[18,32,128]{2,1,0:T(8,128)(2,1)S(1)}, bf16[18,32,128]{2,1,0:T(8,128)(2,1)S(1)}, u32[]{:S(2)}, u32[]{:S(2)}) collective-permute-start(bf16[18,32,128]{2,1,0:T(8,128)(2,1)S(1)} %constant_dynamic-update-slice_fusion.refs_9_), channel_id=1, source_target_pairs={{0,2},{1,15},{2,4},{3,1},{4,6},{5,3},{6,8},{7,5},{8,10},{9,7},{10,... | collective-permute-start | bytes 442376 | tf_op jit(solution)/shard_map/ppermute | solution.py:27
  14.5 9.0 %collective-permute-start.12 = (bf16[18,32,128]{2,1,0:T(8,128)(2,1)S(1)}, bf16[18,32,128]{2,1,0:T(8,128)(2,1)S(1)}, u32[]{:S(2)}, u32[]{:S(2)}) collective-permute-start(bf16[18,32,128]{2,1,0:T(8,128)(2,1)S(1)} %collective-permute-done.10.refs_10_), channel_id=1, source_target_pairs={{0,2},{1,15},{2,4},{3,1},{4,6},{5,3},{6,8},{7,5},{8,10},{9,7},{10,... | collective-permute-start | bytes 442376 | tf_op jit(solution)/shard_map/ppermute | solution.py:27
  16.6 6.9 %collective-permute-start.13 = (bf16[18,32,128]{2,1,0:T(8,128)(2,1)S(1)}, bf16[18,32,128]{2,1,0:T(8,128)(2,1)S(1)}, u32[]{:S(2)}, u32[]{:S(2)}) collective-permute-start(bf16[18,32,128]{2,1,0:T(8,128)(2,1)S(1)} %collective-permute-done.11.refs_11_), channel_id=1, source_target_pairs={{0,2},{1,15},{2,4},{3,1},{4,6},{5,3},{6,8},{7,5},{8,10},{9,7},{10,... | collective-permute-start | bytes 442376 | tf_op jit(solution)/shard_map/ppermute | solution.py:27
  19.7 7.9 %collective-permute-start = (bf16[1024,128]{1,0:T(8,128)(2,1)}, bf16[1024,128]{1,0:T(8,128)(2,1)S(1)}, u32[]{:S(2)}, u32[]{:S(2)}) collective-permute-start(bf16[1024,128]{1,0:T(8,128)(2,1)} %bitcast.7), channel_id=1, source_target_pairs={{0,32},{1,33},{2,34},{3,35},{4,36},{5,37},{6,38},{7,39},{8,40},{9,... | collective-permute-start | bytes 786440 | tf_op jit(solution)/shard_map/ppermute | solution.py:27
  21.0 7.8 %collective-permute-start.1 = (bf16[1024,128]{1,0:T(8,128)(2,1)}, bf16[1024,128]{1,0:T(8,128)(2,1)S(1)}, u32[]{:S(2)}, u32[]{:S(2)}) collective-permute-start(bf16[1024,128]{1,0:T(8,128)(2,1)} %bitcast.8), channel_id=1, source_target_pairs={{0,64},{1,193},{2,66},{3,195},{4,68},{5,197},{6,70},{7,199},{8,72}... | collective-permute-start | bytes 786440 | tf_op jit(solution)/shard_map/ppermute | solution.py:27
  23.5 18.8 %collective-permute-start.14 = (bf16[72,32,128]{2,1,0:T(8,128)(2,1)S(1)}, bf16[72,32,128]{2,1,0:T(8,128)(2,1)S(1)}, u32[]{:S(2)}, u32[]{:S(2)}) collective-permute-start(bf16[72,32,128]{2,1,0:T(8,128)(2,1)S(1)} %pad_maximum_fusion), channel_id=1, source_target_pairs={{0,1},{1,0},{2,3},{3,2},{4,5},{5,4},{6,7},{7,6},{8,9},{9,8},{10,11... | collective-permute-start | bytes 1769480 | tf_op jit(solution)/shard_map/ppermute | solution.py:27
  25.4 5.7 %collective-permute-start.2 = (bf16[1024,128]{1,0:T(8,128)(2,1)}, bf16[1024,128]{1,0:T(8,128)(2,1)S(1)}, u32[]{:S(2)}, u32[]{:S(2)}) collective-permute-start(bf16[1024,128]{1,0:T(8,128)(2,1)} %bitcast.9), channel_id=1, source_target_pairs={{0,192},{1,65},{2,194},{3,67},{4,196},{5,69},{6,198},{7,71},{8,200... | collective-permute-start | bytes 786440 | tf_op jit(solution)/shard_map/ppermute | solution.py:27
  27.6 7.3 %collective-permute-start.5 = (bf16[1024,128]{1,0:T(8,128)(2,1)S(1)}, bf16[1024,128]{1,0:T(8,128)(2,1)S(1)}, u32[]{:S(2)}, u32[]{:S(2)}) collective-permute-start(bf16[1024,128]{1,0:T(8,128)(2,1)S(1)} %collective-permute-done.refs_1_), channel_id=1, source_target_pairs={{0,192},{1,65},{2,194},{3,67},{4,196},{5,69},{6,198},{7,71},{8,200... | collective-permute-start | bytes 786440 | tf_op jit(solution)/shard_map/ppermute | solution.py:27
  28.8 4.3 %collective-permute-start.15 = (bf16[18,32,128]{2,1,0:T(8,128)(2,1)S(1)}, bf16[18,32,128]{2,1,0:T(8,128)(2,1)S(1)}, u32[]{:S(2)}, u32[]{:S(2)}) collective-permute-start(bf16[18,32,128]{2,1,0:T(8,128)(2,1)S(1)} %collective-permute-done.12.refs_12_.a2), channel_id=1, source_target_pairs={{0,2},{1,15},{2,4},{3,1},{4,6},{5,3},{6,8},{7,5},{8,10},{9,7},{10,... | collective-permute-start | bytes 442376 | tf_op jit(solution)/shard_map/ppermute | solution.py:27
  28.8 7.6 %collective-permute-start.16 = (bf16[18,32,128]{2,1,0:T(8,128)(2,1)S(1)}, bf16[18,32,128]{2,1,0:T(8,128)(2,1)S(1)}, u32[]{:S(2)}, u32[]{:S(2)}) collective-permute-start(bf16[18,32,128]{2,1,0:T(8,128)(2,1)S(1)} %collective-permute-done.13.refs_13_.g2), channel_id=1, source_target_pairs={{0,2},{1,15},{2,4},{3,1},{4,6},{5,3},{6,8},{7,5},{8,10},{9,7},{10,... | collective-permute-start | bytes 442376 | tf_op jit(solution)/shard_map/ppermute | solution.py:27
  31.1 8.1 %collective-permute-start.3 = (bf16[1024,128]{1,0:T(8,128)(2,1)S(1)}, bf16[1024,128]{1,0:T(8,128)(2,1)S(1)}, u32[]{:S(2)}, u32[]{:S(2)}) collective-permute-start(bf16[1024,128]{1,0:T(8,128)(2,1)S(1)} %collective-permute-done.1.refs_2_), channel_id=1, source_target_pairs={{0,32},{1,33},{2,34},{3,35},{4,36},{5,37},{6,38},{7,39},{8,40},{9,... | collective-permute-start | bytes 786440 | tf_op jit(solution)/shard_map/ppermute | solution.py:27
  33.1 6.4 %collective-permute-start.4 = (bf16[1024,128]{1,0:T(8,128)(2,1)S(1)}, bf16[1024,128]{1,0:T(8,128)(2,1)S(1)}, u32[]{:S(2)}, u32[]{:S(2)}) collective-permute-start(bf16[1024,128]{1,0:T(8,128)(2,1)S(1)} %collective-permute-done.2.refs_3_), channel_id=1, source_target_pairs={{0,64},{1,193},{2,66},{3,195},{4,68},{5,197},{6,70},{7,199},{8,72}... | collective-permute-start | bytes 786440 | tf_op jit(solution)/shard_map/ppermute | solution.py:27
  34.9 7.4 %collective-permute-start.6 = (bf16[1024,128]{1,0:T(8,128)(2,1)S(1)}, bf16[1024,128]{1,0:T(8,128)(2,1)S(1)}, u32[]{:S(2)}, u32[]{:S(2)}) collective-permute-start(bf16[1024,128]{1,0:T(8,128)(2,1)S(1)} %collective-permute-done.5.refs_6_), channel_id=1, source_target_pairs={{0,64},{1,193},{2,66},{3,195},{4,68},{5,197},{6,70},{7,199},{8,72}... | collective-permute-start | bytes 786440 | tf_op jit(solution)/shard_map/ppermute | solution.py:27
  36.4 8.2 %collective-permute-start.17 = (bf16[36,32,128]{2,1,0:T(8,128)(2,1)S(1)}, bf16[36,32,128]{2,1,0:T(8,128)(2,1)S(1)}, u32[]{:S(2)}, u32[]{:S(2)}) collective-permute-start(bf16[36,32,128]{2,1,0:T(8,128)(2,1)S(1)} %pad_maximum_fusion.1), channel_id=1, source_target_pairs={{0,1},{1,0},{2,3},{3,2},{4,5},{5,4},{6,7},{7,6},{8,9},{9,8},{10,11... | collective-permute-start | bytes 884744 | tf_op jit(solution)/shard_map/ppermute | solution.py:27
  39.2 6.4 %collective-permute-start.18 = (bf16[18,32,128]{2,1,0:T(8,128)(2,1)S(1)}, bf16[18,32,128]{2,1,0:T(8,128)(2,1)S(1)}, u32[]{:S(2)}, u32[]{:S(2)}) collective-permute-start(bf16[18,32,128]{2,1,0:T(8,128)(2,1)S(1)} %collective-permute-done.15.a3), channel_id=1, source_target_pairs={{0,2},{1,15},{2,4},{3,1},{4,6},{5,3},{6,8},{7,5},{8,10},{9,7},{10,... | collective-permute-start | bytes 442376 | tf_op jit(solution)/shard_map/ppermute | solution.py:27
  39.5 6.1 %collective-permute-start.19 = (bf16[18,32,128]{2,1,0:T(8,128)(2,1)S(1)}, bf16[18,32,128]{2,1,0:T(8,128)(2,1)S(1)}, u32[]{:S(2)}, u32[]{:S(2)}) collective-permute-start(bf16[18,32,128]{2,1,0:T(8,128)(2,1)S(1)} %collective-permute-done.16.g3), channel_id=1, source_target_pairs={{0,2},{1,15},{2,4},{3,1},{4,6},{5,3},{6,8},{7,5},{8,10},{9,7},{10,... | collective-permute-start | bytes 442376 | tf_op jit(solution)/shard_map/ppermute | solution.py:27
  46.8 6.1 %collective-permute-start.20 = (bf16[4,256,128]{2,1,0:T(8,128)(2,1)S(1)}, bf16[4,256,128]{2,1,0:T(8,128)(2,1)S(1)}, u32[]{:S(2)}, u32[]{:S(2)}) collective-permute-start(bf16[4,256,128]{2,1,0:T(8,128)(2,1)S(1)} %get-tuple-element.19), channel_id=1, source_target_pairs={{0,1},{1,0},{2,3},{3,2},{4,5},{5,4},{6,7},{7,6},{8,9},{9,8},{10,11... | collective-permute-start | bytes 786440 | tf_op jit(solution)/shard_map/ppermute | solution.py:364
  51.0 7.7 %collective-permute-start.21 = (bf16[4,256,128]{2,1,0:T(8,128)(2,1)S(1)}, bf16[4,256,128]{2,1,0:T(8,128)(2,1)S(1)}, u32[]{:S(2)}, u32[]{:S(2)}) collective-permute-start(bf16[4,256,128]{2,1,0:T(8,128)(2,1)S(1)} %get-tuple-element.22), channel_id=1, source_target_pairs={{1,2},{3,4},{5,6},{7,8},{9,10},{11,12},{13,14},{15,16},{17,18},{19... | collective-permute-start | bytes 786440 | tf_op jit(solution)/shard_map/ppermute | solution.py:363

commit v6 on v5

--- a/solution.py
+++ b/solution.py
@@ -189,7 +189,7 @@
         inner[3 - slot] = value
 
 
-def add_depth(rows, first, weight, hidden, begin, finish):
+def add_depth(rows, first, weight, hidden, begin, finish, after=None, sections=1):
     core = lax.axis_index("tile") % 2
     pad = jnp.zeros((len(rows), 8, CH), jnp.float32)
     hidden[:, 0:8, :] = pad
@@ -212,7 +212,11 @@
             finish(row, pl.ds(start, width), sums[row])
         return 0
 
-    lax.fori_loop(0, COLS // width, strip, 0)
+    steps = COLS // width // sections
+    for section in range(sections):
+        lax.fori_loop(section * steps, (section + 1) * steps, strip, 0, unroll=True)
+        if after is not None:
+            after(pl.ds(section * steps * width, steps * width))
 
 
 def activate(value, bias):
@@ -239,7 +243,7 @@
     )
 
 
-def depth_late_kernel(part, own, outer, bias, weight, out, hidden):
+def depth_late_kernel(part, own, outer, bias, weight, out, hidden, done, sems):
     f32 = jnp.float32
     tile = lax.axis_index("tile")
     core = tile % 2
@@ -250,11 +254,16 @@
         activate(outer[1].astype(f32) + own[0], bias) * inside,
         activate(own[1] + outer[0].astype(f32), bias),
     )
+    copies = Copies(sems)
 
     def finish(row, columns, value):
-        out[row + core * (3 - 2 * row), columns, :] = value.astype(jnp.bfloat16)
-
-    add_depth(rows, -3, weight, hidden, lambda row, columns: part[row, columns, :], finish)
+        done[row + core * (3 - 2 * row), columns, :] = value.astype(jnp.bfloat16)
+
+    def after(columns):
+        copies.start(done.at[:, columns, :], out.at[:, columns, :])
+
+    add_depth(rows, -3, weight, hidden, lambda row, columns: part[row, columns, :], finish, after, 2)
+    copies.wait()
 
 
 def pack_kernel(mine, others, both):
@@ -372,8 +381,9 @@
         kernel,
         out_shape=jax.ShapeDtypeStruct((ROWS, COLS, CH), dtype),
         in_specs=[vmem] * len(operands),
-        out_specs=vmem,
-        scratch_shapes=[pltpu.VMEM((rows, COLS + 16, CH), jnp.float32)],
+        out_specs=vmem if dtype == jnp.float32 else pl.BlockSpec(memory_space=pl.ANY),
+        scratch_shapes=[pltpu.VMEM((rows, COLS + 16, CH), jnp.float32)]
+        + ([] if dtype == jnp.float32 else [pltpu.VMEM((ROWS, COLS, CH), dtype), pltpu.SemaphoreType.DMA((2,))]),
         compiler_params=pltpu.CompilerParams(vmem_limit_bytes=20 << 20),
         cost_estimate=pl.CostEstimate(flops=5 * rows * COLS * 49 * CH, bytes_accessed=2 << 20, transcendentals=0),
         name="depth",

time: 61.3 us -> 61.2 us (level)
  no operation moved by 1% of the time
where the time goes in v6:
time: 61.2 us; the launch traced here: 60.2 us
  starting transfers between devices  39.2 us (64%)
  waiting for transfers between devices  12.7 us (21%)
  Pallas kernels  7.01 us (11%)
  local copies, waits for them, and re-layouts  0.94 us (2%)
    ppermute x20, starting transfers between devices, move(): return lax.ppermute(block, ('chan', 'tile'), pairs)  33.1 us
    ppermute x20, waiting for transfers between devices, move(): return lax.ppermute(block, ('chan', 'tile'), pairs)  8.16 us
    ppermute x1, waiting for transfers between devices, body(): lax.ppermute(outer, 'tile', across + [(j, i) for i, j in across])  4.58 us
    ppermute x1, starting transfers between devices, body(): from_inner = lax.ppermute(inner, 'tile', [(i, i ^ 1) for i in range(32)])  4.19 us
    pallas_call x2, Pallas kernels, depth(): pl.pallas_call(kernel, out_shape=jax.ShapeDtypeStruct((ROWS, COLS, CH), d...  2.56 us
    pallas_call x1, Pallas kernels, body(): pl.pallas_call(first_kernel, out_shape=(jax.ShapeDtypeStruct((PIX, 8 * CH...  2.3 us
    ppermute x1, starting transfers between devices, body(): lax.ppermute(outer, 'tile', across + [(j, i) for i, j in across])  1.91 us
  transfers between devices with their start and end apart: 22, of which 8 were waited for; matrix products, arithmetic and copies ran while one was open for 0% of the time, Pallas kernels for 7%

profile of v6, /device:TPU:1, one launch (start us, length us, event | category | flops | bytes accessed | tf_op | source)
XLA Modules:
  0.0 60.2 jit_solution(14252111819392260920)
XLA Ops:
  0.0 3.2 %collective-permute-start.7 = (bf16[9,32,128]{2,1,0:T(8,128)(2,1)}, bf16[9,32,128]{2,1,0:T(8,128)(2,1)S(1)}, u32[]{:S(2)}, u32[]{:S(2)}) collective-permute-start(bf16[9,32,128]{2,1,0:T(8,128)(2,1)} %bitcast.4), channel_id=1, source_target_pairs={{0,1},{1,0},{2,3},{3,2},{4,5},{5,4},{6,7},{7,6},{8,9},{9,8},{10,11... | collective-permute-start | bytes 221192 | tf_op jit(solution)/shard_map/ppermute | solution.py:27
  3.2 1.2 %collective-permute-start.8 = (bf16[9,32,128]{2,1,0:T(8,128)(2,1)}, bf16[9,32,128]{2,1,0:T(8,128)(2,1)S(1)}, u32[]{:S(2)}, u32[]{:S(2)}) collective-permute-start(bf16[9,32,128]{2,1,0:T(8,128)(2,1)} %bitcast.5), channel_id=1, source_target_pairs={{0,16},{1,17},{2,18},{3,19},{4,20},{5,21},{6,22},{7,23},{8,24},{9,... | collective-permute-start | bytes 221192 | tf_op jit(solution)/shard_map/ppermute | solution.py:27
  5.3 5.7 %collective-permute-start.10 = (bf16[18,32,128]{2,1,0:T(8,128)(2,1)S(1)}, bf16[18,32,128]{2,1,0:T(8,128)(2,1)S(1)}, u32[]{:S(2)}, u32[]{:S(2)}) collective-permute-start(bf16[18,32,128]{2,1,0:T(8,128)(2,1)S(1)} %pack.1.refs_8_), channel_id=1, source_target_pairs={{0,2},{1,15},{2,4},{3,1},{4,6},{5,3},{6,8},{7,5},{8,10},{9,7},{10,... | collective-permute-start | bytes 442376 | tf_op jit(solution)/shard_map/ppermute | solution.py:27
  11.0 1.3 %collective-permute-done.9 = bf16[9,32,128]{2,1,0:T(8,128)(2,1)S(1)} collective-permute-done((bf16[9,32,128]{2,1,0:T(8,128)(2,1)S(1)}, bf16[9,32,128]{2,1,0:T(8,128)(2,1)S(1)}, u32[]{:S(2)}, u32[]{:S(2)}) %collective-permute-start.9) | collective-permute-done | bytes 73760 | tf_op jit(solution)/shard_map/ppermute | solution.py:27
  12.3 2.2 %collective-permute-start.11 = (bf16[18,32,128]{2,1,0:T(8,128)(2,1)S(1)}, bf16[18,32,128]{2,1,0:T(8,128)(2,1)S(1)}, u32[]{:S(2)}, u32[]{:S(2)}) collective-permute-start(bf16[18,32,128]{2,1,0:T(8,128)(2,1)S(1)} %constant_dynamic-update-slice_fusion.refs_9_), channel_id=1, source_target_pairs={{0,2},{1,15},{2,4},{3,1},{4,6},{5,3},{6,8},{7,5},{8,10},{9,7},{10,... | collective-permute-start | bytes 442376 | tf_op jit(solution)/shard_map/ppermute | solution.py:27
  14.5 1.7 %collective-permute-start.12 = (bf16[18,32,128]{2,1,0:T(8,128)(2,1)S(1)}, bf16[18,32,128]{2,1,0:T(8,128)(2,1)S(1)}, u32[]{:S(2)}, u32[]{:S(2)}) collective-permute-start(bf16[18,32,128]{2,1,0:T(8,128)(2,1)S(1)} %collective-permute-done.10.refs_10_), channel_id=1, source_target_pairs={{0,2},{1,15},{2,4},{3,1},{4,6},{5,3},{6,8},{7,5},{8,10},{9,7},{10,... | collective-permute-start | bytes 442376 | tf_op jit(solution)/shard_map/ppermute | solution.py:27
  16.6 3.1 %collective-permute-start.13 = (bf16[18,32,128]{2,1,0:T(8,128)(2,1)S(1)}, bf16[18,32,128]{2,1,0:T(8,128)(2,1)S(1)}, u32[]{:S(2)}, u32[]{:S(2)}) collective-permute-start(bf16[18,32,128]{2,1,0:T(8,128)(2,1)S(1)} %collective-permute-done.11.refs_11_), channel_id=1, source_target_pairs={{0,2},{1,15},{2,4},{3,1},{4,6},{5,3},{6,8},{7,5},{8,10},{9,7},{10,... | collective-permute-start | bytes 442376 | tf_op jit(solution)/shard_map/ppermute | solution.py:27
  19.7 1.3 %collective-permute-start = (bf16[1024,128]{1,0:T(8,128)(2,1)}, bf16[1024,128]{1,0:T(8,128)(2,1)S(1)}, u32[]{:S(2)}, u32[]{:S(2)}) collective-permute-start(bf16[1024,128]{1,0:T(8,128)(2,1)} %bitcast.7), channel_id=1, source_target_pairs={{0,32},{1,33},{2,34},{3,35},{4,36},{5,37},{6,38},{7,39},{8,40},{9,... | collective-permute-start | bytes 786440 | tf_op jit(solution)/shard_map/ppermute | solution.py:27
  21.0 2.5 %collective-permute-start.1 = (bf16[1024,128]{1,0:T(8,128)(2,1)}, bf16[1024,128]{1,0:T(8,128)(2,1)S(1)}, u32[]{:S(2)}, u32[]{:S(2)}) collective-permute-start(bf16[1024,128]{1,0:T(8,128)(2,1)} %bitcast.8), channel_id=1, source_target_pairs={{0,64},{1,193},{2,66},{3,195},{4,68},{5,197},{6,70},{7,199},{8,72}... | collective-permute-start | bytes 786440 | tf_op jit(solution)/shard_map/ppermute | solution.py:27
  23.5 1.8 %collective-permute-start.14 = (bf16[72,32,128]{2,1,0:T(8,128)(2,1)S(1)}, bf16[72,32,128]{2,1,0:T(8,128)(2,1)S(1)}, u32[]{:S(2)}, u32[]{:S(2)}) collective-permute-start(bf16[72,32,128]{2,1,0:T(8,128)(2,1)S(1)} %pad_maximum_fusion), channel_id=1, source_target_pairs={{0,1},{1,0},{2,3},{3,2},{4,5},{5,4},{6,7},{7,6},{8,9},{9,8},{10,11... | collective-permute-start | bytes 1769480 | tf_op jit(solution)/shard_map/ppermute | solution.py:27
  25.4 1.2 %collective-permute-start.2 = (bf16[1024,128]{1,0:T(8,128)(2,1)}, bf16[1024,128]{1,0:T(8,128)(2,1)S(1)}, u32[]{:S(2)}, u32[]{:S(2)}) collective-permute-start(bf16[1024,128]{1,0:T(8,128)(2,1)} %bitcast.9), channel_id=1, source_target_pairs={{0,192},{1,65},{2,194},{3,67},{4,196},{5,69},{6,198},{7,71},{8,200... | collective-permute-start | bytes 786440 | tf_op jit(solution)/shard_map/ppermute | solution.py:27
  27.6 1.2 %collective-permute-start.5 = (bf16[1024,128]{1,0:T(8,128)(2,1)S(1)}, bf16[1024,128]{1,0:T(8,128)(2,1)S(1)}, u32[]{:S(2)}, u32[]{:S(2)}) collective-permute-start(bf16[1024,128]{1,0:T(8,128)(2,1)S(1)} %collective-permute-done.refs_1_), channel_id=1, source_target_pairs={{0,192},{1,65},{2,194},{3,67},{4,196},{5,69},{6,198},{7,71},{8,200... | collective-permute-start | bytes 786440 | tf_op jit(solution)/shard_map/ppermute | solution.py:27
  28.8 2.3 %collective-permute-done.2.refs_3_ = bf16[1024,128]{1,0:T(8,128)(2,1)S(1)} collective-permute-done((bf16[1024,128]{1,0:T(8,128)(2,1)}, bf16[1024,128]{1,0:T(8,128)(2,1)S(1)}, u32[]{:S(2)}, u32[]{:S(2)}) %collective-permute-start.2) | collective-permute-done | bytes 262176 | tf_op jit(solution)/shard_map/ppermute | solution.py:27
  31.8 1.3 %collective-permute-done.15.a3 = bf16[18,32,128]{2,1,0:T(8,128)(2,1)S(1)} collective-permute-done((bf16[18,32,128]{2,1,0:T(8,128)(2,1)S(1)}, bf16[18,32,128]{2,1,0:T(8,128)(2,1)S(1)}, u32[]{:S(2)}, u32[]{:S(2)}) %collective-permute-start.15) | collective-permute-done | bytes 147488 | tf_op jit(solution)/shard_map/ppermute | solution.py:27
  33.1 1.8 %collective-permute-start.4 = (bf16[1024,128]{1,0:T(8,128)(2,1)S(1)}, bf16[1024,128]{1,0:T(8,128)(2,1)S(1)}, u32[]{:S(2)}, u32[]{:S(2)}) collective-permute-start(bf16[1024,128]{1,0:T(8,128)(2,1)S(1)} %collective-permute-done.2.refs_3_), channel_id=1, source_target_pairs={{0,64},{1,193},{2,66},{3,195},{4,68},{5,197},{6,70},{7,199},{8,72}... | collective-permute-start | bytes 786440 | tf_op jit(solution)/shard_map/ppermute | solution.py:27
  34.9 1.5 %collective-permute-start.6 = (bf16[1024,128]{1,0:T(8,128)(2,1)S(1)}, bf16[1024,128]{1,0:T(8,128)(2,1)S(1)}, u32[]{:S(2)}, u32[]{:S(2)}) collective-permute-start(bf16[1024,128]{1,0:T(8,128)(2,1)S(1)} %collective-permute-done.5.refs_6_), channel_id=1, source_target_pairs={{0,64},{1,193},{2,66},{3,195},{4,68},{5,197},{6,70},{7,199},{8,72}... | collective-permute-start | bytes 786440 | tf_op jit(solution)/shard_map/ppermute | solution.py:27
  36.4 2.7 %collective-permute-start.17 = (bf16[36,32,128]{2,1,0:T(8,128)(2,1)S(1)}, bf16[36,32,128]{2,1,0:T(8,128)(2,1)S(1)}, u32[]{:S(2)}, u32[]{:S(2)}) collective-permute-start(bf16[36,32,128]{2,1,0:T(8,128)(2,1)S(1)} %pad_maximum_fusion.1), channel_id=1, source_target_pairs={{0,1},{1,0},{2,3},{3,2},{4,5},{5,4},{6,7},{7,6},{8,9},{9,8},{10,11... | collective-permute-start | bytes 884744 | tf_op jit(solution)/shard_map/ppermute | solution.py:27
  39.5 1.2 %collective-permute-start.19 = (bf16[18,32,128]{2,1,0:T(8,128)(2,1)S(1)}, bf16[18,32,128]{2,1,0:T(8,128)(2,1)S(1)}, u32[]{:S(2)}, u32[]{:S(2)}) collective-permute-start(bf16[18,32,128]{2,1,0:T(8,128)(2,1)S(1)} %collective-permute-done.16.g3), channel_id=1, source_target_pairs={{0,2},{1,15},{2,4},{3,1},{4,6},{5,3},{6,8},{7,5},{8,10},{9,7},{10,... | collective-permute-start | bytes 442376 | tf_op jit(solution)/shard_map/ppermute | solution.py:27
  40.7 1.6 %collective-permute-done.6.refs_7_ = bf16[1024,128]{1,0:T(8,128)(2,1)S(1)} collective-permute-done((bf16[1024,128]{1,0:T(8,128)(2,1)S(1)}, bf16[1024,128]{1,0:T(8,128)(2,1)S(1)}, u32[]{:S(2)}, u32[]{:S(2)}) %collective-permute-start.6) | collective-permute-done | bytes 262176 | tf_op jit(solution)/shard_map/ppermute | solution.py:27
  42.3 2.3 %first.1 = (bf16[1024,1024]{1,0:T(8,128)(2,1)S(1)}, f32[3,1536,128]{2,1,0:T(8,128)S(1)}, f32[1,128]{1,0:T(1,128)S(1)}, f32[1,128]{1,0:T(1,128)S(1)}, f32[7,7,128]{2,1,0:T(8,128)S(1)}) custom-call(bf16[1024,128]{1,0:T(8,128)(2,1)S(1)} %bitcast.10, bf16[1024,128]{1,0:T(8,128)(2,1)S(1)} %collective-permute-done.refs_1_, ...), custom_call_target="tpu_custom_call" | custom-call | flops 1207959552 | bytes 4194304 | tf_op jit(solution)/shard_map/first/pallas_call | solution.py:324
  46.8 4.2 %collective-permute-start.20 = (bf16[4,256,128]{2,1,0:T(8,128)(2,1)S(1)}, bf16[4,256,128]{2,1,0:T(8,128)(2,1)S(1)}, u32[]{:S(2)}, u32[]{:S(2)}) collective-permute-start(bf16[4,256,128]{2,1,0:T(8,128)(2,1)S(1)} %get-tuple-element.19), channel_id=1, source_target_pairs={{0,1},{1,0},{2,3},{3,2},{4,5},{5,4},{6,7},{7,6},{8,9},{9,8},{10,11... | collective-permute-start | bytes 786440 | tf_op jit(solution)/shard_map/ppermute | solution.py:373
  51.0 1.9 %collective-permute-start.21 = (bf16[4,256,128]{2,1,0:T(8,128)(2,1)S(1)}, bf16[4,256,128]{2,1,0:T(8,128)(2,1)S(1)}, u32[]{:S(2)}, u32[]{:S(2)}) collective-permute-start(bf16[4,256,128]{2,1,0:T(8,128)(2,1)S(1)} %get-tuple-element.22), channel_id=1, source_target_pairs={{1,2},{3,4},{5,6},{7,8},{9,10},{11,12},{13,14},{15,16},{17,18},{19... | collective-permute-start | bytes 786440 | tf_op jit(solution)/shard_map/ppermute | solution.py:372
  54.1 4.6 %collective-permute-done.21.outer = bf16[4,256,128]{2,1,0:T(8,128)(2,1)S(1)} collective-permute-done((bf16[4,256,128]{2,1,0:T(8,128)(2,1)S(1)}, bf16[4,256,128]{2,1,0:T(8,128)(2,1)S(1)}, u32[]{:S(2)}, u32[]{:S(2)}) %collective-permute-start.21) | collective-permute-done | bytes 262176 | tf_op jit(solution)/shard_map/ppermute | solution.py:372
  58.7 1.4 %depth.3 = bf16[4,256,128]{2,1,0:T(8,128)(2,1)} custom-call(f32[4,256,128]{2,1,0:T(8,128)S(1)} %depth.2.part, f32[4,256,128]{2,1,0:T(8,128)S(1)} %get-tuple-element.17.own, bf16[4,256,128]{2,1,0:T(8,128)(2,1)S(1)} %collective-permute-done.21.outer, f32[1,128]{1,0:T(1,128)S(1)} %get-tuple-element.16.bias, f32[7,7,128]{2,1,0:T(8,128)S(1)} %get-tuple-element.21.weight), custom_call_target="tpu_custom_call" | custom-call | flops 32112640 | bytes 2097152 | tf_op jit(solution)/shard_map/depth/pallas_call | solution.py:380
  (34 shorter events, 6.7 us)
Async XLA Ops:
  0.0 4.4 %collective-permute-start.7 = (bf16[9,32,128]{2,1,0:T(8,128)(2,1)}, bf16[9,32,128]{2,1,0:T(8,128)(2,1)S(1)}, u32[]{:S(2)}, u32[]{:S(2)}) collective-permute-start(bf16[9,32,128]{2,1,0:T(8,128)(2,1)} %bitcast.4), channel_id=1, source_target_pairs={{0,1},{1,0},{2,3},{3,2},{4,5},{5,4},{6,7},{7,6},{8,9},{9,8},{10,11... | collective-permute-start | bytes 221192 | tf_op jit(solution)/shard_map/ppermute | solution.py:27
  3.2 7.8 %collective-permute-start.8 = (bf16[9,32,128]{2,1,0:T(8,128)(2,1)}, bf16[9,32,128]{2,1,0:T(8,128)(2,1)S(1)}, u32[]{:S(2)}, u32[]{:S(2)}) collective-permute-start(bf16[9,32,128]{2,1,0:T(8,128)(2,1)} %bitcast.5), channel_id=1, source_target_pairs={{0,16},{1,17},{2,18},{3,19},{4,20},{5,21},{6,22},{7,23},{8,24},{9,... | collective-permute-start | bytes 221192 | tf_op jit(solution)/shard_map/ppermute | solution.py:27
  4.4 0.9 %copy-start = (bf16[3,3,32,128]{3,2,1,0:T(8,128)(2,1)S(1)}, bf16[3,3,32,128]{3,2,1,0:T(8,128)(2,1)}, u32[]{:S(2)}) copy-start(bf16[3,3,32,128]{3,2,1,0:T(8,128)(2,1)} %param.6) | copy-start | bytes 221188
  5.3 37.0 %copy-start.1 = (bf16[4,256,128]{2,1,0:T(8,128)(2,1)S(1)}, bf16[4,256,128]{2,1,0:T(8,128)(2,1)}, u32[]{:S(2)}) copy-start(bf16[4,256,128]{2,1,0:T(8,128)(2,1)} %param.5) | copy-start | bytes 786436
  5.3 9.1 %collective-permute-start.10 = (bf16[18,32,128]{2,1,0:T(8,128)(2,1)S(1)}, bf16[18,32,128]{2,1,0:T(8,128)(2,1)S(1)}, u32[]{:S(2)}, u32[]{:S(2)}) collective-permute-start(bf16[18,32,128]{2,1,0:T(8,128)(2,1)S(1)} %pack.1.refs_8_), channel_id=1, source_target_pairs={{0,2},{1,15},{2,4},{3,1},{4,6},{5,3},{6,8},{7,5},{8,10},{9,7},{10,... | collective-permute-start | bytes 442376 | tf_op jit(solution)/shard_map/ppermute | solution.py:27
  11.0 1.3 %collective-permute-start.9 = (bf16[9,32,128]{2,1,0:T(8,128)(2,1)S(1)}, bf16[9,32,128]{2,1,0:T(8,128)(2,1)S(1)}, u32[]{:S(2)}, u32[]{:S(2)}) collective-permute-start(bf16[9,32,128]{2,1,0:T(8,128)(2,1)S(1)} %collective-permute-done.8), channel_id=1, source_target_pairs={{0,1},{1,0},{2,3},{3,2},{4,5},{5,4},{6,7},{7,6},{8,9},{9,8},{10,11... | collective-permute-start | bytes 221192 | tf_op jit(solution)/shard_map/ppermute | solution.py:27
  12.3 4.3 %collective-permute-start.11 = (bf16[18,32,128]{2,1,0:T(8,128)(2,1)S(1)}, bf16[18,32,128]{2,1,0:T(8,128)(2,1)S(1)}, u32[]{:S(2)}, u32[]{:S(2)}) collective-permute-start(bf16[18,32,128]{2,1,0:T(8,128)(2,1)S(1)} %constant_dynamic-update-slice_fusion.refs_9_), channel_id=1, source_target_pairs={{0,2},{1,15},{2,4},{3,1},{4,6},{5,3},{6,8},{7,5},{8,10},{9,7},{10,... | collective-permute-start | bytes 442376 | tf_op jit(solution)/shard_map/ppermute | solution.py:27
  14.5 9.0 %collective-permute-start.12 = (bf16[18,32,128]{2,1,0:T(8,128)(2,1)S(1)}, bf16[18,32,128]{2,1,0:T(8,128)(2,1)S(1)}, u32[]{:S(2)}, u32[]{:S(2)}) collective-permute-start(bf16[18,32,128]{2,1,0:T(8,128)(2,1)S(1)} %collective-permute-done.10.refs_10_), channel_id=1, source_target_pairs={{0,2},{1,15},{2,4},{3,1},{4,6},{5,3},{6,8},{7,5},{8,10},{9,7},{10,... | collective-permute-start | bytes 442376 | tf_op jit(solution)/shard_map/ppermute | solution.py:27
  16.6 6.9 %collective-permute-start.13 = (bf16[18,32,128]{2,1,0:T(8,128)(2,1)S(1)}, bf16[18,32,128]{2,1,0:T(8,128)(2,1)S(1)}, u32[]{:S(2)}, u32[]{:S(2)}) collective-permute-start(bf16[18,32,128]{2,1,0:T(8,128)(2,1)S(1)} %collective-permute-done.11.refs_11_), channel_id=1, source_target_pairs={{0,2},{1,15},{2,4},{3,1},{4,6},{5,3},{6,8},{7,5},{8,10},{9,7},{10,... | collective-permute-start | bytes 442376 | tf_op jit(solution)/shard_map/ppermute | solution.py:27
  19.7 7.9 %collective-permute-start = (bf16[1024,128]{1,0:T(8,128)(2,1)}, bf16[1024,128]{1,0:T(8,128)(2,1)S(1)}, u32[]{:S(2)}, u32[]{:S(2)}) collective-permute-start(bf16[1024,128]{1,0:T(8,128)(2,1)} %bitcast.7), channel_id=1, source_target_pairs={{0,32},{1,33},{2,34},{3,35},{4,36},{5,37},{6,38},{7,39},{8,40},{9,... | collective-permute-start | bytes 786440 | tf_op jit(solution)/shard_map/ppermute | solution.py:27
  21.0 7.8 %collective-permute-start.1 = (bf16[1024,128]{1,0:T(8,128)(2,1)}, bf16[1024,128]{1,0:T(8,128)(2,1)S(1)}, u32[]{:S(2)}, u32[]{:S(2)}) collective-permute-start(bf16[1024,128]{1,0:T(8,128)(2,1)} %bitcast.8), channel_id=1, source_target_pairs={{0,64},{1,193},{2,66},{3,195},{4,68},{5,197},{6,70},{7,199},{8,72}... | collective-permute-start | bytes 786440 | tf_op jit(solution)/shard_map/ppermute | solution.py:27
  23.5 18.8 %collective-permute-start.14 = (bf16[72,32,128]{2,1,0:T(8,128)(2,1)S(1)}, bf16[72,32,128]{2,1,0:T(8,128)(2,1)S(1)}, u32[]{:S(2)}, u32[]{:S(2)}) collective-permute-start(bf16[72,32,128]{2,1,0:T(8,128)(2,1)S(1)} %pad_maximum_fusion), channel_id=1, source_target_pairs={{0,1},{1,0},{2,3},{3,2},{4,5},{5,4},{6,7},{7,6},{8,9},{9,8},{10,11... | collective-permute-start | bytes 1769480 | tf_op jit(solution)/shard_map/ppermute | solution.py:27
  25.4 5.7 %collective-permute-start.2 = (bf16[1024,128]{1,0:T(8,128)(2,1)}, bf16[1024,128]{1,0:T(8,128)(2,1)S(1)}, u32[]{:S(2)}, u32[]{:S(2)}) collective-permute-start(bf16[1024,128]{1,0:T(8,128)(2,1)} %bitcast.9), channel_id=1, source_target_pairs={{0,192},{1,65},{2,194},{3,67},{4,196},{5,69},{6,198},{7,71},{8,200... | collective-permute-start | bytes 786440 | tf_op jit(solution)/shard_map/ppermute | solution.py:27
  27.6 7.3 %collective-permute-start.5 = (bf16[1024,128]{1,0:T(8,128)(2,1)S(1)}, bf16[1024,128]{1,0:T(8,128)(2,1)S(1)}, u32[]{:S(2)}, u32[]{:S(2)}) collective-permute-start(bf16[1024,128]{1,0:T(8,128)(2,1)S(1)} %collective-permute-done.refs_1_), channel_id=1, source_target_pairs={{0,192},{1,65},{2,194},{3,67},{4,196},{5,69},{6,198},{7,71},{8,200... | collective-permute-start | bytes 786440 | tf_op jit(solution)/shard_map/ppermute | solution.py:27
  28.8 4.3 %collective-permute-start.15 = (bf16[18,32,128]{2,1,0:T(8,128)(2,1)S(1)}, bf16[18,32,128]{2,1,0:T(8,128)(2,1)S(1)}, u32[]{:S(2)}, u32[]{:S(2)}) collective-permute-start(bf16[18,32,128]{2,1,0:T(8,128)(2,1)S(1)} %collective-permute-done.12.refs_12_.a2), channel_id=1, source_target_pairs={{0,2},{1,15},{2,4},{3,1},{4,6},{5,3},{6,8},{7,5},{8,10},{9,7},{10,... | collective-permute-start | bytes 442376 | tf_op jit(solution)/shard_map/ppermute | solution.py:27
  28.8 7.6 %collective-permute-start.16 = (bf16[18,32,128]{2,1,0:T(8,128)(2,1)S(1)}, bf16[18,32,128]{2,1,0:T(8,128)(2,1)S(1)}, u32[]{:S(2)}, u32[]{:S(2)}) collective-permute-start(bf16[18,32,128]{2,1,0:T(8,128)(2,1)S(1)} %collective-permute-done.13.refs_13_.g2), channel_id=1, source_target_pairs={{0,2},{1,15},{2,4},{3,1},{4,6},{5,3},{6,8},{7,5},{8,10},{9,7},{10,... | collective-permute-start | bytes 442376 | tf_op jit(solution)/shard_map/ppermute | solution.py:27
  31.1 8.1 %collective-permute-start.3 = (bf16[1024,128]{1,0:T(8,128)(2,1)S(1)}, bf16[1024,128]{1,0:T(8,128)(2,1)S(1)}, u32[]{:S(2)}, u32[]{:S(2)}) collective-permute-start(bf16[1024,128]{1,0:T(8,128)(2,1)S(1)} %collective-permute-done.1.refs_2_), channel_id=1, source_target_pairs={{0,32},{1,33},{2,34},{3,35},{4,36},{5,37},{6,38},{7,39},{8,40},{9,... | collective-permute-start | bytes 786440 | tf_op jit(solution)/shard_map/ppermute | solution.py:27
  33.1 6.4 %collective-permute-start.4 = (bf16[1024,128]{1,0:T(8,128)(2,1)S(1)}, bf16[1024,128]{1,0:T(8,128)(2,1)S(1)}, u32[]{:S(2)}, u32[]{:S(2)}) collective-permute-start(bf16[1024,128]{1,0:T(8,128)(2,1)S(1)} %collective-permute-done.2.refs_3_), channel_id=1, source_target_pairs={{0,64},{1,193},{2,66},{3,195},{4,68},{5,197},{6,70},{7,199},{8,72}... | collective-permute-start | bytes 786440 | tf_op jit(solution)/shard_map/ppermute | solution.py:27
  34.9 7.4 %collective-permute-start.6 = (bf16[1024,128]{1,0:T(8,128)(2,1)S(1)}, bf16[1024,128]{1,0:T(8,128)(2,1)S(1)}, u32[]{:S(2)}, u32[]{:S(2)}) collective-permute-start(bf16[1024,128]{1,0:T(8,128)(2,1)S(1)} %collective-permute-done.5.refs_6_), channel_id=1, source_target_pairs={{0,64},{1,193},{2,66},{3,195},{4,68},{5,197},{6,70},{7,199},{8,72}... | collective-permute-start | bytes 786440 | tf_op jit(solution)/shard_map/ppermute | solution.py:27
  36.4 8.2 %collective-permute-start.17 = (bf16[36,32,128]{2,1,0:T(8,128)(2,1)S(1)}, bf16[36,32,128]{2,1,0:T(8,128)(2,1)S(1)}, u32[]{:S(2)}, u32[]{:S(2)}) collective-permute-start(bf16[36,32,128]{2,1,0:T(8,128)(2,1)S(1)} %pad_maximum_fusion.1), channel_id=1, source_target_pairs={{0,1},{1,0},{2,3},{3,2},{4,5},{5,4},{6,7},{7,6},{8,9},{9,8},{10,11... | collective-permute-start | bytes 884744 | tf_op jit(solution)/shard_map/ppermute | solution.py:27
  39.2 6.4 %collective-permute-start.18 = (bf16[18,32,128]{2,1,0:T(8,128)(2,1)S(1)}, bf16[18,32,128]{2,1,0:T(8,128)(2,1)S(1)}, u32[]{:S(2)}, u32[]{:S(2)}) collective-permute-start(bf16[18,32,128]{2,1,0:T(8,128)(2,1)S(1)} %collective-permute-done.15.a3), channel_id=1, source_target_pairs={{0,2},{1,15},{2,4},{3,1},{4,6},{5,3},{6,8},{7,5},{8,10},{9,7},{10,... | collective-permute-start | bytes 442376 | tf_op jit(solution)/shard_map/ppermute | solution.py:27
  39.5 6.1 %collective-permute-start.19 = (bf16[18,32,128]{2,1,0:T(8,128)(2,1)S(1)}, bf16[18,32,128]{2,1,0:T(8,128)(2,1)S(1)}, u32[]{:S(2)}, u32[]{:S(2)}) collective-permute-start(bf16[18,32,128]{2,1,0:T(8,128)(2,1)S(1)} %collective-permute-done.16.g3), channel_id=1, source_target_pairs={{0,2},{1,15},{2,4},{3,1},{4,6},{5,3},{6,8},{7,5},{8,10},{9,7},{10,... | collective-permute-start | bytes 442376 | tf_op jit(solution)/shard_map/ppermute | solution.py:27
  46.8 6.1 %collective-permute-start.20 = (bf16[4,256,128]{2,1,0:T(8,128)(2,1)S(1)}, bf16[4,256,128]{2,1,0:T(8,128)(2,1)S(1)}, u32[]{:S(2)}, u32[]{:S(2)}) collective-permute-start(bf16[4,256,128]{2,1,0:T(8,128)(2,1)S(1)} %get-tuple-element.19), channel_id=1, source_target_pairs={{0,1},{1,0},{2,3},{3,2},{4,5},{5,4},{6,7},{7,6},{8,9},{9,8},{10,11... | collective-permute-start | bytes 786440 | tf_op jit(solution)/shard_map/ppermute | solution.py:373
  51.0 7.7 %collective-permute-start.21 = (bf16[4,256,128]{2,1,0:T(8,128)(2,1)S(1)}, bf16[4,256,128]{2,1,0:T(8,128)(2,1)S(1)}, u32[]{:S(2)}, u32[]{:S(2)}) collective-permute-start(bf16[4,256,128]{2,1,0:T(8,128)(2,1)S(1)} %get-tuple-element.22), channel_id=1, source_target_pairs={{1,2},{3,4},{5,6},{7,8},{9,10},{11,12},{13,14},{15,16},{17,18},{19... | collective-permute-start | bytes 786440 | tf_op jit(solution)/shard_map/ppermute | solution.py:372

commit v7 on v5

--- a/solution.py
+++ b/solution.py
@@ -48,7 +48,7 @@
 
 
 def to_next(x, y, hi, z, core):
-    return x, y, hi, (z - 1 if core else z + 1), core
+    return x, y, hi, (z + 1 if core else z - 1), core
 
 
 TAPS = (((0, 0), (0, 1)), ((0, 2), (2, 0)), ((2, 1), (2, 2)), ((1, 0), (1, 1)), ((1, 2),))
@@ -99,7 +99,7 @@
         self.target = target
         tile = lax.axis_index("tile")
         self.y_hi, self.z, self.core = tile // 16, (tile // 2) % 8, tile % 2
-        self.partner_back = (self.core + self.z) % 2 == 1
+        self.partner_back = (self.core + self.z) % 2 == 0
 
     def place(self, arrays, odd, first, core):
         for piece in range(4):
@@ -212,7 +212,7 @@
             finish(row, pl.ds(start, width), sums[row])
         return 0
 
-    lax.fori_loop(0, COLS // width, strip, 0)
+    lax.fori_loop(0, COLS // width, strip, 0, unroll=True)
 
 
 def activate(value, bias):

time: 61.3 us -> 61.1 us (level)
  the two profiles are of different devices: /device:TPU:1 before, /device:TPU:24 now
where the time goes in v7:
time: 61.1 us; the launch traced here: 60.9 us
  starting transfers between devices  37.7 us (62%)
  waiting for transfers between devices  15.1 us (25%)
  Pallas kernels  7.01 us (11%)
  local copies, waits for them, and re-layouts  0.91 us (1%)
    ppermute x20, starting transfers between devices, move(): return lax.ppermute(block, ('chan', 'tile'), pairs)  32.7 us
    ppermute x20, waiting for transfers between devices, move(): return lax.ppermute(block, ('chan', 'tile'), pairs)  9.92 us
    ppermute x1, waiting for transfers between devices, body(): lax.ppermute(outer, 'tile', across + [(j, i) for i, j in across])  5.2 us
    ppermute x1, starting transfers between devices, body(): lax.ppermute(outer, 'tile', across + [(j, i) for i, j in across])  4.94 us
    pallas_call x2, Pallas kernels, depth(): pl.pallas_call(kernel, out_shape=jax.ShapeDtypeStruct((ROWS, COLS, CH), d...  2.55 us
    pallas_call x1, Pallas kernels, body(): pl.pallas_call(first_kernel, out_shape=(jax.ShapeDtypeStruct((PIX, 8 * CH...  2.3 us
  transfers between devices with their start and end apart: 22, of which 9 were waited for; matrix products, arithmetic and copies ran while one was open for 0% of the time, Pallas kernels for 7%

profile of v7, /device:TPU:24, one launch (start us, length us, event | category | flops | bytes accessed | tf_op | source)
XLA Modules:
  0.0 60.9 jit_solution(3841771385259411435)
XLA Ops:
  0.0 1.2 %collective-permute-start.8 = (bf16[9,32,128]{2,1,0:T(8,128)(2,1)}, bf16[9,32,128]{2,1,0:T(8,128)(2,1)S(1)}, u32[]{:S(2)}, u32[]{:S(2)}) collective-permute-start(bf16[9,32,128]{2,1,0:T(8,128)(2,1)} %bitcast.5), channel_id=1, source_target_pairs={{0,16},{1,17},{2,18},{3,19},{4,20},{5,21},{6,22},{7,23},{8,24},{9,... | collective-permute-start | bytes 221192 | tf_op jit(solution)/shard_map/ppermute | solution.py:27
  1.5 0.9 %copy-done = bf16[3,3,32,128]{3,2,1,0:T(8,128)(2,1)S(1)} copy-done((bf16[3,3,32,128]{3,2,1,0:T(8,128)(2,1)S(1)}, bf16[3,3,32,128]{3,2,1,0:T(8,128)(2,1)}, u32[]{:S(2)}) %copy-start) | copy-done | bytes 73752
  2.4 5.9 %collective-permute-start.10 = (bf16[18,32,128]{2,1,0:T(8,128)(2,1)S(1)}, bf16[18,32,128]{2,1,0:T(8,128)(2,1)S(1)}, u32[]{:S(2)}, u32[]{:S(2)}) collective-permute-start(bf16[18,32,128]{2,1,0:T(8,128)(2,1)S(1)} %pack.1.refs_8_), channel_id=1, source_target_pairs={{0,14},{1,3},{2,0},{3,5},{4,2},{5,7},{6,4},{7,9},{8,6},{9,11},{10,... | collective-permute-start | bytes 442376 | tf_op jit(solution)/shard_map/ppermute | solution.py:27
  8.3 1.3 %collective-permute-done.9 = bf16[9,32,128]{2,1,0:T(8,128)(2,1)S(1)} collective-permute-done((bf16[9,32,128]{2,1,0:T(8,128)(2,1)S(1)}, bf16[9,32,128]{2,1,0:T(8,128)(2,1)S(1)}, u32[]{:S(2)}, u32[]{:S(2)}) %collective-permute-start.9) | collective-permute-done | bytes 73760 | tf_op jit(solution)/shard_map/ppermute | solution.py:27
  9.6 4.0 %collective-permute-start.11 = (bf16[18,32,128]{2,1,0:T(8,128)(2,1)S(1)}, bf16[18,32,128]{2,1,0:T(8,128)(2,1)S(1)}, u32[]{:S(2)}, u32[]{:S(2)}) collective-permute-start(bf16[18,32,128]{2,1,0:T(8,128)(2,1)S(1)} %constant_dynamic-update-slice_fusion.refs_9_), channel_id=1, source_target_pairs={{0,14},{1,3},{2,0},{3,5},{4,2},{5,7},{6,4},{7,9},{8,6},{9,11},{10,... | collective-permute-start | bytes 442376 | tf_op jit(solution)/shard_map/ppermute | solution.py:27
  13.6 1.0 %collective-permute-start.12 = (bf16[18,32,128]{2,1,0:T(8,128)(2,1)S(1)}, bf16[18,32,128]{2,1,0:T(8,128)(2,1)S(1)}, u32[]{:S(2)}, u32[]{:S(2)}) collective-permute-start(bf16[18,32,128]{2,1,0:T(8,128)(2,1)S(1)} %collective-permute-done.10.refs_10_), channel_id=1, source_target_pairs={{0,14},{1,3},{2,0},{3,5},{4,2},{5,7},{6,4},{7,9},{8,6},{9,11},{10,... | collective-permute-start | bytes 442376 | tf_op jit(solution)/shard_map/ppermute | solution.py:27
  14.7 1.6 %collective-permute-done.11.refs_11_ = bf16[18,32,128]{2,1,0:T(8,128)(2,1)S(1)} collective-permute-done((bf16[18,32,128]{2,1,0:T(8,128)(2,1)S(1)}, bf16[18,32,128]{2,1,0:T(8,128)(2,1)S(1)}, u32[]{:S(2)}, u32[]{:S(2)}) %collective-permute-start.11) | collective-permute-done | bytes 147488 | tf_op jit(solution)/shard_map/ppermute | solution.py:27
  16.3 3.7 %collective-permute-start.13 = (bf16[18,32,128]{2,1,0:T(8,128)(2,1)S(1)}, bf16[18,32,128]{2,1,0:T(8,128)(2,1)S(1)}, u32[]{:S(2)}, u32[]{:S(2)}) collective-permute-start(bf16[18,32,128]{2,1,0:T(8,128)(2,1)S(1)} %collective-permute-done.11.refs_11_), channel_id=1, source_target_pairs={{0,14},{1,3},{2,0},{3,5},{4,2},{5,7},{6,4},{7,9},{8,6},{9,11},{10,... | collective-permute-start | bytes 442376 | tf_op jit(solution)/shard_map/ppermute | solution.py:27
  20.7 1.5 %collective-permute-start.1 = (bf16[1024,128]{1,0:T(8,128)(2,1)}, bf16[1024,128]{1,0:T(8,128)(2,1)S(1)}, u32[]{:S(2)}, u32[]{:S(2)}) collective-permute-start(bf16[1024,128]{1,0:T(8,128)(2,1)} %bitcast.8), channel_id=1, source_target_pairs={{0,64},{1,193},{2,66},{3,195},{4,68},{5,197},{6,70},{7,199},{8,72}... | collective-permute-start | bytes 786440 | tf_op jit(solution)/shard_map/ppermute | solution.py:27
  22.8 2.8 %collective-permute-start.2 = (bf16[1024,128]{1,0:T(8,128)(2,1)}, bf16[1024,128]{1,0:T(8,128)(2,1)S(1)}, u32[]{:S(2)}, u32[]{:S(2)}) collective-permute-start(bf16[1024,128]{1,0:T(8,128)(2,1)} %bitcast.9), channel_id=1, source_target_pairs={{0,192},{1,65},{2,194},{3,67},{4,196},{5,69},{6,198},{7,71},{8,200... | collective-permute-start | bytes 786440 | tf_op jit(solution)/shard_map/ppermute | solution.py:27
  25.7 0.9 %collective-permute-done.refs_1_ = bf16[1024,128]{1,0:T(8,128)(2,1)S(1)} collective-permute-done((bf16[1024,128]{1,0:T(8,128)(2,1)}, bf16[1024,128]{1,0:T(8,128)(2,1)S(1)}, u32[]{:S(2)}, u32[]{:S(2)}) %collective-permute-start) | collective-permute-done | bytes 262176 | tf_op jit(solution)/shard_map/ppermute | solution.py:27
  26.6 2.8 %collective-permute-start.5 = (bf16[1024,128]{1,0:T(8,128)(2,1)S(1)}, bf16[1024,128]{1,0:T(8,128)(2,1)S(1)}, u32[]{:S(2)}, u32[]{:S(2)}) collective-permute-start(bf16[1024,128]{1,0:T(8,128)(2,1)S(1)} %collective-permute-done.refs_1_), channel_id=1, source_target_pairs={{0,192},{1,65},{2,194},{3,67},{4,196},{5,69},{6,198},{7,71},{8,200... | collective-permute-start | bytes 786440 | tf_op jit(solution)/shard_map/ppermute | solution.py:27
  31.6 2.9 %collective-permute-done.15.a3 = bf16[18,32,128]{2,1,0:T(8,128)(2,1)S(1)} collective-permute-done((bf16[18,32,128]{2,1,0:T(8,128)(2,1)S(1)}, bf16[18,32,128]{2,1,0:T(8,128)(2,1)S(1)}, u32[]{:S(2)}, u32[]{:S(2)}) %collective-permute-start.15) | collective-permute-done | bytes 147488 | tf_op jit(solution)/shard_map/ppermute | solution.py:27
  34.7 1.8 %collective-permute-start.6 = (bf16[1024,128]{1,0:T(8,128)(2,1)S(1)}, bf16[1024,128]{1,0:T(8,128)(2,1)S(1)}, u32[]{:S(2)}, u32[]{:S(2)}) collective-permute-start(bf16[1024,128]{1,0:T(8,128)(2,1)S(1)} %collective-permute-done.5.refs_6_), channel_id=1, source_target_pairs={{0,64},{1,193},{2,66},{3,195},{4,68},{5,197},{6,70},{7,199},{8,72}... | collective-permute-start | bytes 786440 | tf_op jit(solution)/shard_map/ppermute | solution.py:27
  36.6 1.8 %collective-permute-done.3.refs_4_ = bf16[1024,128]{1,0:T(8,128)(2,1)S(1)} collective-permute-done((bf16[1024,128]{1,0:T(8,128)(2,1)S(1)}, bf16[1024,128]{1,0:T(8,128)(2,1)S(1)}, u32[]{:S(2)}, u32[]{:S(2)}) %collective-permute-start.3) | collective-permute-done | bytes 262176 | tf_op jit(solution)/shard_map/ppermute | solution.py:27
  38.4 2.5 %collective-permute-start.18 = (bf16[18,32,128]{2,1,0:T(8,128)(2,1)S(1)}, bf16[18,32,128]{2,1,0:T(8,128)(2,1)S(1)}, u32[]{:S(2)}, u32[]{:S(2)}) collective-permute-start(bf16[18,32,128]{2,1,0:T(8,128)(2,1)S(1)} %collective-permute-done.15.a3), channel_id=1, source_target_pairs={{0,14},{1,3},{2,0},{3,5},{4,2},{5,7},{6,4},{7,9},{8,6},{9,11},{10,... | collective-permute-start | bytes 442376 | tf_op jit(solution)/shard_map/ppermute | solution.py:27
  40.9 1.9 %collective-permute-start.19 = (bf16[18,32,128]{2,1,0:T(8,128)(2,1)S(1)}, bf16[18,32,128]{2,1,0:T(8,128)(2,1)S(1)}, u32[]{:S(2)}, u32[]{:S(2)}) collective-permute-start(bf16[18,32,128]{2,1,0:T(8,128)(2,1)S(1)} %collective-permute-done.16.g3), channel_id=1, source_target_pairs={{0,14},{1,3},{2,0},{3,5},{4,2},{5,7},{6,4},{7,9},{8,6},{9,11},{10,... | collective-permute-start | bytes 442376 | tf_op jit(solution)/shard_map/ppermute | solution.py:27
  43.6 2.3 %first.1 = (bf16[1024,1024]{1,0:T(8,128)(2,1)S(1)}, f32[3,1536,128]{2,1,0:T(8,128)S(1)}, f32[1,128]{1,0:T(1,128)S(1)}, f32[1,128]{1,0:T(1,128)S(1)}, f32[7,7,128]{2,1,0:T(8,128)S(1)}) custom-call(bf16[1024,128]{1,0:T(8,128)(2,1)S(1)} %bitcast.10, bf16[1024,128]{1,0:T(8,128)(2,1)S(1)} %collective-permute-done.refs_1_, ...), custom_call_target="tpu_custom_call" | custom-call | flops 1207959552 | bytes 4194304 | tf_op jit(solution)/shard_map/first/pallas_call | solution.py:315
  46.0 1.0 %second.1.base = f32[3,1536,128]{2,1,0:T(8,128)S(1)} custom-call(bf16[1024,1024]{1,0:T(8,128)(2,1)S(1)} %get-tuple-element.14.xs, f32[3,1536,128]{2,1,0:T(8,128)S(1)} %get-tuple-element.15.base, bf16[18,32,128]{2,1,0:T(8,128)(2,1)S(1)} %collective-permute-done.12.refs_12_.a2, bf16[18,32,128]{2,1,0:T(8,128)(2,1)S(1)} %collective-permute-done.13.refs_13_.g2, ...), custom_call_target="tpu_custom_call" | custom-call | flops 603979776 | bytes 4194304 | tf_op jit(solution)/shard_map/second/pallas_call | solution.py:335
  46.9 1.2 %third.1 = (bf16[4,256,128]{2,1,0:T(8,128)(2,1)S(1)}, bf16[4,256,128]{2,1,0:T(8,128)(2,1)S(1)}, bf16[2,256,128]{2,1,0:T(8,128)(2,1)S(1)}, f32[4,256,128]{2,1,0:T(8,128)S(1)}) custom-call(bf16[1024,1024]{1,0:T(8,128)(2,1)S(1)} %get-tuple-element.14.xs, f32[3,1536,128]{2,1,0:T(8,128)S(1)} %second.1.base, bf16[18,32,128]{2,1,0:T(8,128)(2,1)S(1)} %collective-permute-done.15.a3, ...), custom_call_target="tpu_custom_call" | custom-call | flops 603979776 | bytes 4194304 | tf_op jit(solution)/shard_map/third/pallas_call | solution.py:344
  48.2 4.9 %collective-permute-start.21 = (bf16[4,256,128]{2,1,0:T(8,128)(2,1)S(1)}, bf16[4,256,128]{2,1,0:T(8,128)(2,1)S(1)}, u32[]{:S(2)}, u32[]{:S(2)}) collective-permute-start(bf16[4,256,128]{2,1,0:T(8,128)(2,1)S(1)} %get-tuple-element.22), channel_id=1, source_target_pairs={{1,2},{3,4},{5,6},{7,8},{9,10},{11,12},{13,14},{15,16},{17,18},{19... | collective-permute-start | bytes 786440 | tf_op jit(solution)/shard_map/ppermute | solution.py:363
  53.2 1.1 %depth.2.part = f32[4,256,128]{2,1,0:T(8,128)S(1)} custom-call(f32[4,256,128]{2,1,0:T(8,128)S(1)} %get-tuple-element.17.own, bf16[2,256,128]{2,1,0:T(8,128)(2,1)S(1)} %get-tuple-element.18.mid, bf16[4,256,128]{2,1,0:T(8,128)(2,1)S(1)} %collective-permute-done.20.inner, f32[1,128]{1,0:T(1,128)S(1)} %get-tuple-element.16.bias, ...), custom_call_target="tpu_custom_call" | custom-call | flops 48168960 | bytes 2097152 | tf_op jit(solution)/shard_map/depth/pallas_call | solution.py:371
  54.3 5.2 %collective-permute-done.21.outer = bf16[4,256,128]{2,1,0:T(8,128)(2,1)S(1)} collective-permute-done((bf16[4,256,128]{2,1,0:T(8,128)(2,1)S(1)}, bf16[4,256,128]{2,1,0:T(8,128)(2,1)S(1)}, u32[]{:S(2)}, u32[]{:S(2)}) %collective-permute-start.21) | collective-permute-done | bytes 262176 | tf_op jit(solution)/shard_map/ppermute | solution.py:363
  59.5 1.4 %depth.3 = bf16[4,256,128]{2,1,0:T(8,128)(2,1)} custom-call(f32[4,256,128]{2,1,0:T(8,128)S(1)} %depth.2.part, f32[4,256,128]{2,1,0:T(8,128)S(1)} %get-tuple-element.17.own, bf16[4,256,128]{2,1,0:T(8,128)(2,1)S(1)} %collective-permute-done.21.outer, f32[1,128]{1,0:T(1,128)S(1)} %get-tuple-element.16.bias, f32[7,7,128]{2,1,0:T(8,128)S(1)} %get-tuple-element.21.weight), custom_call_target="tpu_custom_call" | custom-call | flops 32112640 | bytes 2097152 | tf_op jit(solution)/shard_map/depth/pallas_call | solution.py:371
  (34 shorter events, 5.1 us)
Async XLA Ops:
  0.0 1.5 %collective-permute-start.7 = (bf16[9,32,128]{2,1,0:T(8,128)(2,1)}, bf16[9,32,128]{2,1,0:T(8,128)(2,1)S(1)}, u32[]{:S(2)}, u32[]{:S(2)}) collective-permute-start(bf16[9,32,128]{2,1,0:T(8,128)(2,1)} %bitcast.4), channel_id=1, source_target_pairs={{0,1},{1,0},{2,3},{3,2},{4,5},{5,4},{6,7},{7,6},{8,9},{9,8},{10,11... | collective-permute-start | bytes 221192 | tf_op jit(solution)/shard_map/ppermute | solution.py:27
  0.0 8.3 %collective-permute-start.8 = (bf16[9,32,128]{2,1,0:T(8,128)(2,1)}, bf16[9,32,128]{2,1,0:T(8,128)(2,1)S(1)}, u32[]{:S(2)}, u32[]{:S(2)}) collective-permute-start(bf16[9,32,128]{2,1,0:T(8,128)(2,1)} %bitcast.5), channel_id=1, source_target_pairs={{0,16},{1,17},{2,18},{3,19},{4,20},{5,21},{6,22},{7,23},{8,24},{9,... | collective-permute-start | bytes 221192 | tf_op jit(solution)/shard_map/ppermute | solution.py:27
  1.5 0.9 %copy-start = (bf16[3,3,32,128]{3,2,1,0:T(8,128)(2,1)S(1)}, bf16[3,3,32,128]{3,2,1,0:T(8,128)(2,1)}, u32[]{:S(2)}) copy-start(bf16[3,3,32,128]{3,2,1,0:T(8,128)(2,1)} %param.6) | copy-start | bytes 221188
  2.4 41.3 %copy-start.1 = (bf16[4,256,128]{2,1,0:T(8,128)(2,1)S(1)}, bf16[4,256,128]{2,1,0:T(8,128)(2,1)}, u32[]{:S(2)}) copy-start(bf16[4,256,128]{2,1,0:T(8,128)(2,1)} %param.5) | copy-start | bytes 786436
  2.4 11.2 %collective-permute-start.10 = (bf16[18,32,128]{2,1,0:T(8,128)(2,1)S(1)}, bf16[18,32,128]{2,1,0:T(8,128)(2,1)S(1)}, u32[]{:S(2)}, u32[]{:S(2)}) collective-permute-start(bf16[18,32,128]{2,1,0:T(8,128)(2,1)S(1)} %pack.1.refs_8_), channel_id=1, source_target_pairs={{0,14},{1,3},{2,0},{3,5},{4,2},{5,7},{6,4},{7,9},{8,6},{9,11},{10,... | collective-permute-start | bytes 442376 | tf_op jit(solution)/shard_map/ppermute | solution.py:27
  8.3 1.3 %collective-permute-start.9 = (bf16[9,32,128]{2,1,0:T(8,128)(2,1)S(1)}, bf16[9,32,128]{2,1,0:T(8,128)(2,1)S(1)}, u32[]{:S(2)}, u32[]{:S(2)}) collective-permute-start(bf16[9,32,128]{2,1,0:T(8,128)(2,1)S(1)} %collective-permute-done.8), channel_id=1, source_target_pairs={{0,1},{1,0},{2,3},{3,2},{4,5},{5,4},{6,7},{7,6},{8,9},{9,8},{10,11... | collective-permute-start | bytes 221192 | tf_op jit(solution)/shard_map/ppermute | solution.py:27
  9.6 6.7 %collective-permute-start.11 = (bf16[18,32,128]{2,1,0:T(8,128)(2,1)S(1)}, bf16[18,32,128]{2,1,0:T(8,128)(2,1)S(1)}, u32[]{:S(2)}, u32[]{:S(2)}) collective-permute-start(bf16[18,32,128]{2,1,0:T(8,128)(2,1)S(1)} %constant_dynamic-update-slice_fusion.refs_9_), channel_id=1, source_target_pairs={{0,14},{1,3},{2,0},{3,5},{4,2},{5,7},{6,4},{7,9},{8,6},{9,11},{10,... | collective-permute-start | bytes 442376 | tf_op jit(solution)/shard_map/ppermute | solution.py:27
  13.6 8.6 %collective-permute-start.12 = (bf16[18,32,128]{2,1,0:T(8,128)(2,1)S(1)}, bf16[18,32,128]{2,1,0:T(8,128)(2,1)S(1)}, u32[]{:S(2)}, u32[]{:S(2)}) collective-permute-start(bf16[18,32,128]{2,1,0:T(8,128)(2,1)S(1)} %collective-permute-done.10.refs_10_), channel_id=1, source_target_pairs={{0,14},{1,3},{2,0},{3,5},{4,2},{5,7},{6,4},{7,9},{8,6},{9,11},{10,... | collective-permute-start | bytes 442376 | tf_op jit(solution)/shard_map/ppermute | solution.py:27
  16.3 6.4 %collective-permute-start.13 = (bf16[18,32,128]{2,1,0:T(8,128)(2,1)S(1)}, bf16[18,32,128]{2,1,0:T(8,128)(2,1)S(1)}, u32[]{:S(2)}, u32[]{:S(2)}) collective-permute-start(bf16[18,32,128]{2,1,0:T(8,128)(2,1)S(1)} %collective-permute-done.11.refs_11_), channel_id=1, source_target_pairs={{0,14},{1,3},{2,0},{3,5},{4,2},{5,7},{6,4},{7,9},{8,6},{9,11},{10,... | collective-permute-start | bytes 442376 | tf_op jit(solution)/shard_map/ppermute | solution.py:27
  20.0 6.6 %collective-permute-start = (bf16[1024,128]{1,0:T(8,128)(2,1)}, bf16[1024,128]{1,0:T(8,128)(2,1)S(1)}, u32[]{:S(2)}, u32[]{:S(2)}) collective-permute-start(bf16[1024,128]{1,0:T(8,128)(2,1)} %bitcast.7), channel_id=1, source_target_pairs={{0,32},{1,33},{2,34},{3,35},{4,36},{5,37},{6,38},{7,39},{8,40},{9,... | collective-permute-start | bytes 786440 | tf_op jit(solution)/shard_map/ppermute | solution.py:27
  20.7 9.5 %collective-permute-start.1 = (bf16[1024,128]{1,0:T(8,128)(2,1)}, bf16[1024,128]{1,0:T(8,128)(2,1)S(1)}, u32[]{:S(2)}, u32[]{:S(2)}) collective-permute-start(bf16[1024,128]{1,0:T(8,128)(2,1)} %bitcast.8), channel_id=1, source_target_pairs={{0,64},{1,193},{2,66},{3,195},{4,68},{5,197},{6,70},{7,199},{8,72}... | collective-permute-start | bytes 786440 | tf_op jit(solution)/shard_map/ppermute | solution.py:27
  22.7 20.9 %collective-permute-start.14 = (bf16[72,32,128]{2,1,0:T(8,128)(2,1)S(1)}, bf16[72,32,128]{2,1,0:T(8,128)(2,1)S(1)}, u32[]{:S(2)}, u32[]{:S(2)}) collective-permute-start(bf16[72,32,128]{2,1,0:T(8,128)(2,1)S(1)} %pad_maximum_fusion), channel_id=1, source_target_pairs={{0,1},{1,0},{2,3},{3,2},{4,5},{5,4},{6,7},{7,6},{8,9},{9,8},{10,11... | collective-permute-start | bytes 1769480 | tf_op jit(solution)/shard_map/ppermute | solution.py:27
  22.8 7.9 %collective-permute-start.2 = (bf16[1024,128]{1,0:T(8,128)(2,1)}, bf16[1024,128]{1,0:T(8,128)(2,1)S(1)}, u32[]{:S(2)}, u32[]{:S(2)}) collective-permute-start(bf16[1024,128]{1,0:T(8,128)(2,1)} %bitcast.9), channel_id=1, source_target_pairs={{0,192},{1,65},{2,194},{3,67},{4,196},{5,69},{6,198},{7,71},{8,200... | collective-permute-start | bytes 786440 | tf_op jit(solution)/shard_map/ppermute | solution.py:27
  26.6 8.1 %collective-permute-start.5 = (bf16[1024,128]{1,0:T(8,128)(2,1)S(1)}, bf16[1024,128]{1,0:T(8,128)(2,1)S(1)}, u32[]{:S(2)}, u32[]{:S(2)}) collective-permute-start(bf16[1024,128]{1,0:T(8,128)(2,1)S(1)} %collective-permute-done.refs_1_), channel_id=1, source_target_pairs={{0,192},{1,65},{2,194},{3,67},{4,196},{5,69},{6,198},{7,71},{8,200... | collective-permute-start | bytes 786440 | tf_op jit(solution)/shard_map/ppermute | solution.py:27
  29.3 5.1 %collective-permute-start.15 = (bf16[18,32,128]{2,1,0:T(8,128)(2,1)S(1)}, bf16[18,32,128]{2,1,0:T(8,128)(2,1)S(1)}, u32[]{:S(2)}, u32[]{:S(2)}) collective-permute-start(bf16[18,32,128]{2,1,0:T(8,128)(2,1)S(1)} %collective-permute-done.12.refs_12_.a2), channel_id=1, source_target_pairs={{0,14},{1,3},{2,0},{3,5},{4,2},{5,7},{6,4},{7,9},{8,6},{9,11},{10,... | collective-permute-start | bytes 442376 | tf_op jit(solution)/shard_map/ppermute | solution.py:27
  30.2 6.3 %collective-permute-start.16 = (bf16[18,32,128]{2,1,0:T(8,128)(2,1)S(1)}, bf16[18,32,128]{2,1,0:T(8,128)(2,1)S(1)}, u32[]{:S(2)}, u32[]{:S(2)}) collective-permute-start(bf16[18,32,128]{2,1,0:T(8,128)(2,1)S(1)} %collective-permute-done.13.refs_13_.g2), channel_id=1, source_target_pairs={{0,14},{1,3},{2,0},{3,5},{4,2},{5,7},{6,4},{7,9},{8,6},{9,11},{10,... | collective-permute-start | bytes 442376 | tf_op jit(solution)/shard_map/ppermute | solution.py:27
  30.7 7.7 %collective-permute-start.3 = (bf16[1024,128]{1,0:T(8,128)(2,1)S(1)}, bf16[1024,128]{1,0:T(8,128)(2,1)S(1)}, u32[]{:S(2)}, u32[]{:S(2)}) collective-permute-start(bf16[1024,128]{1,0:T(8,128)(2,1)S(1)} %collective-permute-done.1.refs_2_), channel_id=1, source_target_pairs={{0,32},{1,33},{2,34},{3,35},{4,36},{5,37},{6,38},{7,39},{8,40},{9,... | collective-permute-start | bytes 786440 | tf_op jit(solution)/shard_map/ppermute | solution.py:27
  34.5 6.5 %collective-permute-start.4 = (bf16[1024,128]{1,0:T(8,128)(2,1)S(1)}, bf16[1024,128]{1,0:T(8,128)(2,1)S(1)}, u32[]{:S(2)}, u32[]{:S(2)}) collective-permute-start(bf16[1024,128]{1,0:T(8,128)(2,1)S(1)} %collective-permute-done.2.refs_3_), channel_id=1, source_target_pairs={{0,64},{1,193},{2,66},{3,195},{4,68},{5,197},{6,70},{7,199},{8,72}... | collective-permute-start | bytes 786440 | tf_op jit(solution)/shard_map/ppermute | solution.py:27
  34.7 9.0 %collective-permute-start.6 = (bf16[1024,128]{1,0:T(8,128)(2,1)S(1)}, bf16[1024,128]{1,0:T(8,128)(2,1)S(1)}, u32[]{:S(2)}, u32[]{:S(2)}) collective-permute-start(bf16[1024,128]{1,0:T(8,128)(2,1)S(1)} %collective-permute-done.5.refs_6_), channel_id=1, source_target_pairs={{0,64},{1,193},{2,66},{3,195},{4,68},{5,197},{6,70},{7,199},{8,72}... | collective-permute-start | bytes 786440 | tf_op jit(solution)/shard_map/ppermute | solution.py:27
  36.5 9.4 %collective-permute-start.17 = (bf16[36,32,128]{2,1,0:T(8,128)(2,1)S(1)}, bf16[36,32,128]{2,1,0:T(8,128)(2,1)S(1)}, u32[]{:S(2)}, u32[]{:S(2)}) collective-permute-start(bf16[36,32,128]{2,1,0:T(8,128)(2,1)S(1)} %pad_maximum_fusion.1), channel_id=1, source_target_pairs={{0,1},{1,0},{2,3},{3,2},{4,5},{5,4},{6,7},{7,6},{8,9},{9,8},{10,11... | collective-permute-start | bytes 884744 | tf_op jit(solution)/shard_map/ppermute | solution.py:27
  38.4 8.5 %collective-permute-start.18 = (bf16[18,32,128]{2,1,0:T(8,128)(2,1)S(1)}, bf16[18,32,128]{2,1,0:T(8,128)(2,1)S(1)}, u32[]{:S(2)}, u32[]{:S(2)}) collective-permute-start(bf16[18,32,128]{2,1,0:T(8,128)(2,1)S(1)} %collective-permute-done.15.a3), channel_id=1, source_target_pairs={{0,14},{1,3},{2,0},{3,5},{4,2},{5,7},{6,4},{7,9},{8,6},{9,11},{10,... | collective-permute-start | bytes 442376 | tf_op jit(solution)/shard_map/ppermute | solution.py:27
  40.9 6.0 %collective-permute-start.19 = (bf16[18,32,128]{2,1,0:T(8,128)(2,1)S(1)}, bf16[18,32,128]{2,1,0:T(8,128)(2,1)S(1)}, u32[]{:S(2)}, u32[]{:S(2)}) collective-permute-start(bf16[18,32,128]{2,1,0:T(8,128)(2,1)S(1)} %collective-permute-done.16.g3), channel_id=1, source_target_pairs={{0,14},{1,3},{2,0},{3,5},{4,2},{5,7},{6,4},{7,9},{8,6},{9,11},{10,... | collective-permute-start | bytes 442376 | tf_op jit(solution)/shard_map/ppermute | solution.py:27
  48.1 5.0 %collective-permute-start.20 = (bf16[4,256,128]{2,1,0:T(8,128)(2,1)S(1)}, bf16[4,256,128]{2,1,0:T(8,128)(2,1)S(1)}, u32[]{:S(2)}, u32[]{:S(2)}) collective-permute-start(bf16[4,256,128]{2,1,0:T(8,128)(2,1)S(1)} %get-tuple-element.19), channel_id=1, source_target_pairs={{0,1},{1,0},{2,3},{3,2},{4,5},{5,4},{6,7},{7,6},{8,9},{9,8},{10,11... | collective-permute-start | bytes 786440 | tf_op jit(solution)/shard_map/ppermute | solution.py:364
  48.2 11.3 %collective-permute-start.21 = (bf16[4,256,128]{2,1,0:T(8,128)(2,1)S(1)}, bf16[4,256,128]{2,1,0:T(8,128)(2,1)S(1)}, u32[]{:S(2)}, u32[]{:S(2)}) collective-permute-start(bf16[4,256,128]{2,1,0:T(8,128)(2,1)S(1)} %get-tuple-element.22), channel_id=1, source_target_pairs={{1,2},{3,4},{5,6},{7,8},{9,10},{11,12},{13,14},{15,16},{17,18},{19... | collective-permute-start | bytes 786440 | tf_op jit(solution)/shard_map/ppermute | solution.py:363
